TPU v7x, 256 devices: a whole 4x4x8 slice. The times are simulated.
256 devices in a mesh: tp: 4 (over y), seq: 64 (over x, z, core).
Axes of the slice: x: 4, y: 4, z: 8, core: 2. Of those that a mesh axis runs over, the one named last changes fastest.
Arguments:
- query_video: bfloat16 [8192, 3072], P('seq', 'tp'), may hold values from -160 to 160
- key_video: bfloat16 [8192, 3072], P('seq', 'tp'), may hold values from -32 to 32
- value_video: bfloat16 [8192, 3072], P('seq', 'tp'), may hold values from -6 to 6
- query_audio: bfloat16 [1024, 3072], P('seq', 'tp'), may hold values from -160 to 160
- key_audio: bfloat16 [1024, 3072], P('seq', 'tp'), may hold values from -32 to 32
- value_audio: bfloat16 [1024, 3072], P('seq', 'tp'), may hold values from -6 to 6
- video_spans: int32 [64, 2], replicated, may hold values from 0 to 64, as said below
- audio_spans: int32 [64, 2], replicated, may hold values from 0 to 64, as said below
- video_output_weight: bfloat16 [3072, 3072], P('tp'), may hold values from -0.109375 to 0.109375
- audio_output_weight: bfloat16 [3072, 3072], P('tp'), may hold values from -0.109375 to 0.109375
Outputs:
- video_out: bfloat16 [8192, 3072], P('seq', 'tp')
- audio_out: bfloat16 [1024, 3072], P('seq', 'tp')
Inputs may be any that keep to these rules, and one draw needn't show every extreme that they name: `video_spans`: row b holds start and end with start <= b < end and end - start <= 65. `audio_spans`: row c holds start and end with start <= c < end and end - start <= 65.
All inputs are finite; a program needn't handle non-finite values.
Results may differ from a plain program's by a relative error of at most 0.013.
Values may be sent and summed in bfloat16 or wider, within the bound.
No kernel may reach another device: no remote copies, remote signals or barrier semaphores. Data moves between devices by JAX's collectives and lax.ppermute only.
A program may use at most 192 MiB of HBM per device.

v0:
```python
import math

import jax
import jax.numpy as jnp
from jax import lax
from jax.sharding import Mesh
from jax.sharding import PartitionSpec as P

HEAD = 128
VBLK = 128
ABLK = 16
SEQ = ("seq_0", "seq_1", "seq_2")


mask_floor = -1e30


def sent_to_all(array, axis):
    count = lax.axis_size(axis)
    return lax.all_to_all(
        jnp.broadcast_to(array[None], (count, *array.shape)), axis, 0, 0, tiled=True
    )


def laid_out(parts, dim):
    parts = jnp.moveaxis(parts, 0, dim)
    lengths = parts.shape
    return parts.reshape(*lengths[:dim], lengths[dim] * lengths[dim + 1], *lengths[dim + 2 :])


def gathered_by_axis(array, axes, dim):
    far, near = axes
    parts = sent_to_all(sent_to_all(array, far), near)
    return laid_out(parts.swapaxes(0, 1).reshape(-1, *array.shape), dim)


def sent_together(arrays, axis, dim, along):
    widths = [a.shape[along] for a in arrays]
    both = jnp.concatenate(arrays, axis=along)
    result = gathered_by_axis(both, axis, dim)
    return tuple(jnp.split(result, [sum(widths[:k]) for k in range(1, len(widths))], axis=along))


def in_one_piece(arrays, axis, dim, along):
    both = jnp.concatenate(arrays, axis=along)
    result, at, done = (lax.all_gather(both, axis, axis=dim, tiled=True), 0, [])
    for a in arrays:
        done.append(lax.slice_in_dim(result, at, at + a.shape[along], axis=along))
        at += a.shape[along]
    return tuple(done)


def cut_along(array, dim, count):
    before, after = (array.shape[:dim], array.shape[dim + 1 :])
    return jnp.moveaxis(array.reshape(*before, count, -1, *after), dim, 0)


def sent_and_summed(array, axis, dim):
    count = lax.axis_size(axis)
    parts = lax.all_to_all(cut_along(array, dim, count), axis, 0, 0, tiled=True)
    return jnp.sum(parts.astype(jnp.float32), axis=0)


def side_by_side(arrays, axis, dim, along):
    widths = [a.shape[along] for a in arrays]
    both = jnp.concatenate(arrays, axis=along)
    result = sent_and_summed(both, axis, dim)
    return tuple(jnp.split(result, [sum(widths[:k]) for k in range(1, len(widths))], axis=along))


def split_heads(values):
    return values.reshape(values.shape[0], values.shape[1] // HEAD, HEAD)


def fresh_state(row_count, heads_here):
    return (
        jnp.full((heads_here, row_count), mask_floor, jnp.float32),
        jnp.zeros((heads_here, row_count), jnp.float32),
        jnp.zeros((row_count, heads_here, HEAD), jnp.float32),
    )


def absorb(carry_state, queries, key_rows, values, allowed):
    row_peak, row_total, numerator = carry_state
    scores = jnp.einsum("qhd,khd->hqk", queries, key_rows, preferred_element_type=jnp.float32) * (
        1.0 / math.sqrt(HEAD)
    )
    masked = jnp.where(allowed[None], scores, mask_floor)
    new_peak = jnp.maximum(row_peak, jnp.max(masked, axis=2))
    weights = jnp.exp(jnp.where(allowed[None], scores - new_peak[:, :, None], mask_floor))
    rescale = jnp.exp(row_peak - new_peak)
    row_total = jnp.sum(weights, axis=2)
    numerator = numerator * rescale.T[:, :, None] + jnp.einsum(
        "hqk,khd->qhd", weights.astype(jnp.bfloat16), values, preferred_element_type=jnp.float32
    )
    return (new_peak, row_total, numerator)


def finish(carry_state):
    row_peak, row_total, numerator = carry_state
    attended = numerator / row_total.T[:, :, None]
    return attended.reshape(attended.shape[0], -1)


def span_bounds(blocks, span_table):
    block_match = blocks[:, None] == jnp.arange(span_table.shape[0], dtype=jnp.int32)[None, :]
    span_first = jnp.sum(jnp.where(block_match, span_table[:, 0][None, :], 0), axis=1)
    beyond = jnp.sum(jnp.where(block_match, span_table[:, 1][None, :], 0), axis=1)
    return (span_first, beyond)


def per_device(
    query_video,
    key_video,
    value_video,
    query_audio,
    key_audio,
    value_audio,
    video_spans,
    audio_spans,
    video_output_weight,
    audio_output_weight,
):
    video_count = query_video.shape[0]
    audio_count = query_audio.shape[0]
    heads_here = query_video.shape[1] // HEAD
    position = lax.axis_index(SEQ)
    video_blocks = (position * video_count + jnp.arange(video_count, dtype=jnp.int32)) // VBLK
    audio_blocks = (position * audio_count + jnp.arange(audio_count, dtype=jnp.int32)) // ABLK
    video_first, video_beyond = span_bounds(video_blocks, video_spans)
    video_queries = split_heads(query_video)
    audio_queries = split_heads(query_audio)
    everything = jnp.ones((1, 1), dtype=jnp.bool_)
    audio_keys_all, audio_values_all = sent_together(
        (key_audio, value_audio), (("seq_0", "seq_1"), "seq_2"), 0, 1
    )
    audio_key_heads = split_heads(audio_keys_all)
    audio_value_heads = split_heads(audio_values_all)
    key_blocks = jnp.arange(audio_keys_all.shape[0], dtype=jnp.int32) // ABLK
    allowed_video = (key_blocks[None, :] >= video_first[:, None]) & (
        key_blocks[None, :] < video_beyond[:, None]
    )
    video_cross = finish(
        absorb(
            fresh_state(video_count, heads_here),
            video_queries,
            audio_key_heads,
            audio_value_heads,
            allowed_video,
        )
    )
    audio_self = finish(
        absorb(
            fresh_state(audio_count, heads_here),
            audio_queries,
            audio_key_heads,
            audio_value_heads,
            everything,
        )
    )
    audio_first, audio_beyond = span_bounds(audio_blocks, audio_spans)
    initial = (fresh_state(video_count, heads_here), fresh_state(audio_count, heads_here))
    segment = in_one_piece((key_video, value_video), SEQ, 0, 1)
    segment_blocks = jnp.arange(segment[0].shape[0], dtype=jnp.int32) // VBLK
    allowed = (segment_blocks[None, :] >= audio_first[:, None]) & (
        segment_blocks[None, :] < audio_beyond[:, None]
    )
    video_self = finish(
        absorb(
            initial[0], video_queries, split_heads(segment[0]), split_heads(segment[1]), everything
        )
    )
    audio_cross = finish(
        absorb(initial[1], audio_queries, split_heads(segment[0]), split_heads(segment[1]), allowed)
    )
    attended_video = (video_self + video_cross).astype(jnp.bfloat16)
    attended_audio = (audio_self + audio_cross).astype(jnp.bfloat16)
    video_part = jnp.dot(attended_video, video_output_weight, preferred_element_type=jnp.float32)
    audio_part = jnp.dot(attended_audio, audio_output_weight, preferred_element_type=jnp.float32)
    video_sum, audio_sum = side_by_side(
        (video_part.astype(jnp.bfloat16), audio_part.astype(jnp.bfloat16)), "tp", 1, 0
    )
    return (video_sum.astype(jnp.bfloat16), audio_sum.astype(jnp.bfloat16))


def solution(mesh):
    finer = Mesh(mesh.devices.reshape(mesh.shape["tp"], 4, 8, 2), ("tp", "seq_0", "seq_1", "seq_2"))
    in_specs = (
        P(SEQ, "tp"),
        P(SEQ, "tp"),
        P(SEQ, "tp"),
        P(SEQ, "tp"),
        P(SEQ, "tp"),
        P(SEQ, "tp"),
        P(),
        P(),
        P("tp", None),
        P("tp", None),
    )
    out_specs = (P(SEQ, "tp"), P(SEQ, "tp"))
    return jax.shard_map(
        per_device, mesh=finer, in_specs=in_specs, out_specs=out_specs, check_vma=False
    )
```

profile of v0, /device:TPU:1, one launch (start us, length us, event | category | flops | bytes accessed | tf_op | source)
XLA Modules:
  0.0 266.8 jit_solution(15034464365806931796)
XLA Ops:
  7.2 0.0 copy-start
  7.2 0.0 all-gather.2.cloned.1.call-start
  7.2 1.1 copy.60
  8.3 0.0 copy-start.6
  8.3 1.1 copy.61
  9.5 0.0 copy-start.7
  9.5 0.0 copy-start.8
  9.5 0.8 pad_maximum_fusion.1
  10.3 0.0 all-gather.2.cloned.1.call-update
  10.3 0.8 pad_maximum_fusion.2
  11.0 1.4 broadcast_in_dim.146
  12.5 11.9 %all-to-all-start = ((bf16[32,16,1536]{2,1,0:T(8,128)(2,1)}), bf16[32,16,1536]{2,1,0:T(8,128)(2,1)S(1)}, u32[]{:S(2)}, u32[]{:S(2)}) async-start(bf16[32,16,1536]{2,1,0:T(8,128)(2,1)} %broadcast_in_dim.146), calls=%async_computation | async-start | bytes 3145728 | tf_op jit(solution)/shard_map/all_to_all | solution.py:20
  24.3 0.0 copy-done.6
  24.4 0.2 copy.62
  24.6 0.0 copy-done.7
  24.6 0.2 select_reduce_fusion.4
  24.8 0.0 copy-done.8
  24.8 0.1 select_reduce_fusion.2
  24.9 0.9 compare_and_fusion.1
  25.7 0.2 compare_and_fusion
  25.9 42.8 %all-to-all-done = bf16[32,16,1536]{2,1,0:T(8,128)(2,1)S(1)} async-done(((bf16[32,16,1536]{2,1,0:T(8,128)(2,1)}), bf16[32,16,1536]{2,1,0:T(8,128)(2,1)S(1)}, u32[]{:S(2)}, u32[]{:S(2)}) %all-to-all-start) | async-done | bytes 1572896 | tf_op jit(solution)/shard_map/all_to_all | solution.py:20
  68.7 0.4 broadcast_in_dim.147
  69.1 12.2 %all_to_all.15 = bf16[2,32,16,1536]{3,2,1,0:T(8,128)(2,1)S(1)} all-to-all(bf16[2,32,16,1536]{3,2,1,0:T(8,128)(2,1)S(1)} %broadcast_in_dim.147), channel_id=1, replica_groups=mesh['tp'=4,'seq_0'=4,'seq_1'=8,'seq_2'=2] {'seq_2'}, dimensions={0} | all-to-all | bytes 6291456 | tf_op jit(solution)/shard_map/all_to_all | solution.py:20
  81.3 0.3 copy.66
  81.6 1.4 fusion.86
  83.0 0.7 copy.67
  83.8 1.7 copy.70
  85.5 0.0 copy-start.2
  85.5 0.0 copy-done
  85.5 0.4 fusion.87
  85.9 0.0 copy-start.3
  85.9 0.0 copy-start.4
  85.9 0.2 fusion.65
  86.1 0.6 copy-done.3
  86.7 1.8 fusion.8
  88.5 0.0 copy-done.4
  88.5 0.7 fusion.13
  89.2 0.0 copy-done.2
  89.2 1.9 fusion.62
  91.1 74.0 %all-gather.2.cloned.1.call-done = bf16[8192,1536]{0,1:T(8,128)(2,1)} async-done(((bf16[128,1536]{0,1:T(8,128)(2,1)}), bf16[8192,1536]{0,1:T(8,128)(2,1)}) %all-gather.2.cloned.1.call-update) | async-done | bytes 25165840 | tf_op jit(solution)/shard_map/all_gather | solution.py:46
  165.1 17.3 %fusion.85 = (bf16[8192,768]{0,1:T(8,128)(2,1)}, bf16[8192,768]{0,1:T(8,128)(2,1)}) fusion(bf16[8192,1536]{0,1:T(8,128)(2,1)} %all-gather.2.cloned.1.call-done), kind=kLoop, calls=%fused_computation.111 | loop fusion | bytes 50331648 | tf_op jit(solution)/shard_map/slice | solution.py:48
  182.4 13.5 %bitcast_reduce_fusion = (f32[6,128]{1,0:T(8,128)S(1)}, f32[6,8192,128]{2,1,0:T(8,128)}) fusion(bf16[8192,6,128]{0,2,1:T(8,128)(2,1)} %bitcast.150, bf16[128,6,128]{0,2,1:T(8,128)(2,1)S(1)} %bitcast.162), kind=kOutput, calls=%fused_computation.1 | convolution fusion | flops 1623194880 | bytes 37948416 | tf_op jit(solution)/shard_map/qhd,khd->hqk/dot_general | solution.py:85
  195.9 5.7 %select_reduce_fusion = (f32[6,16]{1,0:T(8,128)S(1)}, f32[6,16,8192]{2,1,0:T(8,128)S(1)}) fusion(pred[16,8192]{1,0:T(8,128)(4,1)S(1)} %compare_and_fusion, bf16[8192,6,128]{0,2,1:T(8,128)(2,1)} %bitcast.151, bf16[16,768]{1,0:T(8,128)(2,1)S(1)} %copy-done), kind=kOutput, calls=%fused_computation.18 | convolution fusion | flops 203685792 | bytes 15884672 | tf_op jit(solution)/shard_map/qhd,khd->hqk/dot_general | solution.py:85
  201.5 0.9 fusion.11
  202.4 6.4 %fusion.50 = f32[16,6,128]{2,0,1:T(8,128)S(1)} fusion(bf16[8192,6,128]{0,2,1:T(8,128)(2,1)} %bitcast.148, f32[6,16,8192]{2,1,0:T(8,128)S(1)} %get-tuple-element.23, f32[6,16]{1,0:T(8,128)S(1)} %get-tuple-element.17, pred[16,8192]{1,0:T(8,128)(4,1)S(1)} %compare_and_fusion, f32[16,6]{0,1:T(8,128)S(1)} %bitcast.166, f32[16,6]{0,1:T(8,128)S(1)} %get-tuple-element.16), kind=kOutput, calls=%fused_computation.46 | convolution fusion | flops 203710464 | bytes 15910016 | tf_op jit(solution)/shard_map/hqk,khd->qhd/dot_general | solution.py:93
  208.9 2.0 fusion.49
  210.9 3.1 %convolution_convert_fusion.1 = bf16[16,3072]{1,0:T(8,128)(2,1)S(1)} fusion(bf16[768,3072]{1,0:T(8,128)(2,1)} %param.19, bf16[6,2,8,128]{3,2,1,0:T(8,128)(2,1)S(1)} %fusion.49), kind=kOutput, calls=%fused_computation.11 | convolution fusion | flops 75546624 | bytes 4841472 | tf_op jit(solution)/shard_map/dot_general | solution.py:179
  214.0 0.0 copy-start.5
  214.0 0.0 slice-start
  214.0 12.1 %fusion.1 = f32[6,128]{1,0:T(8,128)S(1)} fusion(f32[6,8192,128]{2,1,0:T(8,128)} %get-tuple-element.29, f32[6,128]{1,0:T(8,128)S(1)} %get-tuple-element.11), kind=kLoop, calls=%fused_computation.3 | loop fusion | flops 18873600 | bytes 25171968 | tf_op jit(solution)/shard_map/reduce_sum | solution.py:92
  226.0 0.0 copy-done.5
  226.1 0.0 slice-start.1
  226.1 15.0 %fusion.59 = bf16[128,6,128]{0,2,1:T(8,128)(2,1)S(1)} fusion(f32[128,6,128]{0,2,1:T(8,128)S(1)} %copy-done.5, bf16[8192,6,128]{0,2,1:T(8,128)(2,1)} %bitcast.149, f32[6,8192,128]{2,1,0:T(8,128)} %get-tuple-element.29, f32[6,128]{1,0:T(8,128)S(1)} %get-tuple-element.11, f32[128,6]{0,1:T(8,128)S(1)} %bitcast.164, f32[128,6]{0,1:T(8,128)S(1)} %get-tuple-element.10), kind=kOutput, calls=%fused_computation.49 | convolution fusion | flops 1629880320 | bytes 38347776 | tf_op jit(solution)/shard_map/hqk,khd->qhd/dot_general | solution.py:93
  241.1 0.0 slice-done
  241.1 0.0 slice-done.1
  241.1 0.0 copy-start.1
  241.2 0.8 convolution_convert_fusion
  242.0 0.1 pad_maximum_fusion
  242.0 0.1 copy.110
  242.1 16.4 %all_to_all.16 = bf16[4,144,768]{2,1,0:T(8,128)(2,1)S(1)} all-to-all(bf16[4,144,768]{2,1,0:T(8,128)(2,1)S(1)} %bitcast.160), channel_id=1, replica_groups=mesh['tp'=4,'seq_0'=4,'seq_1'=8,'seq_2'=2] {'tp'}, dimensions={0} | all-to-all | bytes 1769472 | tf_op jit(solution)/shard_map/all_to_all | solution.py:60
  258.5 0.1 reduce
  258.7 0.6 split.21
  259.3 0.7 split.20
  260.0 0.0 copy-done.1
  (11 shorter events, 0.1 us)
Async XLA Ops:
  7.2 78.3 %copy-start = (bf16[16,768]{1,0:T(8,128)(2,1)S(1)}, bf16[16,768]{1,0:T(8,128)(2,1)}, u32[]{:S(2)}) copy-start(bf16[16,768]{1,0:T(8,128)(2,1)} %param.13) | copy-start | bytes 73732
  7.2 157.9 %all-gather.2.cloned.1.call-start = ((), (), s32[]{:S(2)}) async-start(), calls=%async_computation.3 | async-start | bytes 25559040 | tf_op jit(solution)/shard_map/all_gather | solution.py:46
  8.3 16.0 %copy-start.6 = (bf16[128,768]{1,0:T(8,128)(2,1)S(1)}, bf16[128,768]{1,0:T(8,128)(2,1)}, u32[]{:S(2)}) copy-start(bf16[128,768]{1,0:T(8,128)(2,1)} %param.10) | copy-start | bytes 589828
  9.5 15.1 %copy-start.7 = (s32[64,2]{0,1:T(2,128)S(1)}, s32[64,2]{0,1:T(2,128)}, u32[]{:S(2)}) copy-start(s32[64,2]{0,1:T(2,128)} %param.17) | copy-start | bytes 1540
  9.5 15.3 %copy-start.8 = (s32[64,2]{0,1:T(2,128)S(1)}, s32[64,2]{0,1:T(2,128)}, u32[]{:S(2)}) copy-start(s32[64,2]{0,1:T(2,128)} %param.16) | copy-start | bytes 1540
  12.5 56.3 %all-to-all-start = ((bf16[32,16,1536]{2,1,0:T(8,128)(2,1)}), bf16[32,16,1536]{2,1,0:T(8,128)(2,1)S(1)}, u32[]{:S(2)}, u32[]{:S(2)}) async-start(bf16[32,16,1536]{2,1,0:T(8,128)(2,1)} %broadcast_in_dim.146), calls=%async_computation | async-start | bytes 3145728 | tf_op jit(solution)/shard_map/all_to_all | solution.py:20
  85.5 3.7 %copy-start.2 = (bf16[1024,768]{0,1:T(8,128)(2,1)}, bf16[1024,768]{0,1:T(8,128)(2,1)S(1)}, u32[]{:S(2)}) copy-start(bf16[1024,768]{0,1:T(8,128)(2,1)S(1)} %copy.70) | copy-start | bytes 4718596
  85.9 0.8 copy-start.3
  85.9 2.6 copy-start.4
  214.0 12.1 %copy-start.5 = (f32[128,6,128]{0,2,1:T(8,128)S(1)}, f32[128,6,128]{0,2,1:T(8,128)}, u32[]{:S(2)}) copy-start(f32[128,6,128]{0,2,1:T(8,128)} %fusion.62) | copy-start | bytes 1179652
  214.0 27.1 %slice-start = ((s8[4718592]{0:T(1024)(128)(4,1)}), s8[4194304]{0:T(1024)(128)(4,1)S(1)}, s32[]{:S(2)}) async-start(s8[4718592]{0:T(1024)(128)(4,1)} %bitcast.157), calls=%async_computation.4 | async-start | bytes 8388608
  226.1 15.1 %slice-start.1 = ((s8[4718592]{0:T(1024)(128)(4,1)}), s8[524288]{0:T(1024)(128)(4,1)S(1)}, s32[]{:S(2)}) async-start(s8[4718592]{0:T(1024)(128)(4,1)} %bitcast.157), calls=%async_computation.5 | async-start | bytes 1048576
  241.1 18.8 %copy-start.1 = (bf16[16,768]{1,0:T(8,128)(2,1)S(1)}, bf16[16,768]{1,0:T(8,128)(2,1)}, u32[]{:S(2)}) copy-start(bf16[16,768]{1,0:T(8,128)(2,1)} %param.13) | copy-start | bytes 73732
Sparse Core Ops, SparseCore 0:
  10.5 154.4 all-gather.1
where the time goes:
time: 267 us
  waiting for transfers between devices  117 us (44%)
  matrix products  50.6 us (19%)
  blocking collectives  28.6 us (11%)
  local copies, waits for them, and re-layouts  27.6 us (10%)
  other arithmetic  16.9 us (6%)
  between operations  14.3 us (5%)
  starting transfers between devices  11.9 us (4%)
    all_gather x1, waiting for transfers between devices, in_one_piece(): result, at, done = (lax.all_gather(both, axis, axis=dim, tiled=True), 0, [])  74 us
    all_to_all x1, waiting for transfers between devices, sent_to_all(): lax.all_to_all(jnp.broadcast_to(array[None], (count, *array.shape)), axis...  42.8 us
    dot_general x4, matrix products, absorb(): jnp.einsum('hqk,khd->qhd', weights.astype(jnp.bfloat16), values, preferre...  25.4 us
    dot_general x4, matrix products, absorb(): jnp.einsum('qhd,khd->hqk', queries, key_rows, preferred_element_type=jnp....  21.3 us
    slice x1, local copies, waits for them, and re-layouts, in_one_piece(): done.append(lax.slice_in_dim(result, at, at + a.shape[along], axis=along))  17.3 us
    all_to_all x1, blocking collectives, sent_and_summed(): parts = lax.all_to_all(cut_along(array, dim, count), axis, 0, 0, tiled=True)  16.4 us
    reduce_sum x4, other arithmetic, absorb(): row_total = jnp.sum(weights, axis=2)  13.8 us
    all_to_all x1, blocking collectives, sent_to_all(): lax.all_to_all(jnp.broadcast_to(array[None], (count, *array.shape)), axis...  12.2 us
  transfers between devices with their start and end apart: 2, of which 2 were waited for; matrix products, arithmetic and copies ran while one was open for 5% of the time, Pallas kernels for 0%

commit v1 on v0

v1 whole, which is shorter than its diff:
```python
import functools
import math

import jax
import jax.numpy as jnp
from jax import lax
from jax.experimental import pallas as pl
from jax.experimental.pallas import tpu as pltpu
from jax.sharding import Mesh
from jax.sharding import PartitionSpec as P

HEAD = 128
VBLK = 128
ABLK = 16
ROWS = 2 * (VBLK + ABLK)
NX = 4
NZ = 8
SEQ = ("x", "z", "c")
SCALE = math.log2(math.e) / math.sqrt(HEAD)
MASKED = -1e30
LOWEST = -1e29
BF = jnp.bfloat16
F32 = jnp.float32
STATS = 3 * ROWS
PAYLOAD = STATS + 48
TOKENS = VBLK + ABLK


VSPEC = pl.BlockSpec(memory_space=pltpu.VMEM)
SSPEC = pl.BlockSpec(memory_space=pltpu.SMEM)
HSPEC = pl.BlockSpec(memory_space=pltpu.HBM)


def kernel_call(body, outs, in_specs, micros, aliases=None, scratch=(), vmem=32 << 20):
    shapes = tuple(jax.ShapeDtypeStruct(s, d) for s, d in outs)
    return pl.pallas_call(
        body,
        out_shape=shapes,
        in_specs=in_specs,
        out_specs=tuple(VSPEC for _ in shapes),
        scratch_shapes=scratch,
        input_output_aliases=aliases or {},
        cost_estimate=pl.CostEstimate(
            flops=int(micros * 1e9), bytes_accessed=1 << 16, transcendentals=0
        ),
        compiler_params=pltpu.CompilerParams(vmem_limit_bytes=vmem),
    )


def entry_body(
    pos, q_hbm, k_hbm, v_hbm, qa_hbm, ka_hbm, va_hbm, own, far, q, k, v, qa, ka, va, sems,
):
    pairs = ((k_hbm, k), (v_hbm, v), (q_hbm, q), (ka_hbm, ka), (va_hbm, va), (qa_hbm, qa))
    copies = [pltpu.make_async_copy(s, d, sems.at[i]) for i, (s, d) in enumerate(pairs)]
    for cp in copies:
        cp.start()
    for cp in copies:
        cp.wait()
    core = pos[2]
    for half, out in ((1, far), (0, own)):
        side = core if half == 0 else 1 - core
        for h in range(3):
            cols = pl.ds(pl.multiple_of((side * 3 + h) * HEAD, HEAD), HEAD)
            out[h, 0:VBLK, :] = k[:, cols].astype(F32).T.astype(BF)
            out[h, VBLK:TOKENS, :] = ka[:, cols]
            out[3 + h, 0:VBLK, :] = v[:, cols]
            out[3 + h, VBLK:TOKENS, :] = va[:, cols]
            out[6 + h, 0:VBLK, :] = q[:, cols]
            out[6 + h, VBLK:TOKENS, :] = qa[:, cols]


def chip_body(own, near, q_chip, kv_chip, audio):
    for r, src in ((0, own), (1, near)):
        kv_chip[r] = src[0:6]
        for i in range(6):
            audio[i, 16 * r : 16 * (r + 1), :] = src[i, VBLK:TOKENS, :]
        for h in range(3):
            q_chip[h, 128 * r : 128 * (r + 1), :] = src[6 + h, 0:VBLK, :]
            q_chip[h, 256 + 16 * r : 272 + 16 * r, :] = src[6 + h, VBLK:TOKENS, :]


def device_band(x, z, c):
    return (x * NZ + z) * 2 + c


def bf16_parts(a, count):
    parts = []
    for _ in range(count):
        parts.append(a.astype(BF).astype(F32))
        a = a - parts[-1]
    return parts


def ring_body(blocks, ks, first_call, last_call, *refs):
    n, nk = len(blocks), len(ks)
    pos, spans = refs[0], refs[1]
    qs = refs[2 : 2 + nk]
    n_kv = 1 + max(b[2] for b in blocks)
    kvs = [refs[2 + nk + at].at[place, :, 0:VBLK] for _, _, at, place in blocks]
    rest = refs[2 + nk + n_kv :]
    n_in = 0 if first_call else 3 * nk
    ins, outs = rest[:n_in], rest[n_in:]
    x, z, c = pos[0], pos[1], pos[2]
    key_bands = [
        device_band(x, (z + dz + NZ) % NZ, c if dc == 0 else 1 - c) for dz, dc, _, _ in blocks
    ]
    biases = {}
    for i, k in enumerate(ks):
        for r in range(2):
            band = device_band((x - k + NX) % NX, z, c if r == 0 else 1 - c)
            for j, b in enumerate(key_bands):
                ok = jnp.logical_and(spans[2 * band] <= b, b < spans[2 * band + 1])
                biases[i, r, j] = jnp.where(ok, 0.0, MASKED).astype(F32)

    def absorb(h):
        q = jnp.concatenate([qs[i][h] for i in range(nk)], axis=0)
        s = jnp.dot(q, jnp.concatenate([kv[h] for kv in kvs], axis=1), preferred_element_type=F32)
        tops, shifts, totals, ws = [], [], [], []
        for i in range(nk):
            at = i * ROWS
            parts = []
            for j in range(n):
                p = s[at : at + ROWS, 128 * j : 128 * (j + 1)]
                parts.append(
                    jnp.concatenate(
                        [p[:256], p[256:272] + biases[i, 0, j], p[272:288] + biases[i, 1, j]], axis=0
                    )
                )
            top = jnp.max(functools.reduce(jnp.maximum, parts), axis=1, keepdims=True)
            m_old = LOWEST if first_call else ins[3 * i][h]
            m_new = jnp.maximum(jnp.broadcast_to(top, (ROWS, HEAD)), m_old)
            shift = m_new * SCALE
            weights = [jnp.exp2(p * SCALE - shift) for p in parts]
            tops.append(m_new)
            shifts.append(shift)
            totals.append(functools.reduce(jnp.add, weights))
            ws.append(jnp.concatenate([w.astype(BF) for w in weights], axis=1))
        v = jnp.concatenate([kv[3 + h] for kv in kvs], axis=0)
        acc = jnp.dot(jnp.concatenate(ws, axis=0), v, preferred_element_type=F32)
        found = []
        for i in range(nk):
            part, total = acc[i * ROWS : (i + 1) * ROWS], totals[i]
            if not first_call:
                alpha = jnp.exp2(ins[3 * i][h] * SCALE - shifts[i])
                total = total + alpha * ins[3 * i + 1][h]
                part = part + alpha * ins[3 * i + 2][h]
            found.append((tops[i], total, part))
        return found

    if not last_call:

        def step(h, carry):
            for i, found in enumerate(absorb(h)):
                for j in range(3):
                    outs[3 * i + j][h] = found[j]
            return carry

        lax.fori_loop(0, 3, step, 0)
        return

    stats = outs[nk]
    lane = lax.broadcasted_iota(jnp.int32, (ROWS, HEAD), 1)

    def step(h, carry):
        for i, (m, l, acc) in enumerate(absorb(h)):
            outs[i][pl.ds(pl.multiple_of(h * ROWS, 16), ROWS), :] = acc.astype(BF)
            l = jnp.sum(l, axis=1, keepdims=True)
            stats[i] = jnp.where(lane == h, m, jnp.where(lane == 3 + h, l, stats[i]))
        return carry

    stats[...] = jnp.zeros_like(stats)
    lax.fori_loop(0, 3, step, 0)
    for i in range(nk):
        write_stats(outs[i], stats[i])


def write_stats(out, stats):
    tiles = [stats[0:128], stats[128:256]]
    tiles.append(jnp.concatenate([stats[256:288], jnp.zeros((96, HEAD), F32)], axis=0))
    for t, tile in enumerate(tiles):
        rows = tile.T
        parts = []
        for h in range(3):
            parts += bf16_parts(rows[h : h + 1], 3) + bf16_parts(rows[3 + h : 4 + h], 2)
        parts.append(jnp.zeros((1, HEAD), F32))
        out[STATS + 16 * t : STATS + 16 * (t + 1), :] = jnp.concatenate(parts, axis=0).astype(BF)


def audio_body(pos, spans, q0, q1, q2, q3, near, u1, d1, u2, d2, u3, d3, far, o0, o1, o2, o3, stats):
    x, z, c = pos[0], pos[1], pos[2]
    arrays = ((near, 0), (u1, -1), (d1, 1), (u2, -2), (d2, 2), (u3, -3), (d3, 3))
    group = lax.broadcasted_iota(jnp.int32, (1, 256), 1) // ABLK
    bands = jnp.zeros((1, 256), jnp.int32)
    places = [(dz, dc) for _, dz in arrays for dc in range(2)] + [(4, 0), (4, 1)]
    for g, (dz, dc) in enumerate(places):
        band = device_band(x, (z + dz + NZ) % NZ, c if dc == 0 else 1 - c)
        bands = jnp.where(group == g, band, bands)
    biases = []
    for k in range(NX):
        for r in range(2):
            mine = device_band((x - k + NX) % NX, z, c if r == 0 else 1 - c)
            ok = (bands >= spans[128 + 2 * mine]) & (bands < spans[129 + 2 * mine])
            biases.append(jnp.where(ok, 0.0, MASKED))
    lane = lax.broadcasted_iota(jnp.int32, (ROWS, HEAD), 1)
    stats[...] = jnp.zeros_like(stats)

    def head(h, carry):
        def rows_of(i):
            return jnp.concatenate(
                [a[r, i, VBLK:TOKENS, :] for a, _ in arrays for r in range(2)] + [far[i]], axis=0
            )

        keys, values = rows_of(h), rows_of(3 + h)
        q = jnp.concatenate([q0[h], q1[h], q2[h], q3[h]], axis=0)
        scores = lax.dot_general(q, keys, (((1,), (1,)), ((), ())), preferred_element_type=F32)
        ws = []
        for k in range(NX):
            s = scores[k * ROWS : (k + 1) * ROWS]
            s = jnp.concatenate(
                [s[0:128] + biases[2 * k], s[128:256] + biases[2 * k + 1], s[256:288]], axis=0
            )
            top = jnp.maximum(s[:, 0:128], s[:, 128:256])
            m = jnp.maximum(jnp.max(top, axis=1, keepdims=True), LOWEST)
            w = jnp.exp2(s * SCALE - m * SCALE)
            l = jnp.sum(w[:, 0:128] + w[:, 128:256], axis=1, keepdims=True)
            ws.append(w.astype(BF))
            stats[k] = jnp.where(lane == h, m, jnp.where(lane == 3 + h, l, stats[k]))
        acc = jnp.dot(jnp.concatenate(ws, axis=0), values, preferred_element_type=F32)
        for k, out in enumerate((o0, o1, o2, o3)):
            out[pl.ds(pl.multiple_of(h * ROWS, 16), ROWS), :] = acc[k * ROWS : (k + 1) * ROWS].astype(BF)
        return carry

    lax.fori_loop(0, 3, head, 0)
    for k, out in enumerate((o0, o1, o2, o3)):
        write_stats(out, stats[k])


def factors(blocks, t):
    stats = [b[STATS + 16 * t : STATS + 16 * (t + 1), :].astype(F32) for b in blocks]
    rows = []
    for h in range(3):
        at = 5 * h
        ms = [(s[at : at + 1] + s[at + 1 : at + 2]) + s[at + 2 : at + 3] for s in stats]
        ls = [s[at + 3 : at + 4] + s[at + 4 : at + 5] for s in stats]
        top = functools.reduce(jnp.maximum, ms)
        ws = [jnp.exp2((m - top) * SCALE) for m in ms]
        inv = 1.0 / functools.reduce(jnp.add, [w * l for w, l in zip(ws, ls)])
        rows += [w * inv for w in ws]
    return jnp.concatenate(rows + [jnp.zeros((116, HEAD), F32)], axis=0).T


def merged(blocks, cols, h, at, size):
    total = None
    for j, b in enumerate(blocks):
        part = b[h * ROWS + at : h * ROWS + at + size, :].astype(F32)
        part = part * cols[:, 4 * h + j : 4 * h + j + 1]
        total = part if total is None else total + part
    return total


def merge_audio_body(p0, p1, p2, p3, out):
    blocks = (p0, p1, p2, p3)
    for t, size in enumerate((128, 128, 32)):
        cols = factors(blocks, t)
        for h in range(3):
            out[h, 128 * t : 128 * t + size, :] = merged(blocks, cols[:size], h, 128 * t, size)


def merge_body(p0, p1, p2, p3, extra, att_own, att_far):
    blocks = (p0, p1, p2, p3)
    audio = factors(blocks, 2)
    for r, att in ((1, att_far), (0, att_own)):
        video = factors(blocks, r)
        for h in range(3):
            for cols, at, size, to in (
                (video, 128 * r, 128, 0),
                (audio[16 * r : 16 * (r + 1)], 256 + 16 * r, 16, 128),
            ):
                total = extra[h, at : at + size, :] + merged(blocks, cols, h, at, size)
                att[h, to : to + size, :] = total.astype(BF)


def project_body(k, pos, att_own, att_near, wv, wa, out):
    c, y = pos[2], pos[3]
    rows = [pl.ds(pl.multiple_of(side * 384, 128), 384) for side in (c, 1 - c)]
    atts = [jnp.concatenate([a[h] for h in range(3)], axis=1) for a in (att_own, att_near)]
    cols = pl.ds(pl.multiple_of(((y + k) % 4) * 768, 128), 768)
    for lo, hi, w in ((0, 128, wv), (128, 144, wa)):
        part = jnp.dot(atts[0][lo:hi], w[rows[0], cols], preferred_element_type=F32)
        part += jnp.dot(atts[1][lo:hi], w[rows[1], cols], preferred_element_type=F32)
        out[lo:hi, :] = part.astype(BF)


def sum_body(p0, p1, p2, p3, video, audio):
    for out, lo, hi in ((video, 0, VBLK), (audio, VBLK, TOKENS)):
        ps = [p[lo:hi, :].astype(F32) for p in (p0, p1, p2, p3)]
        out[...] = ((ps[0] + ps[1]) + (ps[2] + ps[3])).astype(BF)


def moved(array, axis, by):
    n = lax.axis_size(axis)
    return lax.ppermute(array, axis, [(i, (i + by) % n) for i in range(n)])


def program(qv, kv, vv, qa, ka, va, video_spans, audio_spans, wv, wa):
    pos = jnp.stack([lax.axis_index(a) for a in ("x", "z", "c", "tp")]).astype(jnp.int32)
    spans = jnp.concatenate([audio_spans.reshape(-1), video_spans.reshape(-1)])
    block = pltpu.VMEM((VBLK, 768), BF)
    small = pltpu.VMEM((ABLK, 768), BF)
    own, far = kernel_call(
        entry_body, (((9, TOKENS, HEAD), BF),) * 2, [SSPEC] + [HSPEC] * 6, 2,
        scratch=[block, block, block, small, small, small, pltpu.SemaphoreType.DMA((6,))],
        vmem=66000000,
    )(pos, qv, kv, vv, qa, ka, va)
    near = moved(far, "c", 1)
    q_chip, kv_chip, audio = kernel_call(
        chip_body,
        (((3, ROWS, HEAD), BF), ((2, 6, TOKENS, HEAD), BF), ((6, 32, HEAD), BF)),
        [VSPEC] * 2, 0.5,
    )(own, near)
    audio_far = moved(audio, "z", 4)

    ups, downs = [kv_chip], [kv_chip]
    for _ in range(3):
        ups.append(moved(ups[-1], "z", 1))
        downs.append(moved(downs[-1], "z", -1))
    ups.append(moved(ups[3][:1], "z", 1))
    downs.append(moved(downs[3][1:], "z", -1))

    q_x = [q_chip] + [moved(q_chip, "x", k) for k in range(1, NX)]

    def both(dz, at):
        return [(dz, 0, at, 0), (dz, 1, at, 1)]

    groups = [
        ((kv_chip, ups[1], downs[1]), both(0, 0) + both(-1, 1) + both(1, 2)),
        ((ups[2], downs[2]), both(-2, 0) + both(2, 1)),
        ((ups[3], downs[3]), both(-3, 0) + both(3, 1)),
    ]
    state_shape = (((3, ROWS, HEAD), F32),) * 12
    state = ()
    for i, (arrays, blocks) in enumerate(groups):
        n = len(arrays)
        body = functools.partial(ring_body, blocks, (0, 1, 2, 3), i == 0, False)
        aliases = {} if i == 0 else {6 + n + j: j for j in range(12)}
        state = kernel_call(
            body, state_shape, [SSPEC] * 2 + [VSPEC] * (4 + n + len(state)), len(blocks), aliases
        )(pos, spans, *q_x, *arrays, *state)

    aparts = kernel_call(
        audio_body, (((PAYLOAD, HEAD), BF),) * 4, [SSPEC] * 2 + [VSPEC] * 12, 4,
        scratch=[pltpu.VMEM((NX, ROWS, HEAD), F32)],
    )(pos, spans, *q_x, kv_chip, ups[1], downs[1], ups[2], downs[2], ups[3], downs[3], audio_far)
    aback = [aparts[0]] + [moved(aparts[k], "x", -k) for k in range(1, NX)]

    final = [(-4, 0, 0, 0), (4, 1, 1, 0)]
    packed = kernel_call(
        functools.partial(ring_body, final, (0, 1, 2, 3), False, True),
        (((PAYLOAD, HEAD), BF),) * 4, [SSPEC] * 2 + [VSPEC] * 18, 4,
        scratch=[pltpu.VMEM((NX, ROWS, HEAD), F32)],
    )(pos, spans, *q_x, ups[4], downs[4], *state)
    back = [packed[0]] + [None] * 3
    for k in (2, 1, 3):
        back[k] = moved(packed[k], "x", -k)

    (extra,) = kernel_call(merge_audio_body, (((3, ROWS, HEAD), F32),), [VSPEC] * 4, 1)(*aback)
    att_own, att_far = kernel_call(
        merge_body, (((3, TOKENS, HEAD), BF),) * 2, [VSPEC] * 5, 1
    )(*back, extra)
    att_near = moved(att_far, "c", 1)
    parts = []
    for k in (2, 1, 3, 0):
        (part,) = kernel_call(
            functools.partial(project_body, k), (((TOKENS, 768), BF),), [SSPEC] + [VSPEC] * 4, 1,
        )(pos, att_own, att_near, wv, wa)
        parts.append(moved(part, "tp", k) if k else part)
    return kernel_call(sum_body, (((VBLK, 768), BF), ((ABLK, 768), BF)), [VSPEC] * 4, 0.5)(*parts)


def solution(mesh):
    finer = Mesh(mesh.devices.reshape(mesh.shape["tp"], NX, NZ, 2), ("tp", "x", "z", "c"))
    row = P(SEQ, "tp")
    in_specs = (row,) * 6 + (P(), P()) + (P("tp", None),) * 2
    return jax.shard_map(
        program, mesh=finer, in_specs=in_specs, out_specs=(row, row), check_vma=False
    )
```

time: 267 us -> 105 us (0.39)
  waiting for transfers between devices: 117 us -> 34.6 us
  matrix products: 50.6 us -> 0 us
  Pallas kernels: 0 us -> 29.3 us
  blocking collectives: 28.6 us -> 0 us
  starting transfers between devices: 11.9 us -> 38 us
  local copies, waits for them, and re-layouts: 27.6 us -> 1.53 us
  other arithmetic: 16.9 us -> 0.66 us
  between operations: 14.3 us -> 0.82 us
    all_gather x1 -> x0, waiting for transfers between devices: 74 us -> none  [in_one_piece(): result, at, done = (lax.all_gather(both, axis, axis=dim, tiled=True), 0, [])]
    dot_general x10 -> x0, matrix products: 50.6 us -> none  [the longest x4 25.4 us: absorb(): jnp.einsum('hqk,khd->qhd', weights.astype(jnp.bfloat16), values, preferre...]
    all_to_all x1 -> x0, waiting for transfers between devices: 42.8 us -> none  [sent_to_all(): lax.all_to_all(jnp.broadcast_to(array[None], (count, *array.shape)), axis...]
    ppermute x0 -> x23, starting transfers between devices: none -> 38 us  [moved(): return lax.ppermute(array, axis, [(i, (i + by) % n) for i in range(n)])]
    ppermute x0 -> x23, waiting for transfers between devices: none -> 34.6 us  [moved(): return lax.ppermute(array, axis, [(i, (i + by) % n) for i in range(n)])]
    pallas_call x0 -> x14, Pallas kernels: none -> 29.3 us  [the longest x3 13.7 us: program(): kernel_call(body, state_shape, [SSPEC] * 2 + [VSPEC] * (4 + n + len(state...]
    all_to_all x2 -> x0, blocking collectives: 28.6 us -> none  [the longest x1 16.4 us: sent_and_summed(): parts = lax.all_to_all(cut_along(array, dim, count), axis, 0, 0, tiled=True)]
    slice x1 -> x2, local copies, waits for them, and re-layouts: 17.3 us -> 0.03 us  [the longest x1 0.02 us: program(): ups.append(moved(ups[3][:1], 'z', 1))]
  transfers between devices with their start and end apart: 2 -> 23, of which waited for: 2 -> 10; matrix products, arithmetic and copies ran while one was open for 5% -> 1% of each run, Pallas kernels for 0% -> 20%
where the time goes in v1:
time: 105 us
  starting transfers between devices  38 us (36%)
  waiting for transfers between devices  34.6 us (33%)
  Pallas kernels  29.3 us (28%)
  local copies, waits for them, and re-layouts  1.53 us (1%)
    ppermute x23, starting transfers between devices, moved(): return lax.ppermute(array, axis, [(i, (i + by) % n) for i in range(n)])  38 us
    ppermute x23, waiting for transfers between devices, moved(): return lax.ppermute(array, axis, [(i, (i + by) % n) for i in range(n)])  34.6 us
    pallas_call x3, Pallas kernels, program(): kernel_call(body, state_shape, [SSPEC] * 2 + [VSPEC] * (4 + n + len(state...  13.7 us
    pallas_call x4, Pallas kernels, program(): kernel_call(functools.partial(project_body, k), (((TOKENS, 768), BF),), [...  4.15 us
    pallas_call x1, Pallas kernels, program(): kernel_call(functools.partial(ring_body, final, (0, 1, 2, 3), False, True...  3.4 us
    pallas_call x1, Pallas kernels, program(): kernel_call(entry_body, (((9, TOKENS, HEAD), BF),) * 2, [SSPEC] + [HSPEC]...  2.98 us
    pallas_call x1, Pallas kernels, program(): kernel_call(audio_body, (((PAYLOAD, HEAD), BF),) * 4, [SSPEC] * 2 + [VSPE...  2.84 us
  transfers between devices with their start and end apart: 23, of which 10 were waited for; matrix products, arithmetic and copies ran while one was open for 1% of the time, Pallas kernels for 20%

profile of v1, /device:TPU:1, one launch (start us, length us, event | category | flops | bytes accessed | tf_op | source)
XLA Modules:
  0.0 104.9 jit_solution(3807358611698813094)
XLA Ops:
  0.7 0.7 pad_add_fusion.pos.refs_0_
  1.3 3.0 %shard_map.113 = (bf16[9,144,128]{2,1,0:T(8,128)(2,1)}, bf16[9,144,128]{2,1,0:T(8,128)(2,1)}) custom-call(s32[4]{0:T(128)} %pad_add_fusion.pos.refs_0_, bf16[128,768]{1,0:T(8,128)(2,1)} %q_hbm.1, bf16[128,768]{1,0:T(8,128)(2,1)} %k_hbm.1, bf16[128,768]{1,0:T(8,128)(2,1)} %v_hbm.1, bf16[16,768]{1,0:T(8,128)(2,1)} %qa_hbm.1, bf16[16,768]{1,0:T(8,128)(2,1)} %ka_hbm.1, ...), custom_call_target="tpu_custom_call" | custom-call | flops 2000000000 | bytes 65536 | tf_op jit(solution)/shard_map/pallas_call | solution.py:310
  4.3 3.3 %collective-permute-start = (bf16[9,144,128]{2,1,0:T(8,128)(2,1)}, bf16[9,144,128]{2,1,0:T(8,128)(2,1)S(1)}, u32[]{:S(2)}, u32[]{:S(2)}) collective-permute-start(bf16[9,144,128]{2,1,0:T(8,128)(2,1)} %get-tuple-element.54), channel_id=1, source_target_pairs={{0,1},{1,0},{2,3},{3,2},{4,5},{5,4},{6,7},{7,6},{8,9},{9,8},{10,11... | collective-permute-start | bytes 995336 | tf_op jit(solution)/shard_map/ppermute | solution.py:302
  7.6 1.5 %collective-permute-done.near = bf16[9,144,128]{2,1,0:T(8,128)(2,1)S(1)} collective-permute-done((bf16[9,144,128]{2,1,0:T(8,128)(2,1)}, bf16[9,144,128]{2,1,0:T(8,128)(2,1)S(1)}, u32[]{:S(2)}, u32[]{:S(2)}) %collective-permute-start) | collective-permute-done | bytes 331808 | tf_op jit(solution)/shard_map/ppermute | solution.py:302
  9.1 1.0 copy-done.1
  10.0 0.1 shard_map.114
  10.1 3.9 %collective-permute-start.8 = (bf16[2,6,144,128]{3,2,1,0:T(8,128)(2,1)S(1)}, bf16[2,6,144,128]{3,2,1,0:T(8,128)(2,1)S(1)}, u32[]{:S(2)}, u32[]{:S(2)}) collective-permute-start(bf16[2,6,144,128]{3,2,1,0:T(8,128)(2,1)S(1)} %get-tuple-element.56.refs_6_.near), channel_id=1, source_target_pairs={{0,14},{2,0},{4,2},{6,4},{8,6},{10,8},{12,10},{14,12},{1,15},{3,1}... | collective-permute-start | bytes 1327112 | tf_op jit(solution)/shard_map/ppermute | solution.py:302
  14.0 0.0 collective-permute-start.4
  14.0 9.2 %collective-permute-done.8.refs_8_.d1 = bf16[2,6,144,128]{3,2,1,0:T(8,128)(2,1)S(1)} collective-permute-done((bf16[2,6,144,128]{3,2,1,0:T(8,128)(2,1)S(1)}, bf16[2,6,144,128]{3,2,1,0:T(8,128)(2,1)S(1)}, u32[]{:S(2)}, u32[]{:S(2)}) %collective-permute-start.8) | collective-permute-done | bytes 442400 | tf_op jit(solution)/shard_map/ppermute | solution.py:302
  23.2 3.4 %collective-permute-start.9 = (bf16[2,6,144,128]{3,2,1,0:T(8,128)(2,1)S(1)}, bf16[2,6,144,128]{3,2,1,0:T(8,128)(2,1)S(1)}, u32[]{:S(2)}, u32[]{:S(2)}) collective-permute-start(bf16[2,6,144,128]{3,2,1,0:T(8,128)(2,1)S(1)} %collective-permute-done.8.refs_8_.d1), channel_id=1, source_target_pairs={{0,14},{2,0},{4,2},{6,4},{8,6},{10,8},{12,10},{14,12},{1,15},{3,1}... | collective-permute-start | bytes 1327112 | tf_op jit(solution)/shard_map/ppermute | solution.py:302
  26.6 0.0 collective-permute-done.4.refs_7_.u1
  26.6 0.0 collective-permute-start.5
  26.6 0.1 copy.38
  26.7 0.1 reshape.10
  26.9 0.1 copy.39
  27.0 0.1 reshape.11
  27.1 1.3 %collective-permute-start.1 = (bf16[3,288,128]{2,1,0:T(8,128)(2,1)S(1)}, bf16[3,288,128]{2,1,0:T(8,128)(2,1)S(1)}, u32[]{:S(2)}, u32[]{:S(2)}) collective-permute-start(bf16[3,288,128]{2,1,0:T(8,128)(2,1)S(1)} %get-tuple-element.55.refs_2_.q0), channel_id=1, source_target_pairs={{0,16},{16,32},{32,48},{48,0},{1,17},{17,33},{33,49},{49,1},{2,18}... | collective-permute-start | bytes 663560 | tf_op jit(solution)/shard_map/ppermute | solution.py:302
  28.4 2.5 %collective-permute-start.2 = (bf16[3,288,128]{2,1,0:T(8,128)(2,1)S(1)}, bf16[3,288,128]{2,1,0:T(8,128)(2,1)S(1)}, u32[]{:S(2)}, u32[]{:S(2)}) collective-permute-start(bf16[3,288,128]{2,1,0:T(8,128)(2,1)S(1)} %get-tuple-element.55.refs_2_.q0), channel_id=1, source_target_pairs={{0,32},{16,48},{32,0},{48,16},{1,33},{17,49},{33,1},{49,17},{2,34}... | collective-permute-start | bytes 663560 | tf_op jit(solution)/shard_map/ppermute | solution.py:302
  30.8 1.2 %collective-permute-start.3 = (bf16[3,288,128]{2,1,0:T(8,128)(2,1)S(1)}, bf16[3,288,128]{2,1,0:T(8,128)(2,1)S(1)}, u32[]{:S(2)}, u32[]{:S(2)}) collective-permute-start(bf16[3,288,128]{2,1,0:T(8,128)(2,1)S(1)} %get-tuple-element.55.refs_2_.q0), channel_id=1, source_target_pairs={{0,48},{16,0},{32,16},{48,32},{1,49},{17,1},{33,17},{49,33},{2,50}... | collective-permute-start | bytes 663560 | tf_op jit(solution)/shard_map/ppermute | solution.py:302
  32.0 1.8 %collective-permute-done.1.refs_3_.q1 = bf16[3,288,128]{2,1,0:T(8,128)(2,1)S(1)} collective-permute-done((bf16[3,288,128]{2,1,0:T(8,128)(2,1)S(1)}, bf16[3,288,128]{2,1,0:T(8,128)(2,1)S(1)}, u32[]{:S(2)}, u32[]{:S(2)}) %collective-permute-start.1) | collective-permute-done | bytes 221216 | tf_op jit(solution)/shard_map/ppermute | solution.py:302
  33.9 1.3 %collective-permute-start.15 = (bf16[6,32,128]{2,1,0:T(8,128)(2,1)S(1)}, bf16[6,32,128]{2,1,0:T(8,128)(2,1)S(1)}, u32[]{:S(2)}, u32[]{:S(2)}) collective-permute-start(bf16[6,32,128]{2,1,0:T(8,128)(2,1)S(1)} %get-tuple-element.97), channel_id=1, source_target_pairs={{0,8},{2,10},{4,12},{6,14},{8,0},{10,2},{12,4},{14,6},{1,9},{3,11}... | collective-permute-start | bytes 147464 | tf_op jit(solution)/shard_map/ppermute | solution.py:302
  35.2 0.0 collective-permute-done.9.refs_7_.d2
  35.2 3.1 %collective-permute-start.10 = (bf16[2,6,144,128]{3,2,1,0:T(8,128)(2,1)S(1)}, bf16[2,6,144,128]{3,2,1,0:T(8,128)(2,1)S(1)}, u32[]{:S(2)}, u32[]{:S(2)}) collective-permute-start(bf16[2,6,144,128]{3,2,1,0:T(8,128)(2,1)S(1)} %collective-permute-done.9.refs_7_.d2), channel_id=1, source_target_pairs={{0,14},{2,0},{4,2},{6,4},{8,6},{10,8},{12,10},{14,12},{1,15},{3,1}... | collective-permute-start | bytes 1327112 | tf_op jit(solution)/shard_map/ppermute | solution.py:302
  38.3 0.0 collective-permute-done.5.refs_6_.u2
  38.3 0.0 collective-permute-start.6
  38.3 1.3 %collective-permute-done.2.refs_4_.q2 = bf16[3,288,128]{2,1,0:T(8,128)(2,1)S(1)} collective-permute-done((bf16[3,288,128]{2,1,0:T(8,128)(2,1)S(1)}, bf16[3,288,128]{2,1,0:T(8,128)(2,1)S(1)}, u32[]{:S(2)}, u32[]{:S(2)}) %collective-permute-start.2) | collective-permute-done | bytes 221216 | tf_op jit(solution)/shard_map/ppermute | solution.py:302
  39.6 5.1 %shard_map.115 = (f32[3,288,128]{2,1,0:T(8,128)S(1)}, f32[3,288,128]{2,1,0:T(8,128)S(1)}, f32[3,288,128]{2,1,0:T(8,128)S(1)}, f32[3,288,128]{2,1,0:T(8,128)S(1)}...) custom-call(s32[4]{0:T(128)S(1)} %copy-done, ...), custom_call_target="tpu_custom_call" | custom-call | flops 6000000000 | bytes 65536 | tf_op jit(solution)/shard_map/pallas_call | solution.py:346
  44.7 4.3 %shard_map.116 = (f32[3,288,128]{2,1,0:T(8,128)S(1)}, f32[3,288,128]{2,1,0:T(8,128)S(1)}, f32[3,288,128]{2,1,0:T(8,128)S(1)}, f32[3,288,128]{2,1,0:T(8,128)S(1)}...) custom-call(s32[4]{0:T(128)S(1)} %copy-done, ...), custom_call_target="tpu_custom_call", output_to_operand_aliasing={{0}: (8, {}), {1}: (9, {}), {2}: (10, {}), {3}: (11, {}), {... | custom-call | flops 4000000000 | bytes 65536 | tf_op jit(solution)/shard_map/pallas_call | solution.py:346
  49.0 0.0 collective-permute-done.15.far
  49.0 0.0 collective-permute-done.10.refs_7_.d3
  49.0 2.8 %shard_map.119 = (bf16[912,128]{1,0:T(8,128)(2,1)S(1)}, bf16[912,128]{1,0:T(8,128)(2,1)S(1)}, bf16[912,128]{1,0:T(8,128)(2,1)S(1)}, bf16[912,128]{1,0:T(8,128)(2,1)S(1)}) custom-call(s32[4]{0:T(128)S(1)} %copy-done, s32[256]{0:T(256)S(1)} %constant_dynamic-update-slice_fusion.refs_1_.spans, bf16[3,288,128]{2,1,0:T(8,128)(2,1)S(1)} %get-tuple-element.55.refs_2_.q0, ...), custom_call_target="tpu_custom_call" | custom-call | flops 4000000000 | bytes 65536 | tf_op jit(solution)/shard_map/pallas_call | solution.py:350
  51.9 3.3 %collective-permute-start.16 = (bf16[912,128]{1,0:T(8,128)(2,1)S(1)}, bf16[912,128]{1,0:T(8,128)(2,1)S(1)}, u32[]{:S(2)}, u32[]{:S(2)}) collective-permute-start(bf16[912,128]{1,0:T(8,128)(2,1)S(1)} %get-tuple-element.99), channel_id=1, source_target_pairs={{0,48},{16,0},{32,16},{48,32},{1,49},{17,1},{33,17},{49,33},{2,50}... | collective-permute-start | bytes 700424 | tf_op jit(solution)/shard_map/ppermute | solution.py:302
  55.1 1.0 collective-permute-start.17
  56.2 0.0 collective-permute-start.18
  56.2 2.7 %collective-permute-start.11 = (bf16[1,6,144,128]{3,2,1,0:T(8,128)(2,1)S(1)}, bf16[1,6,144,128]{3,2,1,0:T(8,128)(2,1)S(1)}, u32[]{:S(2)}, u32[]{:S(2)}) collective-permute-start(bf16[1,6,144,128]{3,2,1,0:T(8,128)(2,1)S(1)} %slice.9), channel_id=1, source_target_pairs={{0,14},{2,0},{4,2},{6,4},{8,6},{10,8},{12,10},{14,12},{1,15},{3,1}... | collective-permute-start | bytes 663560 | tf_op jit(solution)/shard_map/ppermute | solution.py:302
  58.9 0.1 collective-permute-start.7
  59.0 4.3 %shard_map.117 = (f32[3,288,128]{2,1,0:T(8,128)S(1)}, f32[3,288,128]{2,1,0:T(8,128)S(1)}, f32[3,288,128]{2,1,0:T(8,128)S(1)}, f32[3,288,128]{2,1,0:T(8,128)S(1)}...) custom-call(s32[4]{0:T(128)S(1)} %copy-done, ...), custom_call_target="tpu_custom_call", output_to_operand_aliasing={{0}: (8, {}), {1}: (9, {}), {2}: (10, {}), {3}: (11, {}), {... | custom-call | flops 4000000000 | bytes 65536 | tf_op jit(solution)/shard_map/pallas_call | solution.py:346
  63.3 0.0 collective-permute-done.11.refs_7_
  63.3 2.0 %collective-permute-done.7.refs_6_ = bf16[1,6,144,128]{3,2,1,0:T(8,128)(2,1)S(1)} collective-permute-done((bf16[1,6,144,128]{3,2,1,0:T(8,128)(2,1)S(1)}, bf16[1,6,144,128]{3,2,1,0:T(8,128)(2,1)S(1)}, u32[]{:S(2)}, u32[]{:S(2)}) %collective-permute-start.7) | collective-permute-done | bytes 221216 | tf_op jit(solution)/shard_map/ppermute | solution.py:302
  65.3 3.4 %shard_map.118 = (bf16[912,128]{1,0:T(8,128)(2,1)S(1)}, bf16[912,128]{1,0:T(8,128)(2,1)S(1)}, bf16[912,128]{1,0:T(8,128)(2,1)S(1)}, bf16[912,128]{1,0:T(8,128)(2,1)S(1)}) custom-call(s32[4]{0:T(128)S(1)} %copy-done, s32[256]{0:T(256)S(1)} %constant_dynamic-update-slice_fusion.refs_1_.spans, bf16[3,288,128]{2,1,0:T(8,128)(2,1)S(1)} %get-tuple-element.55.refs_2_.q0, ...), custom_call_target="tpu_custom_call" | custom-call | flops 4000000000 | bytes 65536 | tf_op jit(solution)/shard_map/pallas_call | solution.py:357
  68.7 2.8 %collective-permute-start.12 = (bf16[912,128]{1,0:T(8,128)(2,1)S(1)}, bf16[912,128]{1,0:T(8,128)(2,1)S(1)}, u32[]{:S(2)}, u32[]{:S(2)}) collective-permute-start(bf16[912,128]{1,0:T(8,128)(2,1)S(1)} %get-tuple-element.94), channel_id=1, source_target_pairs={{0,48},{16,0},{32,16},{48,32},{1,49},{17,1},{33,17},{49,33},{2,50}... | collective-permute-start | bytes 700424 | tf_op jit(solution)/shard_map/ppermute | solution.py:302
  71.5 0.3 collective-permute-start.13
  71.8 0.0 collective-permute-done.16.p1
  71.8 0.4 collective-permute-start.14
  72.2 0.0 collective-permute-done.17.p2
  72.2 0.0 collective-permute-done.18.p3
  72.2 0.7 shard_map.120.extra
  72.9 5.1 %collective-permute-done.12.p1 = bf16[912,128]{1,0:T(8,128)(2,1)S(1)} collective-permute-done((bf16[912,128]{1,0:T(8,128)(2,1)S(1)}, bf16[912,128]{1,0:T(8,128)(2,1)S(1)}, u32[]{:S(2)}, u32[]{:S(2)}) %collective-permute-start.12) | collective-permute-done | bytes 233504 | tf_op jit(solution)/shard_map/ppermute | solution.py:302
  78.0 0.0 collective-permute-done.13.p2
  78.0 5.3 %collective-permute-done.14.p3 = bf16[912,128]{1,0:T(8,128)(2,1)S(1)} collective-permute-done((bf16[912,128]{1,0:T(8,128)(2,1)S(1)}, bf16[912,128]{1,0:T(8,128)(2,1)S(1)}, u32[]{:S(2)}, u32[]{:S(2)}) %collective-permute-start.14) | collective-permute-done | bytes 233504 | tf_op jit(solution)/shard_map/ppermute | solution.py:302
  83.3 0.7 shard_map.121
  84.1 2.8 %collective-permute-start.19 = (bf16[3,144,128]{2,1,0:T(8,128)(2,1)S(1)}, bf16[3,144,128]{2,1,0:T(8,128)(2,1)S(1)}, u32[]{:S(2)}, u32[]{:S(2)}) collective-permute-start(bf16[3,144,128]{2,1,0:T(8,128)(2,1)S(1)} %get-tuple-element.103), channel_id=1, source_target_pairs={{0,1},{1,0},{2,3},{3,2},{4,5},{5,4},{6,7},{7,6},{8,9},{9,8},{10,11... | collective-permute-start | bytes 331784 | tf_op jit(solution)/shard_map/ppermute | solution.py:302
  86.9 1.0 collective-permute-done.19.att_near
  87.9 1.0 shard_map.124
  88.9 2.8 %collective-permute-start.22 = (bf16[144,768]{1,0:T(8,128)(2,1)S(1)}, bf16[144,768]{1,0:T(8,128)(2,1)S(1)}, u32[]{:S(2)}, u32[]{:S(2)}) collective-permute-start(bf16[144,768]{1,0:T(8,128)(2,1)S(1)} %shard_map.124), channel_id=1, source_target_pairs={{0,192},{64,0},{128,64},{192,128},{1,193},{65,1},{129,65},{193,129... | collective-permute-start | bytes 663560 | tf_op jit(solution)/shard_map/ppermute | solution.py:302
  91.7 1.0 shard_map.123
  92.8 0.1 collective-permute-start.21
  92.9 1.0 shard_map.122
  93.9 1.7 %collective-permute-start.20 = (bf16[144,768]{1,0:T(8,128)(2,1)S(1)}, bf16[144,768]{1,0:T(8,128)(2,1)S(1)}, u32[]{:S(2)}, u32[]{:S(2)}) collective-permute-start(bf16[144,768]{1,0:T(8,128)(2,1)S(1)} %shard_map.122), channel_id=1, source_target_pairs={{0,128},{64,192},{128,0},{192,64},{1,129},{65,193},{129,1},{193,65... | collective-permute-start | bytes 663560 | tf_op jit(solution)/shard_map/ppermute | solution.py:302
  95.6 1.0 shard_map.125.p3
  96.7 0.0 collective-permute-done.22.p2
  96.7 4.8 %collective-permute-done.21.p1 = bf16[144,768]{1,0:T(8,128)(2,1)S(1)} collective-permute-done((bf16[144,768]{1,0:T(8,128)(2,1)S(1)}, bf16[144,768]{1,0:T(8,128)(2,1)S(1)}, u32[]{:S(2)}, u32[]{:S(2)}) %collective-permute-start.21) | collective-permute-done | bytes 221216 | tf_op jit(solution)/shard_map/ppermute | solution.py:302
  101.4 2.7 %collective-permute-done.20.p0 = bf16[144,768]{1,0:T(8,128)(2,1)S(1)} collective-permute-done((bf16[144,768]{1,0:T(8,128)(2,1)S(1)}, bf16[144,768]{1,0:T(8,128)(2,1)S(1)}, u32[]{:S(2)}, u32[]{:S(2)}) %collective-permute-start.20) | collective-permute-done | bytes 221216 | tf_op jit(solution)/shard_map/ppermute | solution.py:302
  104.2 0.8 shard_map.126
  (24 shorter events, 0.1 us)
Async XLA Ops:
  0.6 26.0 %copy-start.2 = (s32[64,2]{0,1:T(2,128)S(1)}, s32[64,2]{0,1:T(2,128)}, u32[]{:S(2)}) copy-start(s32[64,2]{0,1:T(2,128)} %param.17) | copy-start | bytes 1540
  0.6 26.2 %copy-start.3 = (s32[64,2]{0,1:T(2,128)S(1)}, s32[64,2]{0,1:T(2,128)}, u32[]{:S(2)}) copy-start(s32[64,2]{0,1:T(2,128)} %param.16) | copy-start | bytes 1540
  1.3 38.3 %copy-start = (s32[4]{0:T(128)S(1)}, s32[4]{0:T(128)}, u32[]{:S(2)}) copy-start(s32[4]{0:T(128)} %pad_add_fusion.pos.refs_0_) | copy-start | bytes 52
  4.3 4.8 %collective-permute-start = (bf16[9,144,128]{2,1,0:T(8,128)(2,1)}, bf16[9,144,128]{2,1,0:T(8,128)(2,1)S(1)}, u32[]{:S(2)}, u32[]{:S(2)}) collective-permute-start(bf16[9,144,128]{2,1,0:T(8,128)(2,1)} %get-tuple-element.54), channel_id=1, source_target_pairs={{0,1},{1,0},{2,3},{3,2},{4,5},{5,4},{6,7},{7,6},{8,9},{9,8},{10,11... | collective-permute-start | bytes 995336 | tf_op jit(solution)/shard_map/ppermute | solution.py:302
  9.1 1.0 copy-start.1
  10.1 13.1 %collective-permute-start.8 = (bf16[2,6,144,128]{3,2,1,0:T(8,128)(2,1)S(1)}, bf16[2,6,144,128]{3,2,1,0:T(8,128)(2,1)S(1)}, u32[]{:S(2)}, u32[]{:S(2)}) collective-permute-start(bf16[2,6,144,128]{3,2,1,0:T(8,128)(2,1)S(1)} %get-tuple-element.56.refs_6_.near), channel_id=1, source_target_pairs={{0,14},{2,0},{4,2},{6,4},{8,6},{10,8},{12,10},{14,12},{1,15},{3,1}... | collective-permute-start | bytes 1327112 | tf_op jit(solution)/shard_map/ppermute | solution.py:302
  14.0 12.6 %collective-permute-start.4 = (bf16[2,6,144,128]{3,2,1,0:T(8,128)(2,1)S(1)}, bf16[2,6,144,128]{3,2,1,0:T(8,128)(2,1)S(1)}, u32[]{:S(2)}, u32[]{:S(2)}) collective-permute-start(bf16[2,6,144,128]{3,2,1,0:T(8,128)(2,1)S(1)} %get-tuple-element.56.refs_6_.near), channel_id=1, source_target_pairs={{0,2},{2,4},{4,6},{6,8},{8,10},{10,12},{12,14},{14,0},{1,3},{3,5},... | collective-permute-start | bytes 1327112 | tf_op jit(solution)/shard_map/ppermute | solution.py:302
  23.2 12.0 %collective-permute-start.9 = (bf16[2,6,144,128]{3,2,1,0:T(8,128)(2,1)S(1)}, bf16[2,6,144,128]{3,2,1,0:T(8,128)(2,1)S(1)}, u32[]{:S(2)}, u32[]{:S(2)}) collective-permute-start(bf16[2,6,144,128]{3,2,1,0:T(8,128)(2,1)S(1)} %collective-permute-done.8.refs_8_.d1), channel_id=1, source_target_pairs={{0,14},{2,0},{4,2},{6,4},{8,6},{10,8},{12,10},{14,12},{1,15},{3,1}... | collective-permute-start | bytes 1327112 | tf_op jit(solution)/shard_map/ppermute | solution.py:302
  26.6 11.7 %collective-permute-start.5 = (bf16[2,6,144,128]{3,2,1,0:T(8,128)(2,1)S(1)}, bf16[2,6,144,128]{3,2,1,0:T(8,128)(2,1)S(1)}, u32[]{:S(2)}, u32[]{:S(2)}) collective-permute-start(bf16[2,6,144,128]{3,2,1,0:T(8,128)(2,1)S(1)} %collective-permute-done.4.refs_7_.u1), channel_id=1, source_target_pairs={{0,2},{2,4},{4,6},{6,8},{8,10},{10,12},{12,14},{14,0},{1,3},{3,5},... | collective-permute-start | bytes 1327112 | tf_op jit(solution)/shard_map/ppermute | solution.py:302
  27.1 6.8 %collective-permute-start.1 = (bf16[3,288,128]{2,1,0:T(8,128)(2,1)S(1)}, bf16[3,288,128]{2,1,0:T(8,128)(2,1)S(1)}, u32[]{:S(2)}, u32[]{:S(2)}) collective-permute-start(bf16[3,288,128]{2,1,0:T(8,128)(2,1)S(1)} %get-tuple-element.55.refs_2_.q0), channel_id=1, source_target_pairs={{0,16},{16,32},{32,48},{48,0},{1,17},{17,33},{33,49},{49,1},{2,18}... | collective-permute-start | bytes 663560 | tf_op jit(solution)/shard_map/ppermute | solution.py:302
  28.4 11.2 %collective-permute-start.2 = (bf16[3,288,128]{2,1,0:T(8,128)(2,1)S(1)}, bf16[3,288,128]{2,1,0:T(8,128)(2,1)S(1)}, u32[]{:S(2)}, u32[]{:S(2)}) collective-permute-start(bf16[3,288,128]{2,1,0:T(8,128)(2,1)S(1)} %get-tuple-element.55.refs_2_.q0), channel_id=1, source_target_pairs={{0,32},{16,48},{32,0},{48,16},{1,33},{17,49},{33,1},{49,17},{2,34}... | collective-permute-start | bytes 663560 | tf_op jit(solution)/shard_map/ppermute | solution.py:302
  30.8 8.8 %collective-permute-start.3 = (bf16[3,288,128]{2,1,0:T(8,128)(2,1)S(1)}, bf16[3,288,128]{2,1,0:T(8,128)(2,1)S(1)}, u32[]{:S(2)}, u32[]{:S(2)}) collective-permute-start(bf16[3,288,128]{2,1,0:T(8,128)(2,1)S(1)} %get-tuple-element.55.refs_2_.q0), channel_id=1, source_target_pairs={{0,48},{16,0},{32,16},{48,32},{1,49},{17,1},{33,17},{49,33},{2,50}... | collective-permute-start | bytes 663560 | tf_op jit(solution)/shard_map/ppermute | solution.py:302
  33.9 15.1 %collective-permute-start.15 = (bf16[6,32,128]{2,1,0:T(8,128)(2,1)S(1)}, bf16[6,32,128]{2,1,0:T(8,128)(2,1)S(1)}, u32[]{:S(2)}, u32[]{:S(2)}) collective-permute-start(bf16[6,32,128]{2,1,0:T(8,128)(2,1)S(1)} %get-tuple-element.97), channel_id=1, source_target_pairs={{0,8},{2,10},{4,12},{6,14},{8,0},{10,2},{12,4},{14,6},{1,9},{3,11}... | collective-permute-start | bytes 147464 | tf_op jit(solution)/shard_map/ppermute | solution.py:302
  35.2 13.8 %collective-permute-start.10 = (bf16[2,6,144,128]{3,2,1,0:T(8,128)(2,1)S(1)}, bf16[2,6,144,128]{3,2,1,0:T(8,128)(2,1)S(1)}, u32[]{:S(2)}, u32[]{:S(2)}) collective-permute-start(bf16[2,6,144,128]{3,2,1,0:T(8,128)(2,1)S(1)} %collective-permute-done.9.refs_7_.d2), channel_id=1, source_target_pairs={{0,14},{2,0},{4,2},{6,4},{8,6},{10,8},{12,10},{14,12},{1,15},{3,1}... | collective-permute-start | bytes 1327112 | tf_op jit(solution)/shard_map/ppermute | solution.py:302
  38.3 10.7 %collective-permute-start.6 = (bf16[2,6,144,128]{3,2,1,0:T(8,128)(2,1)S(1)}, bf16[2,6,144,128]{3,2,1,0:T(8,128)(2,1)S(1)}, u32[]{:S(2)}, u32[]{:S(2)}) collective-permute-start(bf16[2,6,144,128]{3,2,1,0:T(8,128)(2,1)S(1)} %collective-permute-done.5.refs_6_.u2), channel_id=1, source_target_pairs={{0,2},{2,4},{4,6},{6,8},{8,10},{10,12},{12,14},{14,0},{1,3},{3,5},... | collective-permute-start | bytes 1327112 | tf_op jit(solution)/shard_map/ppermute | solution.py:302
  51.9 19.9 %collective-permute-start.16 = (bf16[912,128]{1,0:T(8,128)(2,1)S(1)}, bf16[912,128]{1,0:T(8,128)(2,1)S(1)}, u32[]{:S(2)}, u32[]{:S(2)}) collective-permute-start(bf16[912,128]{1,0:T(8,128)(2,1)S(1)} %get-tuple-element.99), channel_id=1, source_target_pairs={{0,48},{16,0},{32,16},{48,32},{1,49},{17,1},{33,17},{49,33},{2,50}... | collective-permute-start | bytes 700424 | tf_op jit(solution)/shard_map/ppermute | solution.py:302
  55.1 17.0 %collective-permute-start.17 = (bf16[912,128]{1,0:T(8,128)(2,1)S(1)}, bf16[912,128]{1,0:T(8,128)(2,1)S(1)}, u32[]{:S(2)}, u32[]{:S(2)}) collective-permute-start(bf16[912,128]{1,0:T(8,128)(2,1)S(1)} %get-tuple-element.100), channel_id=1, source_target_pairs={{0,32},{16,48},{32,0},{48,16},{1,33},{17,49},{33,1},{49,17},{2,34}... | collective-permute-start | bytes 700424 | tf_op jit(solution)/shard_map/ppermute | solution.py:302
  56.2 16.0 %collective-permute-start.18 = (bf16[912,128]{1,0:T(8,128)(2,1)S(1)}, bf16[912,128]{1,0:T(8,128)(2,1)S(1)}, u32[]{:S(2)}, u32[]{:S(2)}) collective-permute-start(bf16[912,128]{1,0:T(8,128)(2,1)S(1)} %get-tuple-element.101), channel_id=1, source_target_pairs={{0,16},{16,32},{32,48},{48,0},{1,17},{17,33},{33,49},{49,1},{2,18}... | collective-permute-start | bytes 700424 | tf_op jit(solution)/shard_map/ppermute | solution.py:302
  56.2 7.1 %collective-permute-start.11 = (bf16[1,6,144,128]{3,2,1,0:T(8,128)(2,1)S(1)}, bf16[1,6,144,128]{3,2,1,0:T(8,128)(2,1)S(1)}, u32[]{:S(2)}, u32[]{:S(2)}) collective-permute-start(bf16[1,6,144,128]{3,2,1,0:T(8,128)(2,1)S(1)} %slice.9), channel_id=1, source_target_pairs={{0,14},{2,0},{4,2},{6,4},{8,6},{10,8},{12,10},{14,12},{1,15},{3,1}... | collective-permute-start | bytes 663560 | tf_op jit(solution)/shard_map/ppermute | solution.py:302
  58.9 6.4 %collective-permute-start.7 = (bf16[1,6,144,128]{3,2,1,0:T(8,128)(2,1)S(1)}, bf16[1,6,144,128]{3,2,1,0:T(8,128)(2,1)S(1)}, u32[]{:S(2)}, u32[]{:S(2)}) collective-permute-start(bf16[1,6,144,128]{3,2,1,0:T(8,128)(2,1)S(1)} %slice.8), channel_id=1, source_target_pairs={{0,2},{2,4},{4,6},{6,8},{8,10},{10,12},{12,14},{14,0},{1,3},{3,5},... | collective-permute-start | bytes 663560 | tf_op jit(solution)/shard_map/ppermute | solution.py:302
  65.3 22.6 %slice-start = ((s8[4718592]{0:T(1024)(128)(4,1)}), s8[4194304]{0:T(1024)(128)(4,1)S(1)}, s32[]{:S(2)}) async-start(s8[4718592]{0:T(1024)(128)(4,1)} %bitcast.4), calls=%async_computation | async-start | bytes 8388608
  65.3 22.6 %slice-start.2 = ((s8[4718592]{0:T(1024)(128)(4,1)}), s8[4194304]{0:T(1024)(128)(4,1)S(1)}, s32[]{:S(2)}) async-start(s8[4718592]{0:T(1024)(128)(4,1)} %bitcast.6), calls=%async_computation.2 | async-start | bytes 8388608
  65.3 22.6 %slice-start.1 = ((s8[4718592]{0:T(1024)(128)(4,1)}), s8[524288]{0:T(1024)(128)(4,1)S(1)}, s32[]{:S(2)}) async-start(s8[4718592]{0:T(1024)(128)(4,1)} %bitcast.4), calls=%async_computation.1 | async-start | bytes 1048576
  65.3 22.6 %slice-start.3 = ((s8[4718592]{0:T(1024)(128)(4,1)}), s8[524288]{0:T(1024)(128)(4,1)S(1)}, s32[]{:S(2)}) async-start(s8[4718592]{0:T(1024)(128)(4,1)} %bitcast.6), calls=%async_computation.3 | async-start | bytes 1048576
  68.7 9.3 %collective-permute-start.12 = (bf16[912,128]{1,0:T(8,128)(2,1)S(1)}, bf16[912,128]{1,0:T(8,128)(2,1)S(1)}, u32[]{:S(2)}, u32[]{:S(2)}) collective-permute-start(bf16[912,128]{1,0:T(8,128)(2,1)S(1)} %get-tuple-element.94), channel_id=1, source_target_pairs={{0,48},{16,0},{32,16},{48,32},{1,49},{17,1},{33,17},{49,33},{2,50}... | collective-permute-start | bytes 700424 | tf_op jit(solution)/shard_map/ppermute | solution.py:302
  71.5 6.5 %collective-permute-start.13 = (bf16[912,128]{1,0:T(8,128)(2,1)S(1)}, bf16[912,128]{1,0:T(8,128)(2,1)S(1)}, u32[]{:S(2)}, u32[]{:S(2)}) collective-permute-start(bf16[912,128]{1,0:T(8,128)(2,1)S(1)} %get-tuple-element.95), channel_id=1, source_target_pairs={{0,32},{16,48},{32,0},{48,16},{1,33},{17,49},{33,1},{49,17},{2,34}... | collective-permute-start | bytes 700424 | tf_op jit(solution)/shard_map/ppermute | solution.py:302
  71.8 11.6 %collective-permute-start.14 = (bf16[912,128]{1,0:T(8,128)(2,1)S(1)}, bf16[912,128]{1,0:T(8,128)(2,1)S(1)}, u32[]{:S(2)}, u32[]{:S(2)}) collective-permute-start(bf16[912,128]{1,0:T(8,128)(2,1)S(1)} %get-tuple-element.96), channel_id=1, source_target_pairs={{0,16},{16,32},{32,48},{48,0},{1,17},{17,33},{33,49},{49,1},{2,18}... | collective-permute-start | bytes 700424 | tf_op jit(solution)/shard_map/ppermute | solution.py:302
  84.1 3.8 %collective-permute-start.19 = (bf16[3,144,128]{2,1,0:T(8,128)(2,1)S(1)}, bf16[3,144,128]{2,1,0:T(8,128)(2,1)S(1)}, u32[]{:S(2)}, u32[]{:S(2)}) collective-permute-start(bf16[3,144,128]{2,1,0:T(8,128)(2,1)S(1)} %get-tuple-element.103), channel_id=1, source_target_pairs={{0,1},{1,0},{2,3},{3,2},{4,5},{5,4},{6,7},{7,6},{8,9},{9,8},{10,11... | collective-permute-start | bytes 331784 | tf_op jit(solution)/shard_map/ppermute | solution.py:302
  88.9 7.7 %collective-permute-start.22 = (bf16[144,768]{1,0:T(8,128)(2,1)S(1)}, bf16[144,768]{1,0:T(8,128)(2,1)S(1)}, u32[]{:S(2)}, u32[]{:S(2)}) collective-permute-start(bf16[144,768]{1,0:T(8,128)(2,1)S(1)} %shard_map.124), channel_id=1, source_target_pairs={{0,192},{64,0},{128,64},{192,128},{1,193},{65,1},{129,65},{193,129... | collective-permute-start | bytes 663560 | tf_op jit(solution)/shard_map/ppermute | solution.py:302
  92.8 8.6 %collective-permute-start.21 = (bf16[144,768]{1,0:T(8,128)(2,1)S(1)}, bf16[144,768]{1,0:T(8,128)(2,1)S(1)}, u32[]{:S(2)}, u32[]{:S(2)}) collective-permute-start(bf16[144,768]{1,0:T(8,128)(2,1)S(1)} %shard_map.123), channel_id=1, source_target_pairs={{0,64},{64,128},{128,192},{192,0},{1,65},{65,129},{129,193},{193,1... | collective-permute-start | bytes 663560 | tf_op jit(solution)/shard_map/ppermute | solution.py:302
  93.9 10.2 %collective-permute-start.20 = (bf16[144,768]{1,0:T(8,128)(2,1)S(1)}, bf16[144,768]{1,0:T(8,128)(2,1)S(1)}, u32[]{:S(2)}, u32[]{:S(2)}) collective-permute-start(bf16[144,768]{1,0:T(8,128)(2,1)S(1)} %shard_map.122), channel_id=1, source_target_pairs={{0,128},{64,192},{128,0},{192,64},{1,129},{65,193},{129,1},{193,65... | collective-permute-start | bytes 663560 | tf_op jit(solution)/shard_map/ppermute | solution.py:302

commit v2 on v1

--- a/solution.py
+++ b/solution.py
@@ -45,6 +45,13 @@
         ),
         compiler_params=pltpu.CompilerParams(vmem_limit_bytes=vmem),
     )
+
+
+def placed(body):
+    def run(*refs):
+        body(tuple(lax.axis_index(a) for a in ("x", "z", "c", "tp")), *refs)
+
+    return run
 
 
 def entry_body(
@@ -69,14 +76,14 @@
             out[6 + h, VBLK:TOKENS, :] = qa[:, cols]
 
 
-def chip_body(own, near, q_chip, kv_chip, audio):
-    for r, src in ((0, own), (1, near)):
-        kv_chip[r] = src[0:6]
-        for i in range(6):
-            audio[i, 16 * r : 16 * (r + 1), :] = src[i, VBLK:TOKENS, :]
-        for h in range(3):
-            q_chip[h, 128 * r : 128 * (r + 1), :] = src[6 + h, 0:VBLK, :]
-            q_chip[h, 256 + 16 * r : 272 + 16 * r, :] = src[6 + h, VBLK:TOKENS, :]
+def chip_body(r, src, *refs):
+    q_chip, kv_chip, audio = refs[-3:]
+    kv_chip[r] = src[0:6]
+    for i in range(6):
+        audio[i, 16 * r : 16 * (r + 1), :] = src[i, VBLK:TOKENS, :]
+    for h in range(3):
+        q_chip[h, 128 * r : 128 * (r + 1), :] = src[6 + h, 0:VBLK, :]
+        q_chip[h, 256 + 16 * r : 272 + 16 * r, :] = src[6 + h, VBLK:TOKENS, :]
 
 
 def device_band(x, z, c):
@@ -303,21 +310,20 @@
 
 
 def program(qv, kv, vv, qa, ka, va, video_spans, audio_spans, wv, wa):
-    pos = jnp.stack([lax.axis_index(a) for a in ("x", "z", "c", "tp")]).astype(jnp.int32)
     spans = jnp.concatenate([audio_spans.reshape(-1), video_spans.reshape(-1)])
     block = pltpu.VMEM((VBLK, 768), BF)
     small = pltpu.VMEM((ABLK, 768), BF)
     own, far = kernel_call(
-        entry_body, (((9, TOKENS, HEAD), BF),) * 2, [SSPEC] + [HSPEC] * 6, 2,
+        placed(entry_body), (((9, TOKENS, HEAD), BF),) * 2, [HSPEC] * 6, 2,
         scratch=[block, block, block, small, small, small, pltpu.SemaphoreType.DMA((6,))],
         vmem=66000000,
-    )(pos, qv, kv, vv, qa, ka, va)
+    )(qv, kv, vv, qa, ka, va)
     near = moved(far, "c", 1)
+    chip_shapes = (((3, ROWS, HEAD), BF), ((2, 6, TOKENS, HEAD), BF), ((6, 32, HEAD), BF))
+    halves = kernel_call(functools.partial(chip_body, 0), chip_shapes, [VSPEC], 0.5)(own)
     q_chip, kv_chip, audio = kernel_call(
-        chip_body,
-        (((3, ROWS, HEAD), BF), ((2, 6, TOKENS, HEAD), BF), ((6, 32, HEAD), BF)),
-        [VSPEC] * 2, 0.5,
-    )(own, near)
+        functools.partial(chip_body, 1), chip_shapes, [VSPEC] * 4, 0.5, {1: 0, 2: 1, 3: 2}
+    )(near, *halves)
     audio_far = moved(audio, "z", 4)
 
     ups, downs = [kv_chip], [kv_chip]
@@ -335,44 +341,41 @@
     groups = [
         ((kv_chip, ups[1], downs[1]), both(0, 0) + both(-1, 1) + both(1, 2)),
         ((ups[2], downs[2]), both(-2, 0) + both(2, 1)),
-        ((ups[3], downs[3]), both(-3, 0) + both(3, 1)),
     ]
     state_shape = (((3, ROWS, HEAD), F32),) * 12
     state = ()
     for i, (arrays, blocks) in enumerate(groups):
         n = len(arrays)
-        body = functools.partial(ring_body, blocks, (0, 1, 2, 3), i == 0, False)
-        aliases = {} if i == 0 else {6 + n + j: j for j in range(12)}
+        body = placed(functools.partial(ring_body, blocks, (0, 1, 2, 3), i == 0, False))
+        aliases = {} if i == 0 else {5 + n + j: j for j in range(12)}
         state = kernel_call(
-            body, state_shape, [SSPEC] * 2 + [VSPEC] * (4 + n + len(state)), len(blocks), aliases
-        )(pos, spans, *q_x, *arrays, *state)
+            body, state_shape, [SSPEC] + [VSPEC] * (4 + n + len(state)), len(blocks), aliases
+        )(spans, *q_x, *arrays, *state)
 
     aparts = kernel_call(
-        audio_body, (((PAYLOAD, HEAD), BF),) * 4, [SSPEC] * 2 + [VSPEC] * 12, 4,
+        placed(audio_body), (((PAYLOAD, HEAD), BF),) * 4, [SSPEC] + [VSPEC] * 12, 4,
         scratch=[pltpu.VMEM((NX, ROWS, HEAD), F32)],
-    )(pos, spans, *q_x, kv_chip, ups[1], downs[1], ups[2], downs[2], ups[3], downs[3], audio_far)
+    )(spans, *q_x, kv_chip, ups[1], downs[1], ups[2], downs[2], ups[3], downs[3], audio_far)
     aback = [aparts[0]] + [moved(aparts[k], "x", -k) for k in range(1, NX)]
 
-    final = [(-4, 0, 0, 0), (4, 1, 1, 0)]
+    final = both(-3, 0) + both(3, 1) + [(-4, 0, 2, 0), (4, 1, 3, 0)]
     packed = kernel_call(
-        functools.partial(ring_body, final, (0, 1, 2, 3), False, True),
-        (((PAYLOAD, HEAD), BF),) * 4, [SSPEC] * 2 + [VSPEC] * 18, 4,
+        placed(functools.partial(ring_body, final, (0, 1, 2, 3), False, True)),
+        (((PAYLOAD, HEAD), BF),) * 4, [SSPEC] + [VSPEC] * 20, 6,
         scratch=[pltpu.VMEM((NX, ROWS, HEAD), F32)],
-    )(pos, spans, *q_x, ups[4], downs[4], *state)
+    )(spans, *q_x, ups[3], downs[3], ups[4], downs[4], *state)
     back = [packed[0]] + [None] * 3
     for k in (2, 1, 3):
         back[k] = moved(packed[k], "x", -k)
 
     (extra,) = kernel_call(merge_audio_body, (((3, ROWS, HEAD), F32),), [VSPEC] * 4, 1)(*aback)
-    att_own, att_far = kernel_call(
-        merge_body, (((3, TOKENS, HEAD), BF),) * 2, [VSPEC] * 5, 1
-    )(*back, extra)
+    att_own, att_far = kernel_call(merge_body, (((3, TOKENS, HEAD), BF),) * 2, [VSPEC] * 5, 1)(*back, extra)
     att_near = moved(att_far, "c", 1)
     parts = []
     for k in (2, 1, 3, 0):
         (part,) = kernel_call(
-            functools.partial(project_body, k), (((TOKENS, 768), BF),), [SSPEC] + [VSPEC] * 4, 1,
-        )(pos, att_own, att_near, wv, wa)
+            placed(functools.partial(project_body, k)), (((TOKENS, 768), BF),), [VSPEC] * 4, 1,
+        )(att_own, att_near, wv, wa)
         parts.append(moved(part, "tp", k) if k else part)
     return kernel_call(sum_body, (((VBLK, 768), BF), ((ABLK, 768), BF)), [VSPEC] * 4, 0.5)(*parts)
 
@@ -381,6 +384,4 @@
     finer = Mesh(mesh.devices.reshape(mesh.shape["tp"], NX, NZ, 2), ("tp", "x", "z", "c"))
     row = P(SEQ, "tp")
     in_specs = (row,) * 6 + (P(), P()) + (P("tp", None),) * 2
-    return jax.shard_map(
-        program, mesh=finer, in_specs=in_specs, out_specs=(row, row), check_vma=False
-    )
+    return jax.shard_map(program, mesh=finer, in_specs=in_specs, out_specs=(row, row), check_vma=False)

time: 105 us -> 99.7 us (0.950)
  waiting for transfers between devices: 34.6 us -> 29.8 us
  starting transfers between devices: 38 us -> 42.2 us
  Pallas kernels: 29.3 us -> 25.2 us
    ppermute x23, waiting for transfers between devices: 34.6 us -> 29.8 us  [moved(): return lax.ppermute(array, axis, [(i, (i + by) % n) for i in range(n)])]
    ppermute x23, starting transfers between devices: 38 us -> 42.2 us  [moved(): return lax.ppermute(array, axis, [(i, (i + by) % n) for i in range(n)])]
    pallas_call x11, Pallas kernels: 27.1 us -> 22.9 us  [the longest x2 9.35 us: program(): kernel_call(body, state_shape, [SSPEC] + [VSPEC] * (4 + n + len(state)),...]
  transfers between devices with their start and end apart: 23 -> 23, of which waited for: 10 -> 10; matrix products, arithmetic and copies ran while one was open for 1% -> 1% of each run, Pallas kernels for 20% -> 21%
where the time goes in v2:
time: 99.7 us; the launch traced here: 99.5 us
  starting transfers between devices  42.2 us (42%)
  waiting for transfers between devices  29.8 us (30%)
  Pallas kernels  25.2 us (25%)
  local copies, waits for them, and re-layouts  1.54 us (2%)
    ppermute x23, starting transfers between devices, moved(): return lax.ppermute(array, axis, [(i, (i + by) % n) for i in range(n)])  42.2 us
    ppermute x23, waiting for transfers between devices, moved(): return lax.ppermute(array, axis, [(i, (i + by) % n) for i in range(n)])  29.8 us
    pallas_call x2, Pallas kernels, program(): kernel_call(body, state_shape, [SSPEC] + [VSPEC] * (4 + n + len(state)),...  9.35 us
    pallas_call x1, Pallas kernels, program(): kernel_call(placed(functools.partial(ring_body, final, (0, 1, 2, 3), Fals...  6.52 us
    pallas_call x1, Pallas kernels, program(): kernel_call(placed(audio_body), (((PAYLOAD, HEAD), BF),) * 4, [SSPEC] + [...  2.83 us
    pallas_call x1, Pallas kernels, program(): kernel_call(placed(entry_body), (((9, TOKENS, HEAD), BF),) * 2, [HSPEC] *...  2.19 us
  transfers between devices with their start and end apart: 23, of which 10 were waited for; matrix products, arithmetic and copies ran while one was open for 1% of the time, Pallas kernels for 21%

profile of v2, /device:TPU:1, one launch (start us, length us, event | category | flops | bytes accessed | tf_op | source)
XLA Modules:
  0.0 99.5 jit_solution(9554024794375082751)
XLA Ops:
  0.7 2.2 %shard_map.113 = (bf16[9,144,128]{2,1,0:T(8,128)(2,1)}, bf16[9,144,128]{2,1,0:T(8,128)(2,1)}) custom-call(bf16[128,768]{1,0:T(8,128)(2,1)} %refs_0_.1, bf16[128,768]{1,0:T(8,128)(2,1)} %refs_1_.1, bf16[128,768]{1,0:T(8,128)(2,1)} %refs_2_.5, bf16[16,768]{1,0:T(8,128)(2,1)} %refs_3_.5, bf16[16,768]{1,0:T(8,128)(2,1)} %refs_4_.1, bf16[16,768]{1,0:T(8,128)(2,1)} %refs_5_.1), custom_call_target="tpu_custom_call" | custom-call | flops 2000000000 | bytes 65536 | tf_op jit(solution)/shard_map/pallas_call | solution.py:316
  2.9 3.3 %collective-permute-start = (bf16[9,144,128]{2,1,0:T(8,128)(2,1)}, bf16[9,144,128]{2,1,0:T(8,128)(2,1)S(1)}, u32[]{:S(2)}, u32[]{:S(2)}) collective-permute-start(bf16[9,144,128]{2,1,0:T(8,128)(2,1)} %get-tuple-element.44), channel_id=1, source_target_pairs={{0,1},{1,0},{2,3},{3,2},{4,5},{5,4},{6,7},{7,6},{8,9},{9,8},{10,11... | collective-permute-start | bytes 995336 | tf_op jit(solution)/shard_map/ppermute | solution.py:309
  6.1 1.0 copy-done
  7.1 0.5 collective-permute-done.src
  7.6 0.1 collective-permute-start.4
  7.7 3.9 %collective-permute-start.7 = (bf16[2,6,144,128]{3,2,1,0:T(8,128)(2,1)S(1)}, bf16[2,6,144,128]{3,2,1,0:T(8,128)(2,1)S(1)}, u32[]{:S(2)}, u32[]{:S(2)}) collective-permute-start(bf16[2,6,144,128]{3,2,1,0:T(8,128)(2,1)S(1)} %get-tuple-element.50.refs_5_), channel_id=1, source_target_pairs={{0,14},{2,0},{4,2},{6,4},{8,6},{10,8},{12,10},{14,12},{1,15},{3,1}... | collective-permute-start | bytes 1327112 | tf_op jit(solution)/shard_map/ppermute | solution.py:309
  11.7 10.1 %collective-permute-done.4.refs_6_ = bf16[2,6,144,128]{3,2,1,0:T(8,128)(2,1)S(1)} collective-permute-done((bf16[2,6,144,128]{3,2,1,0:T(8,128)(2,1)S(1)}, bf16[2,6,144,128]{3,2,1,0:T(8,128)(2,1)S(1)}, u32[]{:S(2)}, u32[]{:S(2)}) %collective-permute-start.4) | collective-permute-done | bytes 442400 | tf_op jit(solution)/shard_map/ppermute | solution.py:309
  21.8 0.0 collective-permute-start.5
  21.8 0.0 collective-permute-done.7.refs_7_
  21.8 2.7 %collective-permute-start.8 = (bf16[2,6,144,128]{3,2,1,0:T(8,128)(2,1)S(1)}, bf16[2,6,144,128]{3,2,1,0:T(8,128)(2,1)S(1)}, u32[]{:S(2)}, u32[]{:S(2)}) collective-permute-start(bf16[2,6,144,128]{3,2,1,0:T(8,128)(2,1)S(1)} %collective-permute-done.7.refs_7_), channel_id=1, source_target_pairs={{0,14},{2,0},{4,2},{6,4},{8,6},{10,8},{12,10},{14,12},{1,15},{3,1}... | collective-permute-start | bytes 1327112 | tf_op jit(solution)/shard_map/ppermute | solution.py:309
  24.4 0.1 copy.29
  24.5 0.1 reshape.10
  24.7 0.1 copy.30
  24.8 0.1 reshape.11
  24.9 1.3 %collective-permute-start.1 = (bf16[3,288,128]{2,1,0:T(8,128)(2,1)S(1)}, bf16[3,288,128]{2,1,0:T(8,128)(2,1)S(1)}, u32[]{:S(2)}, u32[]{:S(2)}) collective-permute-start(bf16[3,288,128]{2,1,0:T(8,128)(2,1)S(1)} %get-tuple-element.49.refs_1_), channel_id=1, source_target_pairs={{0,16},{16,32},{32,48},{48,0},{1,17},{17,33},{33,49},{49,1},{2,18}... | collective-permute-start | bytes 663560 | tf_op jit(solution)/shard_map/ppermute | solution.py:309
  26.2 2.5 %collective-permute-start.2 = (bf16[3,288,128]{2,1,0:T(8,128)(2,1)S(1)}, bf16[3,288,128]{2,1,0:T(8,128)(2,1)S(1)}, u32[]{:S(2)}, u32[]{:S(2)}) collective-permute-start(bf16[3,288,128]{2,1,0:T(8,128)(2,1)S(1)} %get-tuple-element.49.refs_1_), channel_id=1, source_target_pairs={{0,32},{16,48},{32,0},{48,16},{1,33},{17,49},{33,1},{49,17},{2,34}... | collective-permute-start | bytes 663560 | tf_op jit(solution)/shard_map/ppermute | solution.py:309
  28.7 1.2 %collective-permute-start.3 = (bf16[3,288,128]{2,1,0:T(8,128)(2,1)S(1)}, bf16[3,288,128]{2,1,0:T(8,128)(2,1)S(1)}, u32[]{:S(2)}, u32[]{:S(2)}) collective-permute-start(bf16[3,288,128]{2,1,0:T(8,128)(2,1)S(1)} %get-tuple-element.49.refs_1_), channel_id=1, source_target_pairs={{0,48},{16,0},{32,16},{48,32},{1,49},{17,1},{33,17},{49,33},{2,50}... | collective-permute-start | bytes 663560 | tf_op jit(solution)/shard_map/ppermute | solution.py:309
  29.9 1.8 %collective-permute-done.1.refs_2_ = bf16[3,288,128]{2,1,0:T(8,128)(2,1)S(1)} collective-permute-done((bf16[3,288,128]{2,1,0:T(8,128)(2,1)S(1)}, bf16[3,288,128]{2,1,0:T(8,128)(2,1)S(1)}, u32[]{:S(2)}, u32[]{:S(2)}) %collective-permute-start.1) | collective-permute-done | bytes 221216 | tf_op jit(solution)/shard_map/ppermute | solution.py:309
  31.7 3.4 %collective-permute-start.15 = (bf16[6,32,128]{2,1,0:T(8,128)(2,1)S(1)}, bf16[6,32,128]{2,1,0:T(8,128)(2,1)S(1)}, u32[]{:S(2)}, u32[]{:S(2)}) collective-permute-start(bf16[6,32,128]{2,1,0:T(8,128)(2,1)S(1)} %get-tuple-element.79), channel_id=1, source_target_pairs={{0,8},{2,10},{4,12},{6,14},{8,0},{10,2},{12,4},{14,6},{1,9},{3,11}... | collective-permute-start | bytes 147464 | tf_op jit(solution)/shard_map/ppermute | solution.py:309
  35.1 0.0 collective-permute-done.5.refs_5_.refs_8_
  35.1 0.0 collective-permute-start.6
  35.1 0.0 collective-permute-done.8.refs_6_.refs_9_
  35.2 2.7 %collective-permute-start.9 = (bf16[2,6,144,128]{3,2,1,0:T(8,128)(2,1)S(1)}, bf16[2,6,144,128]{3,2,1,0:T(8,128)(2,1)S(1)}, u32[]{:S(2)}, u32[]{:S(2)}) collective-permute-start(bf16[2,6,144,128]{3,2,1,0:T(8,128)(2,1)S(1)} %collective-permute-done.8.refs_6_.refs_9_), channel_id=1, source_target_pairs={{0,14},{2,0},{4,2},{6,4},{8,6},{10,8},{12,10},{14,12},{1,15},{3,1}... | collective-permute-start | bytes 1327112 | tf_op jit(solution)/shard_map/ppermute | solution.py:309
  37.8 0.0 collective-permute-done.2.refs_3_
  37.8 0.0 collective-permute-done.3.refs_4_
  37.8 5.1 %shard_map.116 = (f32[3,288,128]{2,1,0:T(8,128)S(1)}, f32[3,288,128]{2,1,0:T(8,128)S(1)}, f32[3,288,128]{2,1,0:T(8,128)S(1)}, f32[3,288,128]{2,1,0:T(8,128)S(1)}...) custom-call(s32[256]{0:T(256)S(1)} %constant_dynamic-update-slice_fu, ...), custom_call_target="tpu_custom_call" | custom-call | flops 6000000000 | bytes 65536 | tf_op jit(solution)/shard_map/pallas_call | solution.py:351
  42.9 4.3 %shard_map.117 = (f32[3,288,128]{2,1,0:T(8,128)S(1)}, f32[3,288,128]{2,1,0:T(8,128)S(1)}, f32[3,288,128]{2,1,0:T(8,128)S(1)}, f32[3,288,128]{2,1,0:T(8,128)S(1)}...) custom-call(s32[256]{0:T(256)S(1)} %constant_dynamic-update-slice_fu, ...), custom_call_target="tpu_custom_call", output_to_operand_aliasing={{0}: (7, {}), {1}: (8, {}), {2}: (9, {}), {3}: (10, {}), {4... | custom-call | flops 4000000000 | bytes 65536 | tf_op jit(solution)/shard_map/pallas_call | solution.py:351
  47.2 0.0 collective-permute-done.6.refs_5_.refs_10_
  47.2 0.1 collective-permute-start.10
  47.3 0.0 collective-permute-done.9.refs_6_.refs_11_
  47.4 2.9 %collective-permute-start.11 = (bf16[1,6,144,128]{3,2,1,0:T(8,128)(2,1)S(1)}, bf16[1,6,144,128]{3,2,1,0:T(8,128)(2,1)S(1)}, u32[]{:S(2)}, u32[]{:S(2)}) collective-permute-start(bf16[1,6,144,128]{3,2,1,0:T(8,128)(2,1)S(1)} %slice.9), channel_id=1, source_target_pairs={{0,14},{2,0},{4,2},{6,4},{8,6},{10,8},{12,10},{14,12},{1,15},{3,1}... | collective-permute-start | bytes 663560 | tf_op jit(solution)/shard_map/ppermute | solution.py:309
  50.3 0.0 collective-permute-done.15.refs_12_
  50.3 2.8 %shard_map.119 = (bf16[912,128]{1,0:T(8,128)(2,1)S(1)}, bf16[912,128]{1,0:T(8,128)(2,1)S(1)}, bf16[912,128]{1,0:T(8,128)(2,1)S(1)}, bf16[912,128]{1,0:T(8,128)(2,1)S(1)}) custom-call(s32[256]{0:T(256)S(1)} %constant_dynamic-update-slice_fusion.refs_0_, bf16[3,288,128]{2,1,0:T(8,128)(2,1)S(1)} %get-tuple-element.49.refs_1_, ...), custom_call_target="tpu_custom_call" | custom-call | flops 4000000000 | bytes 65536 | tf_op jit(solution)/shard_map/pallas_call | solution.py:355
  53.1 2.7 %collective-permute-start.16 = (bf16[912,128]{1,0:T(8,128)(2,1)S(1)}, bf16[912,128]{1,0:T(8,128)(2,1)S(1)}, u32[]{:S(2)}, u32[]{:S(2)}) collective-permute-start(bf16[912,128]{1,0:T(8,128)(2,1)S(1)} %get-tuple-element.81), channel_id=1, source_target_pairs={{0,48},{16,0},{32,16},{48,32},{1,49},{17,1},{33,17},{49,33},{2,50}... | collective-permute-start | bytes 700424 | tf_op jit(solution)/shard_map/ppermute | solution.py:309
  55.8 1.0 %collective-permute-start.17 = (bf16[912,128]{1,0:T(8,128)(2,1)S(1)}, bf16[912,128]{1,0:T(8,128)(2,1)S(1)}, u32[]{:S(2)}, u32[]{:S(2)}) collective-permute-start(bf16[912,128]{1,0:T(8,128)(2,1)S(1)} %get-tuple-element.82), channel_id=1, source_target_pairs={{0,32},{16,48},{32,0},{48,16},{1,33},{17,49},{33,1},{49,17},{2,34}... | collective-permute-start | bytes 700424 | tf_op jit(solution)/shard_map/ppermute | solution.py:309
  56.8 0.0 collective-permute-start.18
  56.8 0.0 collective-permute-done.10.refs_7_
  56.8 0.0 collective-permute-done.11.refs_8_
  56.8 0.0 slice-start
  56.8 0.0 slice-start.2
  56.8 0.0 slice-start.1
  56.9 0.0 slice-start.3
  56.9 6.5 %shard_map.118 = (bf16[912,128]{1,0:T(8,128)(2,1)S(1)}, bf16[912,128]{1,0:T(8,128)(2,1)S(1)}, bf16[912,128]{1,0:T(8,128)(2,1)S(1)}, bf16[912,128]{1,0:T(8,128)(2,1)S(1)}) custom-call(s32[256]{0:T(256)S(1)} %constant_dynamic-update-slice_fusion.refs_0_, bf16[3,288,128]{2,1,0:T(8,128)(2,1)S(1)} %get-tuple-element.49.refs_1_, ...), custom_call_target="tpu_custom_call" | custom-call | flops 6000000000 | bytes 65536 | tf_op jit(solution)/shard_map/pallas_call | solution.py:362
  63.4 2.7 %collective-permute-start.12 = (bf16[912,128]{1,0:T(8,128)(2,1)S(1)}, bf16[912,128]{1,0:T(8,128)(2,1)S(1)}, u32[]{:S(2)}, u32[]{:S(2)}) collective-permute-start(bf16[912,128]{1,0:T(8,128)(2,1)S(1)} %get-tuple-element.76), channel_id=1, source_target_pairs={{0,48},{16,0},{32,16},{48,32},{1,49},{17,1},{33,17},{49,33},{2,50}... | collective-permute-start | bytes 700424 | tf_op jit(solution)/shard_map/ppermute | solution.py:309
  66.1 0.7 collective-permute-start.13
  66.9 0.0 collective-permute-done.18.p3
  66.9 0.7 shard_map.120.extra
  67.6 4.1 %collective-permute-done.12.p1 = bf16[912,128]{1,0:T(8,128)(2,1)S(1)} collective-permute-done((bf16[912,128]{1,0:T(8,128)(2,1)S(1)}, bf16[912,128]{1,0:T(8,128)(2,1)S(1)}, u32[]{:S(2)}, u32[]{:S(2)}) %collective-permute-start.12) | collective-permute-done | bytes 233504 | tf_op jit(solution)/shard_map/ppermute | solution.py:309
  71.7 1.3 %collective-permute-done.13.p2 = bf16[912,128]{1,0:T(8,128)(2,1)S(1)} collective-permute-done((bf16[912,128]{1,0:T(8,128)(2,1)S(1)}, bf16[912,128]{1,0:T(8,128)(2,1)S(1)}, u32[]{:S(2)}, u32[]{:S(2)}) %collective-permute-start.13) | collective-permute-done | bytes 233504 | tf_op jit(solution)/shard_map/ppermute | solution.py:309
  73.1 2.4 %collective-permute-done.14.p3 = bf16[912,128]{1,0:T(8,128)(2,1)S(1)} collective-permute-done((bf16[912,128]{1,0:T(8,128)(2,1)S(1)}, bf16[912,128]{1,0:T(8,128)(2,1)S(1)}, u32[]{:S(2)}, u32[]{:S(2)}) %collective-permute-start.14) | collective-permute-done | bytes 233504 | tf_op jit(solution)/shard_map/ppermute | solution.py:309
  75.4 0.7 shard_map.121
  76.1 6.5 %collective-permute-start.19 = (bf16[3,144,128]{2,1,0:T(8,128)(2,1)S(1)}, bf16[3,144,128]{2,1,0:T(8,128)(2,1)S(1)}, u32[]{:S(2)}, u32[]{:S(2)}) collective-permute-start(bf16[3,144,128]{2,1,0:T(8,128)(2,1)S(1)} %get-tuple-element.85), channel_id=1, source_target_pairs={{0,1},{1,0},{2,3},{3,2},{4,5},{5,4},{6,7},{7,6},{8,9},{9,8},{10,11... | collective-permute-start | bytes 331784 | tf_op jit(solution)/shard_map/ppermute | solution.py:309
  82.6 1.0 collective-permute-done.19.refs_1_
  83.6 0.5 shard_map.124
  84.1 2.8 %collective-permute-start.22 = (bf16[144,768]{1,0:T(8,128)(2,1)S(1)}, bf16[144,768]{1,0:T(8,128)(2,1)S(1)}, u32[]{:S(2)}, u32[]{:S(2)}) collective-permute-start(bf16[144,768]{1,0:T(8,128)(2,1)S(1)} %shard_map.124), channel_id=1, source_target_pairs={{0,192},{64,0},{128,64},{192,128},{1,193},{65,1},{129,65},{193,129... | collective-permute-start | bytes 663560 | tf_op jit(solution)/shard_map/ppermute | solution.py:309
  86.9 0.5 shard_map.123
  87.4 0.1 collective-permute-start.21
  87.5 0.5 shard_map.122
  88.0 1.7 %collective-permute-start.20 = (bf16[144,768]{1,0:T(8,128)(2,1)S(1)}, bf16[144,768]{1,0:T(8,128)(2,1)S(1)}, u32[]{:S(2)}, u32[]{:S(2)}) collective-permute-start(bf16[144,768]{1,0:T(8,128)(2,1)S(1)} %shard_map.122), channel_id=1, source_target_pairs={{0,128},{64,192},{128,0},{192,64},{1,129},{65,193},{129,1},{193,65... | collective-permute-start | bytes 663560 | tf_op jit(solution)/shard_map/ppermute | solution.py:309
  89.7 0.5 shard_map.125.p3
  90.2 1.2 %collective-permute-done.22.p2 = bf16[144,768]{1,0:T(8,128)(2,1)S(1)} collective-permute-done((bf16[144,768]{1,0:T(8,128)(2,1)S(1)}, bf16[144,768]{1,0:T(8,128)(2,1)S(1)}, u32[]{:S(2)}, u32[]{:S(2)}) %collective-permute-start.22) | collective-permute-done | bytes 221216 | tf_op jit(solution)/shard_map/ppermute | solution.py:309
  91.3 4.7 %collective-permute-done.21.p1 = bf16[144,768]{1,0:T(8,128)(2,1)S(1)} collective-permute-done((bf16[144,768]{1,0:T(8,128)(2,1)S(1)}, bf16[144,768]{1,0:T(8,128)(2,1)S(1)}, u32[]{:S(2)}, u32[]{:S(2)}) %collective-permute-start.21) | collective-permute-done | bytes 221216 | tf_op jit(solution)/shard_map/ppermute | solution.py:309
  96.0 2.7 %collective-permute-done.20.p0 = bf16[144,768]{1,0:T(8,128)(2,1)S(1)} collective-permute-done((bf16[144,768]{1,0:T(8,128)(2,1)S(1)}, bf16[144,768]{1,0:T(8,128)(2,1)S(1)}, u32[]{:S(2)}, u32[]{:S(2)}) %collective-permute-start.20) | collective-permute-done | bytes 221216 | tf_op jit(solution)/shard_map/ppermute | solution.py:309
  98.8 0.8 shard_map.126
  (21 shorter events, 0.1 us)
Async XLA Ops:
  0.6 23.8 %copy-start.1 = (s32[64,2]{0,1:T(2,128)S(1)}, s32[64,2]{0,1:T(2,128)}, u32[]{:S(2)}) copy-start(s32[64,2]{0,1:T(2,128)} %param.17) | copy-start | bytes 1540
  0.6 24.0 %copy-start.2 = (s32[64,2]{0,1:T(2,128)S(1)}, s32[64,2]{0,1:T(2,128)}, u32[]{:S(2)}) copy-start(s32[64,2]{0,1:T(2,128)} %param.16) | copy-start | bytes 1540
  2.9 4.8 %collective-permute-start = (bf16[9,144,128]{2,1,0:T(8,128)(2,1)}, bf16[9,144,128]{2,1,0:T(8,128)(2,1)S(1)}, u32[]{:S(2)}, u32[]{:S(2)}) collective-permute-start(bf16[9,144,128]{2,1,0:T(8,128)(2,1)} %get-tuple-element.44), channel_id=1, source_target_pairs={{0,1},{1,0},{2,3},{3,2},{4,5},{5,4},{6,7},{7,6},{8,9},{9,8},{10,11... | collective-permute-start | bytes 995336 | tf_op jit(solution)/shard_map/ppermute | solution.py:309
  6.1 1.0 copy-start
  7.6 14.1 %collective-permute-start.4 = (bf16[2,6,144,128]{3,2,1,0:T(8,128)(2,1)S(1)}, bf16[2,6,144,128]{3,2,1,0:T(8,128)(2,1)S(1)}, u32[]{:S(2)}, u32[]{:S(2)}) collective-permute-start(bf16[2,6,144,128]{3,2,1,0:T(8,128)(2,1)S(1)} %get-tuple-element.50.refs_5_), channel_id=1, source_target_pairs={{0,2},{2,4},{4,6},{6,8},{8,10},{10,12},{12,14},{14,0},{1,3},{3,5},... | collective-permute-start | bytes 1327112 | tf_op jit(solution)/shard_map/ppermute | solution.py:309
  7.7 14.0 %collective-permute-start.7 = (bf16[2,6,144,128]{3,2,1,0:T(8,128)(2,1)S(1)}, bf16[2,6,144,128]{3,2,1,0:T(8,128)(2,1)S(1)}, u32[]{:S(2)}, u32[]{:S(2)}) collective-permute-start(bf16[2,6,144,128]{3,2,1,0:T(8,128)(2,1)S(1)} %get-tuple-element.50.refs_5_), channel_id=1, source_target_pairs={{0,14},{2,0},{4,2},{6,4},{8,6},{10,8},{12,10},{14,12},{1,15},{3,1}... | collective-permute-start | bytes 1327112 | tf_op jit(solution)/shard_map/ppermute | solution.py:309
  21.8 13.4 %collective-permute-start.5 = (bf16[2,6,144,128]{3,2,1,0:T(8,128)(2,1)S(1)}, bf16[2,6,144,128]{3,2,1,0:T(8,128)(2,1)S(1)}, u32[]{:S(2)}, u32[]{:S(2)}) collective-permute-start(bf16[2,6,144,128]{3,2,1,0:T(8,128)(2,1)S(1)} %collective-permute-done.4.refs_6_), channel_id=1, source_target_pairs={{0,2},{2,4},{4,6},{6,8},{8,10},{10,12},{12,14},{14,0},{1,3},{3,5},... | collective-permute-start | bytes 1327112 | tf_op jit(solution)/shard_map/ppermute | solution.py:309
  21.8 13.4 %collective-permute-start.8 = (bf16[2,6,144,128]{3,2,1,0:T(8,128)(2,1)S(1)}, bf16[2,6,144,128]{3,2,1,0:T(8,128)(2,1)S(1)}, u32[]{:S(2)}, u32[]{:S(2)}) collective-permute-start(bf16[2,6,144,128]{3,2,1,0:T(8,128)(2,1)S(1)} %collective-permute-done.7.refs_7_), channel_id=1, source_target_pairs={{0,14},{2,0},{4,2},{6,4},{8,6},{10,8},{12,10},{14,12},{1,15},{3,1}... | collective-permute-start | bytes 1327112 | tf_op jit(solution)/shard_map/ppermute | solution.py:309
  24.9 6.8 %collective-permute-start.1 = (bf16[3,288,128]{2,1,0:T(8,128)(2,1)S(1)}, bf16[3,288,128]{2,1,0:T(8,128)(2,1)S(1)}, u32[]{:S(2)}, u32[]{:S(2)}) collective-permute-start(bf16[3,288,128]{2,1,0:T(8,128)(2,1)S(1)} %get-tuple-element.49.refs_1_), channel_id=1, source_target_pairs={{0,16},{16,32},{32,48},{48,0},{1,17},{17,33},{33,49},{49,1},{2,18}... | collective-permute-start | bytes 663560 | tf_op jit(solution)/shard_map/ppermute | solution.py:309
  26.2 11.6 %collective-permute-start.2 = (bf16[3,288,128]{2,1,0:T(8,128)(2,1)S(1)}, bf16[3,288,128]{2,1,0:T(8,128)(2,1)S(1)}, u32[]{:S(2)}, u32[]{:S(2)}) collective-permute-start(bf16[3,288,128]{2,1,0:T(8,128)(2,1)S(1)} %get-tuple-element.49.refs_1_), channel_id=1, source_target_pairs={{0,32},{16,48},{32,0},{48,16},{1,33},{17,49},{33,1},{49,17},{2,34}... | collective-permute-start | bytes 663560 | tf_op jit(solution)/shard_map/ppermute | solution.py:309
  28.7 9.2 %collective-permute-start.3 = (bf16[3,288,128]{2,1,0:T(8,128)(2,1)S(1)}, bf16[3,288,128]{2,1,0:T(8,128)(2,1)S(1)}, u32[]{:S(2)}, u32[]{:S(2)}) collective-permute-start(bf16[3,288,128]{2,1,0:T(8,128)(2,1)S(1)} %get-tuple-element.49.refs_1_), channel_id=1, source_target_pairs={{0,48},{16,0},{32,16},{48,32},{1,49},{17,1},{33,17},{49,33},{2,50}... | collective-permute-start | bytes 663560 | tf_op jit(solution)/shard_map/ppermute | solution.py:309
  31.7 18.6 %collective-permute-start.15 = (bf16[6,32,128]{2,1,0:T(8,128)(2,1)S(1)}, bf16[6,32,128]{2,1,0:T(8,128)(2,1)S(1)}, u32[]{:S(2)}, u32[]{:S(2)}) collective-permute-start(bf16[6,32,128]{2,1,0:T(8,128)(2,1)S(1)} %get-tuple-element.79), channel_id=1, source_target_pairs={{0,8},{2,10},{4,12},{6,14},{8,0},{10,2},{12,4},{14,6},{1,9},{3,11}... | collective-permute-start | bytes 147464 | tf_op jit(solution)/shard_map/ppermute | solution.py:309
  35.1 12.1 %collective-permute-start.6 = (bf16[2,6,144,128]{3,2,1,0:T(8,128)(2,1)S(1)}, bf16[2,6,144,128]{3,2,1,0:T(8,128)(2,1)S(1)}, u32[]{:S(2)}, u32[]{:S(2)}) collective-permute-start(bf16[2,6,144,128]{3,2,1,0:T(8,128)(2,1)S(1)} %collective-permute-done.5.refs_5_.refs_8_), channel_id=1, source_target_pairs={{0,2},{2,4},{4,6},{6,8},{8,10},{10,12},{12,14},{14,0},{1,3},{3,5},... | collective-permute-start | bytes 1327112 | tf_op jit(solution)/shard_map/ppermute | solution.py:309
  35.2 12.2 %collective-permute-start.9 = (bf16[2,6,144,128]{3,2,1,0:T(8,128)(2,1)S(1)}, bf16[2,6,144,128]{3,2,1,0:T(8,128)(2,1)S(1)}, u32[]{:S(2)}, u32[]{:S(2)}) collective-permute-start(bf16[2,6,144,128]{3,2,1,0:T(8,128)(2,1)S(1)} %collective-permute-done.8.refs_6_.refs_9_), channel_id=1, source_target_pairs={{0,14},{2,0},{4,2},{6,4},{8,6},{10,8},{12,10},{14,12},{1,15},{3,1}... | collective-permute-start | bytes 1327112 | tf_op jit(solution)/shard_map/ppermute | solution.py:309
  47.2 9.6 %collective-permute-start.10 = (bf16[1,6,144,128]{3,2,1,0:T(8,128)(2,1)S(1)}, bf16[1,6,144,128]{3,2,1,0:T(8,128)(2,1)S(1)}, u32[]{:S(2)}, u32[]{:S(2)}) collective-permute-start(bf16[1,6,144,128]{3,2,1,0:T(8,128)(2,1)S(1)} %slice.8), channel_id=1, source_target_pairs={{0,2},{2,4},{4,6},{6,8},{8,10},{10,12},{12,14},{14,0},{1,3},{3,5},... | collective-permute-start | bytes 663560 | tf_op jit(solution)/shard_map/ppermute | solution.py:309
  47.4 9.5 %collective-permute-start.11 = (bf16[1,6,144,128]{3,2,1,0:T(8,128)(2,1)S(1)}, bf16[1,6,144,128]{3,2,1,0:T(8,128)(2,1)S(1)}, u32[]{:S(2)}, u32[]{:S(2)}) collective-permute-start(bf16[1,6,144,128]{3,2,1,0:T(8,128)(2,1)S(1)} %slice.9), channel_id=1, source_target_pairs={{0,14},{2,0},{4,2},{6,4},{8,6},{10,8},{12,10},{14,12},{1,15},{3,1}... | collective-permute-start | bytes 663560 | tf_op jit(solution)/shard_map/ppermute | solution.py:309
  53.1 13.8 %collective-permute-start.16 = (bf16[912,128]{1,0:T(8,128)(2,1)S(1)}, bf16[912,128]{1,0:T(8,128)(2,1)S(1)}, u32[]{:S(2)}, u32[]{:S(2)}) collective-permute-start(bf16[912,128]{1,0:T(8,128)(2,1)S(1)} %get-tuple-element.81), channel_id=1, source_target_pairs={{0,48},{16,0},{32,16},{48,32},{1,49},{17,1},{33,17},{49,33},{2,50}... | collective-permute-start | bytes 700424 | tf_op jit(solution)/shard_map/ppermute | solution.py:309
  55.8 11.1 %collective-permute-start.17 = (bf16[912,128]{1,0:T(8,128)(2,1)S(1)}, bf16[912,128]{1,0:T(8,128)(2,1)S(1)}, u32[]{:S(2)}, u32[]{:S(2)}) collective-permute-start(bf16[912,128]{1,0:T(8,128)(2,1)S(1)} %get-tuple-element.82), channel_id=1, source_target_pairs={{0,32},{16,48},{32,0},{48,16},{1,33},{17,49},{33,1},{49,17},{2,34}... | collective-permute-start | bytes 700424 | tf_op jit(solution)/shard_map/ppermute | solution.py:309
  56.8 10.1 %collective-permute-start.18 = (bf16[912,128]{1,0:T(8,128)(2,1)S(1)}, bf16[912,128]{1,0:T(8,128)(2,1)S(1)}, u32[]{:S(2)}, u32[]{:S(2)}) collective-permute-start(bf16[912,128]{1,0:T(8,128)(2,1)S(1)} %get-tuple-element.83), channel_id=1, source_target_pairs={{0,16},{16,32},{32,48},{48,0},{1,17},{17,33},{33,49},{49,1},{2,18}... | collective-permute-start | bytes 700424 | tf_op jit(solution)/shard_map/ppermute | solution.py:309
  56.8 26.7 %slice-start = ((s8[4718592]{0:T(1024)(128)(4,1)}), s8[4194304]{0:T(1024)(128)(4,1)S(1)}, s32[]{:S(2)}) async-start(s8[4718592]{0:T(1024)(128)(4,1)} %bitcast), calls=%async_computation | async-start | bytes 8388608
  56.8 26.7 %slice-start.2 = ((s8[4718592]{0:T(1024)(128)(4,1)}), s8[4194304]{0:T(1024)(128)(4,1)S(1)}, s32[]{:S(2)}) async-start(s8[4718592]{0:T(1024)(128)(4,1)} %bitcast.2), calls=%async_computation.2 | async-start | bytes 8388608
  56.8 26.7 %slice-start.1 = ((s8[4718592]{0:T(1024)(128)(4,1)}), s8[524288]{0:T(1024)(128)(4,1)S(1)}, s32[]{:S(2)}) async-start(s8[4718592]{0:T(1024)(128)(4,1)} %bitcast), calls=%async_computation.1 | async-start | bytes 1048576
  56.9 26.7 %slice-start.3 = ((s8[4718592]{0:T(1024)(128)(4,1)}), s8[524288]{0:T(1024)(128)(4,1)S(1)}, s32[]{:S(2)}) async-start(s8[4718592]{0:T(1024)(128)(4,1)} %bitcast.2), calls=%async_computation.3 | async-start | bytes 1048576
  63.4 8.3 %collective-permute-start.12 = (bf16[912,128]{1,0:T(8,128)(2,1)S(1)}, bf16[912,128]{1,0:T(8,128)(2,1)S(1)}, u32[]{:S(2)}, u32[]{:S(2)}) collective-permute-start(bf16[912,128]{1,0:T(8,128)(2,1)S(1)} %get-tuple-element.76), channel_id=1, source_target_pairs={{0,48},{16,0},{32,16},{48,32},{1,49},{17,1},{33,17},{49,33},{2,50}... | collective-permute-start | bytes 700424 | tf_op jit(solution)/shard_map/ppermute | solution.py:309
  66.1 6.9 %collective-permute-start.13 = (bf16[912,128]{1,0:T(8,128)(2,1)S(1)}, bf16[912,128]{1,0:T(8,128)(2,1)S(1)}, u32[]{:S(2)}, u32[]{:S(2)}) collective-permute-start(bf16[912,128]{1,0:T(8,128)(2,1)S(1)} %get-tuple-element.77), channel_id=1, source_target_pairs={{0,32},{16,48},{32,0},{48,16},{1,33},{17,49},{33,1},{49,17},{2,34}... | collective-permute-start | bytes 700424 | tf_op jit(solution)/shard_map/ppermute | solution.py:309
  66.9 8.5 %collective-permute-start.14 = (bf16[912,128]{1,0:T(8,128)(2,1)S(1)}, bf16[912,128]{1,0:T(8,128)(2,1)S(1)}, u32[]{:S(2)}, u32[]{:S(2)}) collective-permute-start(bf16[912,128]{1,0:T(8,128)(2,1)S(1)} %get-tuple-element.78), channel_id=1, source_target_pairs={{0,16},{16,32},{32,48},{48,0},{1,17},{17,33},{33,49},{49,1},{2,18}... | collective-permute-start | bytes 700424 | tf_op jit(solution)/shard_map/ppermute | solution.py:309
  76.1 7.4 %collective-permute-start.19 = (bf16[3,144,128]{2,1,0:T(8,128)(2,1)S(1)}, bf16[3,144,128]{2,1,0:T(8,128)(2,1)S(1)}, u32[]{:S(2)}, u32[]{:S(2)}) collective-permute-start(bf16[3,144,128]{2,1,0:T(8,128)(2,1)S(1)} %get-tuple-element.85), channel_id=1, source_target_pairs={{0,1},{1,0},{2,3},{3,2},{4,5},{5,4},{6,7},{7,6},{8,9},{9,8},{10,11... | collective-permute-start | bytes 331784 | tf_op jit(solution)/shard_map/ppermute | solution.py:309
  84.1 7.2 %collective-permute-start.22 = (bf16[144,768]{1,0:T(8,128)(2,1)S(1)}, bf16[144,768]{1,0:T(8,128)(2,1)S(1)}, u32[]{:S(2)}, u32[]{:S(2)}) collective-permute-start(bf16[144,768]{1,0:T(8,128)(2,1)S(1)} %shard_map.124), channel_id=1, source_target_pairs={{0,192},{64,0},{128,64},{192,128},{1,193},{65,1},{129,65},{193,129... | collective-permute-start | bytes 663560 | tf_op jit(solution)/shard_map/ppermute | solution.py:309
  87.4 8.7 %collective-permute-start.21 = (bf16[144,768]{1,0:T(8,128)(2,1)S(1)}, bf16[144,768]{1,0:T(8,128)(2,1)S(1)}, u32[]{:S(2)}, u32[]{:S(2)}) collective-permute-start(bf16[144,768]{1,0:T(8,128)(2,1)S(1)} %shard_map.123), channel_id=1, source_target_pairs={{0,64},{64,128},{128,192},{192,0},{1,65},{65,129},{129,193},{193,1... | collective-permute-start | bytes 663560 | tf_op jit(solution)/shard_map/ppermute | solution.py:309
  88.0 10.8 %collective-permute-start.20 = (bf16[144,768]{1,0:T(8,128)(2,1)S(1)}, bf16[144,768]{1,0:T(8,128)(2,1)S(1)}, u32[]{:S(2)}, u32[]{:S(2)}) collective-permute-start(bf16[144,768]{1,0:T(8,128)(2,1)S(1)} %shard_map.122), channel_id=1, source_target_pairs={{0,128},{64,192},{128,0},{192,64},{1,129},{65,193},{129,1},{193,65... | collective-permute-start | bytes 663560 | tf_op jit(solution)/shard_map/ppermute | solution.py:309

commit v3 on v2

--- a/solution.py
+++ b/solution.py
@@ -162,7 +162,8 @@
                     outs[3 * i + j][h] = found[j]
             return carry
 
-        lax.fori_loop(0, 3, step, 0)
+        for h in range(3):
+            step(h, 0)
         return
 
     stats = outs[nk]
@@ -176,7 +177,8 @@
         return carry
 
     stats[...] = jnp.zeros_like(stats)
-    lax.fori_loop(0, 3, step, 0)
+    for h in range(3):
+        step(h, 0)
     for i in range(nk):
         write_stats(outs[i], stats[i])
 
@@ -237,7 +239,8 @@
             out[pl.ds(pl.multiple_of(h * ROWS, 16), ROWS), :] = acc[k * ROWS : (k + 1) * ROWS].astype(BF)
         return carry
 
-    lax.fori_loop(0, 3, head, 0)
+    for h in range(3):
+        head(h, 0)
     for k, out in enumerate((o0, o1, o2, o3)):
         write_stats(out, stats[k])
 

time: 99.7 us -> 97.4 us (0.977)
  Pallas kernels: 25.2 us -> 22.7 us
  waiting for transfers between devices: 29.8 us -> 31.4 us
  starting transfers between devices: 42.2 us -> 40.8 us
    ppermute x23, waiting for transfers between devices: 29.8 us -> 31.4 us  [moved(): return lax.ppermute(array, axis, [(i, (i + by) % n) for i in range(n)])]
    ppermute x23, starting transfers between devices: 42.2 us -> 40.8 us  [moved(): return lax.ppermute(array, axis, [(i, (i + by) % n) for i in range(n)])]
  transfers between devices with their start and end apart: 23 -> 23, of which waited for: 10 -> 11; matrix products, arithmetic and copies ran while one was open for 1% -> 1% of each run, Pallas kernels for 21% -> 19%
where the time goes in v3:
time: 97.4 us; the launch traced here: 97.3 us
  starting transfers between devices  40.8 us (42%)
  waiting for transfers between devices  31.4 us (32%)
  Pallas kernels  22.7 us (23%)
  local copies, waits for them, and re-layouts  1.54 us (2%)
    ppermute x23, starting transfers between devices, moved(): return lax.ppermute(array, axis, [(i, (i + by) % n) for i in range(n)])  40.8 us
    ppermute x23, waiting for transfers between devices, moved(): return lax.ppermute(array, axis, [(i, (i + by) % n) for i in range(n)])  31.4 us
    pallas_call x2, Pallas kernels, program(): kernel_call(body, state_shape, [SSPEC] + [VSPEC] * (4 + n + len(state)),...  8.46 us
    pallas_call x1, Pallas kernels, program(): kernel_call(placed(functools.partial(ring_body, final, (0, 1, 2, 3), Fals...  5.61 us
    pallas_call x1, Pallas kernels, program(): kernel_call(placed(audio_body), (((PAYLOAD, HEAD), BF),) * 4, [SSPEC] + [...  2.2 us
    pallas_call x1, Pallas kernels, program(): kernel_call(placed(entry_body), (((9, TOKENS, HEAD), BF),) * 2, [HSPEC] *...  2.19 us
    pallas_call x4, Pallas kernels, program(): kernel_call(placed(functools.partial(project_body, k)), (((TOKENS, 768),...  1.99 us
  transfers between devices with their start and end apart: 23, of which 11 were waited for; matrix products, arithmetic and copies ran while one was open for 1% of the time, Pallas kernels for 19%

profile of v3, /device:TPU:1, one launch (start us, length us, event | category | flops | bytes accessed | tf_op | source)
XLA Modules:
  0.0 97.3 jit_solution(3420977142369860729)
XLA Ops:
  0.7 2.2 %shard_map.113 = (bf16[9,144,128]{2,1,0:T(8,128)(2,1)}, bf16[9,144,128]{2,1,0:T(8,128)(2,1)}) custom-call(bf16[128,768]{1,0:T(8,128)(2,1)} %refs_0_.1, bf16[128,768]{1,0:T(8,128)(2,1)} %refs_1_.1, bf16[128,768]{1,0:T(8,128)(2,1)} %refs_2_.5, bf16[16,768]{1,0:T(8,128)(2,1)} %refs_3_.5, bf16[16,768]{1,0:T(8,128)(2,1)} %refs_4_.1, bf16[16,768]{1,0:T(8,128)(2,1)} %refs_5_.1), custom_call_target="tpu_custom_call" | custom-call | flops 2000000000 | bytes 65536 | tf_op jit(solution)/shard_map/pallas_call | solution.py:319
  2.9 3.3 %collective-permute-start = (bf16[9,144,128]{2,1,0:T(8,128)(2,1)}, bf16[9,144,128]{2,1,0:T(8,128)(2,1)S(1)}, u32[]{:S(2)}, u32[]{:S(2)}) collective-permute-start(bf16[9,144,128]{2,1,0:T(8,128)(2,1)} %get-tuple-element.44), channel_id=1, source_target_pairs={{0,1},{1,0},{2,3},{3,2},{4,5},{5,4},{6,7},{7,6},{8,9},{9,8},{10,11... | collective-permute-start | bytes 995336 | tf_op jit(solution)/shard_map/ppermute | solution.py:312
  6.1 1.0 copy-done
  7.1 0.5 collective-permute-done.src
  7.6 0.1 collective-permute-start.4
  7.7 3.9 %collective-permute-start.7 = (bf16[2,6,144,128]{3,2,1,0:T(8,128)(2,1)S(1)}, bf16[2,6,144,128]{3,2,1,0:T(8,128)(2,1)S(1)}, u32[]{:S(2)}, u32[]{:S(2)}) collective-permute-start(bf16[2,6,144,128]{3,2,1,0:T(8,128)(2,1)S(1)} %get-tuple-element.50.refs_5_), channel_id=1, source_target_pairs={{0,14},{2,0},{4,2},{6,4},{8,6},{10,8},{12,10},{14,12},{1,15},{3,1}... | collective-permute-start | bytes 1327112 | tf_op jit(solution)/shard_map/ppermute | solution.py:312
  11.7 10.1 %collective-permute-done.4.refs_6_ = bf16[2,6,144,128]{3,2,1,0:T(8,128)(2,1)S(1)} collective-permute-done((bf16[2,6,144,128]{3,2,1,0:T(8,128)(2,1)S(1)}, bf16[2,6,144,128]{3,2,1,0:T(8,128)(2,1)S(1)}, u32[]{:S(2)}, u32[]{:S(2)}) %collective-permute-start.4) | collective-permute-done | bytes 442400 | tf_op jit(solution)/shard_map/ppermute | solution.py:312
  21.8 0.0 collective-permute-start.5
  21.8 0.0 collective-permute-done.7.refs_7_
  21.8 2.7 %collective-permute-start.8 = (bf16[2,6,144,128]{3,2,1,0:T(8,128)(2,1)S(1)}, bf16[2,6,144,128]{3,2,1,0:T(8,128)(2,1)S(1)}, u32[]{:S(2)}, u32[]{:S(2)}) collective-permute-start(bf16[2,6,144,128]{3,2,1,0:T(8,128)(2,1)S(1)} %collective-permute-done.7.refs_7_), channel_id=1, source_target_pairs={{0,14},{2,0},{4,2},{6,4},{8,6},{10,8},{12,10},{14,12},{1,15},{3,1}... | collective-permute-start | bytes 1327112 | tf_op jit(solution)/shard_map/ppermute | solution.py:312
  24.4 0.1 copy.29
  24.5 0.1 reshape.10
  24.7 0.1 copy.30
  24.8 0.1 reshape.11
  24.9 1.3 %collective-permute-start.1 = (bf16[3,288,128]{2,1,0:T(8,128)(2,1)S(1)}, bf16[3,288,128]{2,1,0:T(8,128)(2,1)S(1)}, u32[]{:S(2)}, u32[]{:S(2)}) collective-permute-start(bf16[3,288,128]{2,1,0:T(8,128)(2,1)S(1)} %get-tuple-element.49.refs_1_), channel_id=1, source_target_pairs={{0,16},{16,32},{32,48},{48,0},{1,17},{17,33},{33,49},{49,1},{2,18}... | collective-permute-start | bytes 663560 | tf_op jit(solution)/shard_map/ppermute | solution.py:312
  26.2 2.5 %collective-permute-start.2 = (bf16[3,288,128]{2,1,0:T(8,128)(2,1)S(1)}, bf16[3,288,128]{2,1,0:T(8,128)(2,1)S(1)}, u32[]{:S(2)}, u32[]{:S(2)}) collective-permute-start(bf16[3,288,128]{2,1,0:T(8,128)(2,1)S(1)} %get-tuple-element.49.refs_1_), channel_id=1, source_target_pairs={{0,32},{16,48},{32,0},{48,16},{1,33},{17,49},{33,1},{49,17},{2,34}... | collective-permute-start | bytes 663560 | tf_op jit(solution)/shard_map/ppermute | solution.py:312
  28.7 1.2 %collective-permute-start.3 = (bf16[3,288,128]{2,1,0:T(8,128)(2,1)S(1)}, bf16[3,288,128]{2,1,0:T(8,128)(2,1)S(1)}, u32[]{:S(2)}, u32[]{:S(2)}) collective-permute-start(bf16[3,288,128]{2,1,0:T(8,128)(2,1)S(1)} %get-tuple-element.49.refs_1_), channel_id=1, source_target_pairs={{0,48},{16,0},{32,16},{48,32},{1,49},{17,1},{33,17},{49,33},{2,50}... | collective-permute-start | bytes 663560 | tf_op jit(solution)/shard_map/ppermute | solution.py:312
  29.9 1.8 %collective-permute-done.1.refs_2_ = bf16[3,288,128]{2,1,0:T(8,128)(2,1)S(1)} collective-permute-done((bf16[3,288,128]{2,1,0:T(8,128)(2,1)S(1)}, bf16[3,288,128]{2,1,0:T(8,128)(2,1)S(1)}, u32[]{:S(2)}, u32[]{:S(2)}) %collective-permute-start.1) | collective-permute-done | bytes 221216 | tf_op jit(solution)/shard_map/ppermute | solution.py:312
  31.7 3.4 %collective-permute-start.15 = (bf16[6,32,128]{2,1,0:T(8,128)(2,1)S(1)}, bf16[6,32,128]{2,1,0:T(8,128)(2,1)S(1)}, u32[]{:S(2)}, u32[]{:S(2)}) collective-permute-start(bf16[6,32,128]{2,1,0:T(8,128)(2,1)S(1)} %get-tuple-element.79), channel_id=1, source_target_pairs={{0,8},{2,10},{4,12},{6,14},{8,0},{10,2},{12,4},{14,6},{1,9},{3,11}... | collective-permute-start | bytes 147464 | tf_op jit(solution)/shard_map/ppermute | solution.py:312
  35.1 0.0 collective-permute-done.5.refs_5_.refs_8_
  35.1 0.0 collective-permute-start.6
  35.1 0.0 collective-permute-done.8.refs_6_.refs_9_
  35.2 2.7 %collective-permute-start.9 = (bf16[2,6,144,128]{3,2,1,0:T(8,128)(2,1)S(1)}, bf16[2,6,144,128]{3,2,1,0:T(8,128)(2,1)S(1)}, u32[]{:S(2)}, u32[]{:S(2)}) collective-permute-start(bf16[2,6,144,128]{3,2,1,0:T(8,128)(2,1)S(1)} %collective-permute-done.8.refs_6_.refs_9_), channel_id=1, source_target_pairs={{0,14},{2,0},{4,2},{6,4},{8,6},{10,8},{12,10},{14,12},{1,15},{3,1}... | collective-permute-start | bytes 1327112 | tf_op jit(solution)/shard_map/ppermute | solution.py:312
  37.8 0.0 collective-permute-done.2.refs_3_
  37.8 4.8 %shard_map.116 = (f32[3,288,128]{2,1,0:T(8,128)S(1)}, f32[3,288,128]{2,1,0:T(8,128)S(1)}, f32[3,288,128]{2,1,0:T(8,128)S(1)}, f32[3,288,128]{2,1,0:T(8,128)S(1)}...) custom-call(s32[256]{0:T(256)S(1)} %constant_dynamic-update-slice_fu, ...), custom_call_target="tpu_custom_call" | custom-call | flops 6000000000 | bytes 65536 | tf_op jit(solution)/shard_map/pallas_call | solution.py:354
  42.6 3.7 %shard_map.117 = (f32[3,288,128]{2,1,0:T(8,128)S(1)}, f32[3,288,128]{2,1,0:T(8,128)S(1)}, f32[3,288,128]{2,1,0:T(8,128)S(1)}, f32[3,288,128]{2,1,0:T(8,128)S(1)}...) custom-call(s32[256]{0:T(256)S(1)} %constant_dynamic-update-slice_fu, ...), custom_call_target="tpu_custom_call", output_to_operand_aliasing={{0}: (7, {}), {1}: (8, {}), {2}: (9, {}), {3}: (10, {}), {4... | custom-call | flops 4000000000 | bytes 65536 | tf_op jit(solution)/shard_map/pallas_call | solution.py:354
  46.3 0.2 collective-permute-done.6.refs_5_.refs_10_
  46.5 0.1 collective-permute-start.10
  46.6 0.0 collective-permute-done.9.refs_6_.refs_11_
  46.6 2.7 %collective-permute-start.11 = (bf16[1,6,144,128]{3,2,1,0:T(8,128)(2,1)S(1)}, bf16[1,6,144,128]{3,2,1,0:T(8,128)(2,1)S(1)}, u32[]{:S(2)}, u32[]{:S(2)}) collective-permute-start(bf16[1,6,144,128]{3,2,1,0:T(8,128)(2,1)S(1)} %slice.9), channel_id=1, source_target_pairs={{0,14},{2,0},{4,2},{6,4},{8,6},{10,8},{12,10},{14,12},{1,15},{3,1}... | collective-permute-start | bytes 663560 | tf_op jit(solution)/shard_map/ppermute | solution.py:312
  49.4 2.2 %shard_map.119 = (bf16[912,128]{1,0:T(8,128)(2,1)S(1)}, bf16[912,128]{1,0:T(8,128)(2,1)S(1)}, bf16[912,128]{1,0:T(8,128)(2,1)S(1)}, bf16[912,128]{1,0:T(8,128)(2,1)S(1)}) custom-call(s32[256]{0:T(256)S(1)} %constant_dynamic-update-slice_fusion.refs_0_, bf16[3,288,128]{2,1,0:T(8,128)(2,1)S(1)} %get-tuple-element.49.refs_1_, ...), custom_call_target="tpu_custom_call" | custom-call | flops 4000000000 | bytes 65536 | tf_op jit(solution)/shard_map/pallas_call | solution.py:358
  51.6 2.5 %collective-permute-start.16 = (bf16[912,128]{1,0:T(8,128)(2,1)S(1)}, bf16[912,128]{1,0:T(8,128)(2,1)S(1)}, u32[]{:S(2)}, u32[]{:S(2)}) collective-permute-start(bf16[912,128]{1,0:T(8,128)(2,1)S(1)} %get-tuple-element.81), channel_id=1, source_target_pairs={{0,48},{16,0},{32,16},{48,32},{1,49},{17,1},{33,17},{49,33},{2,50}... | collective-permute-start | bytes 700424 | tf_op jit(solution)/shard_map/ppermute | solution.py:312
  54.1 1.0 %collective-permute-start.17 = (bf16[912,128]{1,0:T(8,128)(2,1)S(1)}, bf16[912,128]{1,0:T(8,128)(2,1)S(1)}, u32[]{:S(2)}, u32[]{:S(2)}) collective-permute-start(bf16[912,128]{1,0:T(8,128)(2,1)S(1)} %get-tuple-element.82), channel_id=1, source_target_pairs={{0,32},{16,48},{32,0},{48,16},{1,33},{17,49},{33,1},{49,17},{2,34}... | collective-permute-start | bytes 700424 | tf_op jit(solution)/shard_map/ppermute | solution.py:312
  55.1 0.0 collective-permute-start.18
  55.1 0.0 collective-permute-done.10.refs_7_
  55.1 0.0 slice-start
  55.1 0.0 slice-start.2
  55.1 0.0 slice-start.1
  55.2 0.0 slice-start.3
  55.2 5.6 %shard_map.118 = (bf16[912,128]{1,0:T(8,128)(2,1)S(1)}, bf16[912,128]{1,0:T(8,128)(2,1)S(1)}, bf16[912,128]{1,0:T(8,128)(2,1)S(1)}, bf16[912,128]{1,0:T(8,128)(2,1)S(1)}) custom-call(s32[256]{0:T(256)S(1)} %constant_dynamic-update-slice_fusion.refs_0_, bf16[3,288,128]{2,1,0:T(8,128)(2,1)S(1)} %get-tuple-element.49.refs_1_, ...), custom_call_target="tpu_custom_call" | custom-call | flops 6000000000 | bytes 65536 | tf_op jit(solution)/shard_map/pallas_call | solution.py:365
  60.8 2.7 %collective-permute-start.12 = (bf16[912,128]{1,0:T(8,128)(2,1)S(1)}, bf16[912,128]{1,0:T(8,128)(2,1)S(1)}, u32[]{:S(2)}, u32[]{:S(2)}) collective-permute-start(bf16[912,128]{1,0:T(8,128)(2,1)S(1)} %get-tuple-element.76), channel_id=1, source_target_pairs={{0,48},{16,0},{32,16},{48,32},{1,49},{17,1},{33,17},{49,33},{2,50}... | collective-permute-start | bytes 700424 | tf_op jit(solution)/shard_map/ppermute | solution.py:312
  63.5 0.7 collective-permute-start.13
  64.3 0.0 collective-permute-done.16.p1
  64.3 0.0 collective-permute-start.14
  64.3 0.0 collective-permute-done.17.p2
  64.3 0.0 collective-permute-done.18.p3
  64.3 0.7 shard_map.120.extra
  65.0 5.1 %collective-permute-done.12.p1 = bf16[912,128]{1,0:T(8,128)(2,1)S(1)} collective-permute-done((bf16[912,128]{1,0:T(8,128)(2,1)S(1)}, bf16[912,128]{1,0:T(8,128)(2,1)S(1)}, u32[]{:S(2)}, u32[]{:S(2)}) %collective-permute-start.12) | collective-permute-done | bytes 233504 | tf_op jit(solution)/shard_map/ppermute | solution.py:312
  70.1 1.3 %collective-permute-done.13.p2 = bf16[912,128]{1,0:T(8,128)(2,1)S(1)} collective-permute-done((bf16[912,128]{1,0:T(8,128)(2,1)S(1)}, bf16[912,128]{1,0:T(8,128)(2,1)S(1)}, u32[]{:S(2)}, u32[]{:S(2)}) %collective-permute-start.13) | collective-permute-done | bytes 233504 | tf_op jit(solution)/shard_map/ppermute | solution.py:312
  71.3 2.9 %collective-permute-done.14.p3 = bf16[912,128]{1,0:T(8,128)(2,1)S(1)} collective-permute-done((bf16[912,128]{1,0:T(8,128)(2,1)S(1)}, bf16[912,128]{1,0:T(8,128)(2,1)S(1)}, u32[]{:S(2)}, u32[]{:S(2)}) %collective-permute-start.14) | collective-permute-done | bytes 233504 | tf_op jit(solution)/shard_map/ppermute | solution.py:312
  74.2 0.7 shard_map.121
  74.9 5.4 %collective-permute-start.19 = (bf16[3,144,128]{2,1,0:T(8,128)(2,1)S(1)}, bf16[3,144,128]{2,1,0:T(8,128)(2,1)S(1)}, u32[]{:S(2)}, u32[]{:S(2)}) collective-permute-start(bf16[3,144,128]{2,1,0:T(8,128)(2,1)S(1)} %get-tuple-element.85), channel_id=1, source_target_pairs={{0,1},{1,0},{2,3},{3,2},{4,5},{5,4},{6,7},{7,6},{8,9},{9,8},{10,11... | collective-permute-start | bytes 331784 | tf_op jit(solution)/shard_map/ppermute | solution.py:312
  80.3 1.0 collective-permute-done.19.refs_1_
  81.3 0.5 shard_map.124
  81.8 2.8 %collective-permute-start.22 = (bf16[144,768]{1,0:T(8,128)(2,1)S(1)}, bf16[144,768]{1,0:T(8,128)(2,1)S(1)}, u32[]{:S(2)}, u32[]{:S(2)}) collective-permute-start(bf16[144,768]{1,0:T(8,128)(2,1)S(1)} %shard_map.124), channel_id=1, source_target_pairs={{0,192},{64,0},{128,64},{192,128},{1,193},{65,1},{129,65},{193,129... | collective-permute-start | bytes 663560 | tf_op jit(solution)/shard_map/ppermute | solution.py:312
  84.6 0.5 shard_map.123
  85.1 0.1 collective-permute-start.21
  85.2 0.5 shard_map.122
  85.7 1.7 %collective-permute-start.20 = (bf16[144,768]{1,0:T(8,128)(2,1)S(1)}, bf16[144,768]{1,0:T(8,128)(2,1)S(1)}, u32[]{:S(2)}, u32[]{:S(2)}) collective-permute-start(bf16[144,768]{1,0:T(8,128)(2,1)S(1)} %shard_map.122), channel_id=1, source_target_pairs={{0,128},{64,192},{128,0},{192,64},{1,129},{65,193},{129,1},{193,65... | collective-permute-start | bytes 663560 | tf_op jit(solution)/shard_map/ppermute | solution.py:312
  87.4 0.5 shard_map.125.p3
  87.9 1.1 %collective-permute-done.22.p2 = bf16[144,768]{1,0:T(8,128)(2,1)S(1)} collective-permute-done((bf16[144,768]{1,0:T(8,128)(2,1)S(1)}, bf16[144,768]{1,0:T(8,128)(2,1)S(1)}, u32[]{:S(2)}, u32[]{:S(2)}) %collective-permute-start.22) | collective-permute-done | bytes 221216 | tf_op jit(solution)/shard_map/ppermute | solution.py:312
  89.0 4.7 %collective-permute-done.21.p1 = bf16[144,768]{1,0:T(8,128)(2,1)S(1)} collective-permute-done((bf16[144,768]{1,0:T(8,128)(2,1)S(1)}, bf16[144,768]{1,0:T(8,128)(2,1)S(1)}, u32[]{:S(2)}, u32[]{:S(2)}) %collective-permute-start.21) | collective-permute-done | bytes 221216 | tf_op jit(solution)/shard_map/ppermute | solution.py:312
  93.7 2.7 %collective-permute-done.20.p0 = bf16[144,768]{1,0:T(8,128)(2,1)S(1)} collective-permute-done((bf16[144,768]{1,0:T(8,128)(2,1)S(1)}, bf16[144,768]{1,0:T(8,128)(2,1)S(1)}, u32[]{:S(2)}, u32[]{:S(2)}) %collective-permute-start.20) | collective-permute-done | bytes 221216 | tf_op jit(solution)/shard_map/ppermute | solution.py:312
  96.5 0.8 shard_map.126
  (21 shorter events, 0.1 us)
Async XLA Ops:
  0.6 23.8 %copy-start.1 = (s32[64,2]{0,1:T(2,128)S(1)}, s32[64,2]{0,1:T(2,128)}, u32[]{:S(2)}) copy-start(s32[64,2]{0,1:T(2,128)} %param.17) | copy-start | bytes 1540
  0.6 24.0 %copy-start.2 = (s32[64,2]{0,1:T(2,128)S(1)}, s32[64,2]{0,1:T(2,128)}, u32[]{:S(2)}) copy-start(s32[64,2]{0,1:T(2,128)} %param.16) | copy-start | bytes 1540
  2.9 4.8 %collective-permute-start = (bf16[9,144,128]{2,1,0:T(8,128)(2,1)}, bf16[9,144,128]{2,1,0:T(8,128)(2,1)S(1)}, u32[]{:S(2)}, u32[]{:S(2)}) collective-permute-start(bf16[9,144,128]{2,1,0:T(8,128)(2,1)} %get-tuple-element.44), channel_id=1, source_target_pairs={{0,1},{1,0},{2,3},{3,2},{4,5},{5,4},{6,7},{7,6},{8,9},{9,8},{10,11... | collective-permute-start | bytes 995336 | tf_op jit(solution)/shard_map/ppermute | solution.py:312
  6.1 1.0 %copy-start = (bf16[9,144,128]{2,1,0:T(8,128)(2,1)S(1)}, bf16[9,144,128]{2,1,0:T(8,128)(2,1)}, u32[]{:S(2)}) copy-start(bf16[9,144,128]{2,1,0:T(8,128)(2,1)} %get-tuple-element.45.src) | copy-start | bytes 995332
  7.6 14.1 %collective-permute-start.4 = (bf16[2,6,144,128]{3,2,1,0:T(8,128)(2,1)S(1)}, bf16[2,6,144,128]{3,2,1,0:T(8,128)(2,1)S(1)}, u32[]{:S(2)}, u32[]{:S(2)}) collective-permute-start(bf16[2,6,144,128]{3,2,1,0:T(8,128)(2,1)S(1)} %get-tuple-element.50.refs_5_), channel_id=1, source_target_pairs={{0,2},{2,4},{4,6},{6,8},{8,10},{10,12},{12,14},{14,0},{1,3},{3,5},... | collective-permute-start | bytes 1327112 | tf_op jit(solution)/shard_map/ppermute | solution.py:312
  7.7 14.0 %collective-permute-start.7 = (bf16[2,6,144,128]{3,2,1,0:T(8,128)(2,1)S(1)}, bf16[2,6,144,128]{3,2,1,0:T(8,128)(2,1)S(1)}, u32[]{:S(2)}, u32[]{:S(2)}) collective-permute-start(bf16[2,6,144,128]{3,2,1,0:T(8,128)(2,1)S(1)} %get-tuple-element.50.refs_5_), channel_id=1, source_target_pairs={{0,14},{2,0},{4,2},{6,4},{8,6},{10,8},{12,10},{14,12},{1,15},{3,1}... | collective-permute-start | bytes 1327112 | tf_op jit(solution)/shard_map/ppermute | solution.py:312
  21.8 13.4 %collective-permute-start.5 = (bf16[2,6,144,128]{3,2,1,0:T(8,128)(2,1)S(1)}, bf16[2,6,144,128]{3,2,1,0:T(8,128)(2,1)S(1)}, u32[]{:S(2)}, u32[]{:S(2)}) collective-permute-start(bf16[2,6,144,128]{3,2,1,0:T(8,128)(2,1)S(1)} %collective-permute-done.4.refs_6_), channel_id=1, source_target_pairs={{0,2},{2,4},{4,6},{6,8},{8,10},{10,12},{12,14},{14,0},{1,3},{3,5},... | collective-permute-start | bytes 1327112 | tf_op jit(solution)/shard_map/ppermute | solution.py:312
  21.8 13.4 %collective-permute-start.8 = (bf16[2,6,144,128]{3,2,1,0:T(8,128)(2,1)S(1)}, bf16[2,6,144,128]{3,2,1,0:T(8,128)(2,1)S(1)}, u32[]{:S(2)}, u32[]{:S(2)}) collective-permute-start(bf16[2,6,144,128]{3,2,1,0:T(8,128)(2,1)S(1)} %collective-permute-done.7.refs_7_), channel_id=1, source_target_pairs={{0,14},{2,0},{4,2},{6,4},{8,6},{10,8},{12,10},{14,12},{1,15},{3,1}... | collective-permute-start | bytes 1327112 | tf_op jit(solution)/shard_map/ppermute | solution.py:312
  24.9 6.8 %collective-permute-start.1 = (bf16[3,288,128]{2,1,0:T(8,128)(2,1)S(1)}, bf16[3,288,128]{2,1,0:T(8,128)(2,1)S(1)}, u32[]{:S(2)}, u32[]{:S(2)}) collective-permute-start(bf16[3,288,128]{2,1,0:T(8,128)(2,1)S(1)} %get-tuple-element.49.refs_1_), channel_id=1, source_target_pairs={{0,16},{16,32},{32,48},{48,0},{1,17},{17,33},{33,49},{49,1},{2,18}... | collective-permute-start | bytes 663560 | tf_op jit(solution)/shard_map/ppermute | solution.py:312
  26.2 11.6 %collective-permute-start.2 = (bf16[3,288,128]{2,1,0:T(8,128)(2,1)S(1)}, bf16[3,288,128]{2,1,0:T(8,128)(2,1)S(1)}, u32[]{:S(2)}, u32[]{:S(2)}) collective-permute-start(bf16[3,288,128]{2,1,0:T(8,128)(2,1)S(1)} %get-tuple-element.49.refs_1_), channel_id=1, source_target_pairs={{0,32},{16,48},{32,0},{48,16},{1,33},{17,49},{33,1},{49,17},{2,34}... | collective-permute-start | bytes 663560 | tf_op jit(solution)/shard_map/ppermute | solution.py:312
  28.7 9.2 %collective-permute-start.3 = (bf16[3,288,128]{2,1,0:T(8,128)(2,1)S(1)}, bf16[3,288,128]{2,1,0:T(8,128)(2,1)S(1)}, u32[]{:S(2)}, u32[]{:S(2)}) collective-permute-start(bf16[3,288,128]{2,1,0:T(8,128)(2,1)S(1)} %get-tuple-element.49.refs_1_), channel_id=1, source_target_pairs={{0,48},{16,0},{32,16},{48,32},{1,49},{17,1},{33,17},{49,33},{2,50}... | collective-permute-start | bytes 663560 | tf_op jit(solution)/shard_map/ppermute | solution.py:312
  31.7 17.7 %collective-permute-start.15 = (bf16[6,32,128]{2,1,0:T(8,128)(2,1)S(1)}, bf16[6,32,128]{2,1,0:T(8,128)(2,1)S(1)}, u32[]{:S(2)}, u32[]{:S(2)}) collective-permute-start(bf16[6,32,128]{2,1,0:T(8,128)(2,1)S(1)} %get-tuple-element.79), channel_id=1, source_target_pairs={{0,8},{2,10},{4,12},{6,14},{8,0},{10,2},{12,4},{14,6},{1,9},{3,11}... | collective-permute-start | bytes 147464 | tf_op jit(solution)/shard_map/ppermute | solution.py:312
  35.1 11.3 %collective-permute-start.6 = (bf16[2,6,144,128]{3,2,1,0:T(8,128)(2,1)S(1)}, bf16[2,6,144,128]{3,2,1,0:T(8,128)(2,1)S(1)}, u32[]{:S(2)}, u32[]{:S(2)}) collective-permute-start(bf16[2,6,144,128]{3,2,1,0:T(8,128)(2,1)S(1)} %collective-permute-done.5.refs_5_.refs_8_), channel_id=1, source_target_pairs={{0,2},{2,4},{4,6},{6,8},{8,10},{10,12},{12,14},{14,0},{1,3},{3,5},... | collective-permute-start | bytes 1327112 | tf_op jit(solution)/shard_map/ppermute | solution.py:312
  35.2 11.4 %collective-permute-start.9 = (bf16[2,6,144,128]{3,2,1,0:T(8,128)(2,1)S(1)}, bf16[2,6,144,128]{3,2,1,0:T(8,128)(2,1)S(1)}, u32[]{:S(2)}, u32[]{:S(2)}) collective-permute-start(bf16[2,6,144,128]{3,2,1,0:T(8,128)(2,1)S(1)} %collective-permute-done.8.refs_6_.refs_9_), channel_id=1, source_target_pairs={{0,14},{2,0},{4,2},{6,4},{8,6},{10,8},{12,10},{14,12},{1,15},{3,1}... | collective-permute-start | bytes 1327112 | tf_op jit(solution)/shard_map/ppermute | solution.py:312
  46.5 8.6 %collective-permute-start.10 = (bf16[1,6,144,128]{3,2,1,0:T(8,128)(2,1)S(1)}, bf16[1,6,144,128]{3,2,1,0:T(8,128)(2,1)S(1)}, u32[]{:S(2)}, u32[]{:S(2)}) collective-permute-start(bf16[1,6,144,128]{3,2,1,0:T(8,128)(2,1)S(1)} %slice.8), channel_id=1, source_target_pairs={{0,2},{2,4},{4,6},{6,8},{8,10},{10,12},{12,14},{14,0},{1,3},{3,5},... | collective-permute-start | bytes 663560 | tf_op jit(solution)/shard_map/ppermute | solution.py:312
  46.6 8.5 %collective-permute-start.11 = (bf16[1,6,144,128]{3,2,1,0:T(8,128)(2,1)S(1)}, bf16[1,6,144,128]{3,2,1,0:T(8,128)(2,1)S(1)}, u32[]{:S(2)}, u32[]{:S(2)}) collective-permute-start(bf16[1,6,144,128]{3,2,1,0:T(8,128)(2,1)S(1)} %slice.9), channel_id=1, source_target_pairs={{0,14},{2,0},{4,2},{6,4},{8,6},{10,8},{12,10},{14,12},{1,15},{3,1}... | collective-permute-start | bytes 663560 | tf_op jit(solution)/shard_map/ppermute | solution.py:312
  51.6 12.7 %collective-permute-start.16 = (bf16[912,128]{1,0:T(8,128)(2,1)S(1)}, bf16[912,128]{1,0:T(8,128)(2,1)S(1)}, u32[]{:S(2)}, u32[]{:S(2)}) collective-permute-start(bf16[912,128]{1,0:T(8,128)(2,1)S(1)} %get-tuple-element.81), channel_id=1, source_target_pairs={{0,48},{16,0},{32,16},{48,32},{1,49},{17,1},{33,17},{49,33},{2,50}... | collective-permute-start | bytes 700424 | tf_op jit(solution)/shard_map/ppermute | solution.py:312
  54.1 10.2 %collective-permute-start.17 = (bf16[912,128]{1,0:T(8,128)(2,1)S(1)}, bf16[912,128]{1,0:T(8,128)(2,1)S(1)}, u32[]{:S(2)}, u32[]{:S(2)}) collective-permute-start(bf16[912,128]{1,0:T(8,128)(2,1)S(1)} %get-tuple-element.82), channel_id=1, source_target_pairs={{0,32},{16,48},{32,0},{48,16},{1,33},{17,49},{33,1},{49,17},{2,34}... | collective-permute-start | bytes 700424 | tf_op jit(solution)/shard_map/ppermute | solution.py:312
  55.1 9.2 %collective-permute-start.18 = (bf16[912,128]{1,0:T(8,128)(2,1)S(1)}, bf16[912,128]{1,0:T(8,128)(2,1)S(1)}, u32[]{:S(2)}, u32[]{:S(2)}) collective-permute-start(bf16[912,128]{1,0:T(8,128)(2,1)S(1)} %get-tuple-element.83), channel_id=1, source_target_pairs={{0,16},{16,32},{32,48},{48,0},{1,17},{17,33},{33,49},{49,1},{2,18}... | collective-permute-start | bytes 700424 | tf_op jit(solution)/shard_map/ppermute | solution.py:312
  55.1 26.1 %slice-start = ((s8[4718592]{0:T(1024)(128)(4,1)}), s8[4194304]{0:T(1024)(128)(4,1)S(1)}, s32[]{:S(2)}) async-start(s8[4718592]{0:T(1024)(128)(4,1)} %bitcast), calls=%async_computation | async-start | bytes 8388608
  55.1 26.1 %slice-start.2 = ((s8[4718592]{0:T(1024)(128)(4,1)}), s8[4194304]{0:T(1024)(128)(4,1)S(1)}, s32[]{:S(2)}) async-start(s8[4718592]{0:T(1024)(128)(4,1)} %bitcast.2), calls=%async_computation.2 | async-start | bytes 8388608
  55.1 26.1 %slice-start.1 = ((s8[4718592]{0:T(1024)(128)(4,1)}), s8[524288]{0:T(1024)(128)(4,1)S(1)}, s32[]{:S(2)}) async-start(s8[4718592]{0:T(1024)(128)(4,1)} %bitcast), calls=%async_computation.1 | async-start | bytes 1048576
  55.2 26.1 %slice-start.3 = ((s8[4718592]{0:T(1024)(128)(4,1)}), s8[524288]{0:T(1024)(128)(4,1)S(1)}, s32[]{:S(2)}) async-start(s8[4718592]{0:T(1024)(128)(4,1)} %bitcast.2), calls=%async_computation.3 | async-start | bytes 1048576
  60.8 9.3 %collective-permute-start.12 = (bf16[912,128]{1,0:T(8,128)(2,1)S(1)}, bf16[912,128]{1,0:T(8,128)(2,1)S(1)}, u32[]{:S(2)}, u32[]{:S(2)}) collective-permute-start(bf16[912,128]{1,0:T(8,128)(2,1)S(1)} %get-tuple-element.76), channel_id=1, source_target_pairs={{0,48},{16,0},{32,16},{48,32},{1,49},{17,1},{33,17},{49,33},{2,50}... | collective-permute-start | bytes 700424 | tf_op jit(solution)/shard_map/ppermute | solution.py:312
  63.5 7.8 %collective-permute-start.13 = (bf16[912,128]{1,0:T(8,128)(2,1)S(1)}, bf16[912,128]{1,0:T(8,128)(2,1)S(1)}, u32[]{:S(2)}, u32[]{:S(2)}) collective-permute-start(bf16[912,128]{1,0:T(8,128)(2,1)S(1)} %get-tuple-element.77), channel_id=1, source_target_pairs={{0,32},{16,48},{32,0},{48,16},{1,33},{17,49},{33,1},{49,17},{2,34}... | collective-permute-start | bytes 700424 | tf_op jit(solution)/shard_map/ppermute | solution.py:312
  64.3 9.9 %collective-permute-start.14 = (bf16[912,128]{1,0:T(8,128)(2,1)S(1)}, bf16[912,128]{1,0:T(8,128)(2,1)S(1)}, u32[]{:S(2)}, u32[]{:S(2)}) collective-permute-start(bf16[912,128]{1,0:T(8,128)(2,1)S(1)} %get-tuple-element.78), channel_id=1, source_target_pairs={{0,16},{16,32},{32,48},{48,0},{1,17},{17,33},{33,49},{49,1},{2,18}... | collective-permute-start | bytes 700424 | tf_op jit(solution)/shard_map/ppermute | solution.py:312
  74.9 6.3 %collective-permute-start.19 = (bf16[3,144,128]{2,1,0:T(8,128)(2,1)S(1)}, bf16[3,144,128]{2,1,0:T(8,128)(2,1)S(1)}, u32[]{:S(2)}, u32[]{:S(2)}) collective-permute-start(bf16[3,144,128]{2,1,0:T(8,128)(2,1)S(1)} %get-tuple-element.85), channel_id=1, source_target_pairs={{0,1},{1,0},{2,3},{3,2},{4,5},{5,4},{6,7},{7,6},{8,9},{9,8},{10,11... | collective-permute-start | bytes 331784 | tf_op jit(solution)/shard_map/ppermute | solution.py:312
  81.8 7.2 %collective-permute-start.22 = (bf16[144,768]{1,0:T(8,128)(2,1)S(1)}, bf16[144,768]{1,0:T(8,128)(2,1)S(1)}, u32[]{:S(2)}, u32[]{:S(2)}) collective-permute-start(bf16[144,768]{1,0:T(8,128)(2,1)S(1)} %shard_map.124), channel_id=1, source_target_pairs={{0,192},{64,0},{128,64},{192,128},{1,193},{65,1},{129,65},{193,129... | collective-permute-start | bytes 663560 | tf_op jit(solution)/shard_map/ppermute | solution.py:312
  85.1 8.6 %collective-permute-start.21 = (bf16[144,768]{1,0:T(8,128)(2,1)S(1)}, bf16[144,768]{1,0:T(8,128)(2,1)S(1)}, u32[]{:S(2)}, u32[]{:S(2)}) collective-permute-start(bf16[144,768]{1,0:T(8,128)(2,1)S(1)} %shard_map.123), channel_id=1, source_target_pairs={{0,64},{64,128},{128,192},{192,0},{1,65},{65,129},{129,193},{193,1... | collective-permute-start | bytes 663560 | tf_op jit(solution)/shard_map/ppermute | solution.py:312
  85.7 10.8 %collective-permute-start.20 = (bf16[144,768]{1,0:T(8,128)(2,1)S(1)}, bf16[144,768]{1,0:T(8,128)(2,1)S(1)}, u32[]{:S(2)}, u32[]{:S(2)}) collective-permute-start(bf16[144,768]{1,0:T(8,128)(2,1)S(1)} %shard_map.122), channel_id=1, source_target_pairs={{0,128},{64,192},{128,0},{192,64},{1,129},{65,193},{129,1},{193,65... | collective-permute-start | bytes 663560 | tf_op jit(solution)/shard_map/ppermute | solution.py:312

commit v4 on v3

--- a/solution.py
+++ b/solution.py
@@ -61,19 +61,25 @@
     copies = [pltpu.make_async_copy(s, d, sems.at[i]) for i, (s, d) in enumerate(pairs)]
     for cp in copies:
         cp.start()
-    for cp in copies:
+    core = pos[2]
+
+    def targets():
+        for half, out in ((1, far), (0, own)):
+            side = core if half == 0 else 1 - core
+            for h in range(3):
+                yield out, h, pl.ds(pl.multiple_of((side * 3 + h) * HEAD, HEAD), HEAD)
+
+    copies[0].wait()
+    for out, h, cols in targets():
+        out[h, 0:VBLK, :] = k[:, cols].astype(F32).T.astype(BF)
+    for cp in copies[1:]:
         cp.wait()
-    core = pos[2]
-    for half, out in ((1, far), (0, own)):
-        side = core if half == 0 else 1 - core
-        for h in range(3):
-            cols = pl.ds(pl.multiple_of((side * 3 + h) * HEAD, HEAD), HEAD)
-            out[h, 0:VBLK, :] = k[:, cols].astype(F32).T.astype(BF)
-            out[h, VBLK:TOKENS, :] = ka[:, cols]
-            out[3 + h, 0:VBLK, :] = v[:, cols]
-            out[3 + h, VBLK:TOKENS, :] = va[:, cols]
-            out[6 + h, 0:VBLK, :] = q[:, cols]
-            out[6 + h, VBLK:TOKENS, :] = qa[:, cols]
+    for out, h, cols in targets():
+        out[h, VBLK:TOKENS, :] = ka[:, cols]
+        out[3 + h, 0:VBLK, :] = v[:, cols]
+        out[3 + h, VBLK:TOKENS, :] = va[:, cols]
+        out[6 + h, 0:VBLK, :] = q[:, cols]
+        out[6 + h, VBLK:TOKENS, :] = qa[:, cols]
 
 
 def chip_body(r, src, *refs):

time: 97.4 us -> 97.3 us (level)
  no operation moved by 1% of the time
where the time goes in v4:
time: 97.3 us; the launch traced here: 97.2 us
  starting transfers between devices  40.8 us (42%)
  waiting for transfers between devices  31.4 us (32%)
  Pallas kernels  22.7 us (23%)
  local copies, waits for them, and re-layouts  1.54 us (2%)
    ppermute x23, starting transfers between devices, moved(): return lax.ppermute(array, axis, [(i, (i + by) % n) for i in range(n)])  40.8 us
    ppermute x23, waiting for transfers between devices, moved(): return lax.ppermute(array, axis, [(i, (i + by) % n) for i in range(n)])  31.4 us
    pallas_call x2, Pallas kernels, program(): kernel_call(body, state_shape, [SSPEC] + [VSPEC] * (4 + n + len(state)),...  8.46 us
    pallas_call x1, Pallas kernels, program(): kernel_call(placed(functools.partial(ring_body, final, (0, 1, 2, 3), Fals...  5.61 us
    pallas_call x1, Pallas kernels, program(): kernel_call(placed(audio_body), (((PAYLOAD, HEAD), BF),) * 4, [SSPEC] + [...  2.2 us
    pallas_call x1, Pallas kernels, program(): kernel_call(placed(entry_body), (((9, TOKENS, HEAD), BF),) * 2, [HSPEC] *...  2.12 us
    pallas_call x4, Pallas kernels, program(): kernel_call(placed(functools.partial(project_body, k)), (((TOKENS, 768),...  1.98 us
  transfers between devices with their start and end apart: 23, of which 11 were waited for; matrix products, arithmetic and copies ran while one was open for 1% of the time, Pallas kernels for 19%

profile of v4, /device:TPU:1, one launch (start us, length us, event | category | flops | bytes accessed | tf_op | source)
XLA Modules:
  0.0 97.2 jit_solution(1146478261840392256)
XLA Ops:
  0.7 2.1 %shard_map.113 = (bf16[9,144,128]{2,1,0:T(8,128)(2,1)}, bf16[9,144,128]{2,1,0:T(8,128)(2,1)}) custom-call(bf16[128,768]{1,0:T(8,128)(2,1)} %refs_0_.1, bf16[128,768]{1,0:T(8,128)(2,1)} %refs_1_.1, bf16[128,768]{1,0:T(8,128)(2,1)} %refs_2_.5, bf16[16,768]{1,0:T(8,128)(2,1)} %refs_3_.5, bf16[16,768]{1,0:T(8,128)(2,1)} %refs_4_.1, bf16[16,768]{1,0:T(8,128)(2,1)} %refs_5_.1), custom_call_target="tpu_custom_call" | custom-call | flops 2000000000 | bytes 65536 | tf_op jit(solution)/shard_map/pallas_call | solution.py:325
  2.8 3.3 %collective-permute-start = (bf16[9,144,128]{2,1,0:T(8,128)(2,1)}, bf16[9,144,128]{2,1,0:T(8,128)(2,1)S(1)}, u32[]{:S(2)}, u32[]{:S(2)}) collective-permute-start(bf16[9,144,128]{2,1,0:T(8,128)(2,1)} %get-tuple-element.44), channel_id=1, source_target_pairs={{0,1},{1,0},{2,3},{3,2},{4,5},{5,4},{6,7},{7,6},{8,9},{9,8},{10,11... | collective-permute-start | bytes 995336 | tf_op jit(solution)/shard_map/ppermute | solution.py:318
  6.1 1.0 %copy-done = bf16[9,144,128]{2,1,0:T(8,128)(2,1)S(1)} copy-done((bf16[9,144,128]{2,1,0:T(8,128)(2,1)S(1)}, bf16[9,144,128]{2,1,0:T(8,128)(2,1)}, u32[]{:S(2)}) %copy-start) | copy-done | bytes 331800
  7.1 0.5 collective-permute-done.src
  7.6 0.1 collective-permute-start.4
  7.7 3.9 %collective-permute-start.7 = (bf16[2,6,144,128]{3,2,1,0:T(8,128)(2,1)S(1)}, bf16[2,6,144,128]{3,2,1,0:T(8,128)(2,1)S(1)}, u32[]{:S(2)}, u32[]{:S(2)}) collective-permute-start(bf16[2,6,144,128]{3,2,1,0:T(8,128)(2,1)S(1)} %get-tuple-element.50.refs_5_), channel_id=1, source_target_pairs={{0,14},{2,0},{4,2},{6,4},{8,6},{10,8},{12,10},{14,12},{1,15},{3,1}... | collective-permute-start | bytes 1327112 | tf_op jit(solution)/shard_map/ppermute | solution.py:318
  11.6 10.1 %collective-permute-done.4.refs_6_ = bf16[2,6,144,128]{3,2,1,0:T(8,128)(2,1)S(1)} collective-permute-done((bf16[2,6,144,128]{3,2,1,0:T(8,128)(2,1)S(1)}, bf16[2,6,144,128]{3,2,1,0:T(8,128)(2,1)S(1)}, u32[]{:S(2)}, u32[]{:S(2)}) %collective-permute-start.4) | collective-permute-done | bytes 442400 | tf_op jit(solution)/shard_map/ppermute | solution.py:318
  21.7 0.0 collective-permute-start.5
  21.7 0.0 collective-permute-done.7.refs_7_
  21.7 2.7 %collective-permute-start.8 = (bf16[2,6,144,128]{3,2,1,0:T(8,128)(2,1)S(1)}, bf16[2,6,144,128]{3,2,1,0:T(8,128)(2,1)S(1)}, u32[]{:S(2)}, u32[]{:S(2)}) collective-permute-start(bf16[2,6,144,128]{3,2,1,0:T(8,128)(2,1)S(1)} %collective-permute-done.7.refs_7_), channel_id=1, source_target_pairs={{0,14},{2,0},{4,2},{6,4},{8,6},{10,8},{12,10},{14,12},{1,15},{3,1}... | collective-permute-start | bytes 1327112 | tf_op jit(solution)/shard_map/ppermute | solution.py:318
  24.4 0.1 copy.29
  24.5 0.1 reshape.10
  24.6 0.1 copy.30
  24.7 0.1 reshape.11
  24.9 1.3 %collective-permute-start.1 = (bf16[3,288,128]{2,1,0:T(8,128)(2,1)S(1)}, bf16[3,288,128]{2,1,0:T(8,128)(2,1)S(1)}, u32[]{:S(2)}, u32[]{:S(2)}) collective-permute-start(bf16[3,288,128]{2,1,0:T(8,128)(2,1)S(1)} %get-tuple-element.49.refs_1_), channel_id=1, source_target_pairs={{0,16},{16,32},{32,48},{48,0},{1,17},{17,33},{33,49},{49,1},{2,18}... | collective-permute-start | bytes 663560 | tf_op jit(solution)/shard_map/ppermute | solution.py:318
  26.1 2.5 %collective-permute-start.2 = (bf16[3,288,128]{2,1,0:T(8,128)(2,1)S(1)}, bf16[3,288,128]{2,1,0:T(8,128)(2,1)S(1)}, u32[]{:S(2)}, u32[]{:S(2)}) collective-permute-start(bf16[3,288,128]{2,1,0:T(8,128)(2,1)S(1)} %get-tuple-element.49.refs_1_), channel_id=1, source_target_pairs={{0,32},{16,48},{32,0},{48,16},{1,33},{17,49},{33,1},{49,17},{2,34}... | collective-permute-start | bytes 663560 | tf_op jit(solution)/shard_map/ppermute | solution.py:318
  28.6 1.2 %collective-permute-start.3 = (bf16[3,288,128]{2,1,0:T(8,128)(2,1)S(1)}, bf16[3,288,128]{2,1,0:T(8,128)(2,1)S(1)}, u32[]{:S(2)}, u32[]{:S(2)}) collective-permute-start(bf16[3,288,128]{2,1,0:T(8,128)(2,1)S(1)} %get-tuple-element.49.refs_1_), channel_id=1, source_target_pairs={{0,48},{16,0},{32,16},{48,32},{1,49},{17,1},{33,17},{49,33},{2,50}... | collective-permute-start | bytes 663560 | tf_op jit(solution)/shard_map/ppermute | solution.py:318
  29.8 1.8 %collective-permute-done.1.refs_2_ = bf16[3,288,128]{2,1,0:T(8,128)(2,1)S(1)} collective-permute-done((bf16[3,288,128]{2,1,0:T(8,128)(2,1)S(1)}, bf16[3,288,128]{2,1,0:T(8,128)(2,1)S(1)}, u32[]{:S(2)}, u32[]{:S(2)}) %collective-permute-start.1) | collective-permute-done | bytes 221216 | tf_op jit(solution)/shard_map/ppermute | solution.py:318
  31.6 3.4 %collective-permute-start.15 = (bf16[6,32,128]{2,1,0:T(8,128)(2,1)S(1)}, bf16[6,32,128]{2,1,0:T(8,128)(2,1)S(1)}, u32[]{:S(2)}, u32[]{:S(2)}) collective-permute-start(bf16[6,32,128]{2,1,0:T(8,128)(2,1)S(1)} %get-tuple-element.79), channel_id=1, source_target_pairs={{0,8},{2,10},{4,12},{6,14},{8,0},{10,2},{12,4},{14,6},{1,9},{3,11}... | collective-permute-start | bytes 147464 | tf_op jit(solution)/shard_map/ppermute | solution.py:318
  35.1 0.0 collective-permute-done.5.refs_5_.refs_8_
  35.1 0.0 collective-permute-start.6
  35.1 0.0 collective-permute-done.8.refs_6_.refs_9_
  35.1 2.7 %collective-permute-start.9 = (bf16[2,6,144,128]{3,2,1,0:T(8,128)(2,1)S(1)}, bf16[2,6,144,128]{3,2,1,0:T(8,128)(2,1)S(1)}, u32[]{:S(2)}, u32[]{:S(2)}) collective-permute-start(bf16[2,6,144,128]{3,2,1,0:T(8,128)(2,1)S(1)} %collective-permute-done.8.refs_6_.refs_9_), channel_id=1, source_target_pairs={{0,14},{2,0},{4,2},{6,4},{8,6},{10,8},{12,10},{14,12},{1,15},{3,1}... | collective-permute-start | bytes 1327112 | tf_op jit(solution)/shard_map/ppermute | solution.py:318
  37.8 0.0 collective-permute-done.2.refs_3_
  37.8 0.0 collective-permute-done.3.refs_4_
  37.8 4.8 %shard_map.116 = (f32[3,288,128]{2,1,0:T(8,128)S(1)}, f32[3,288,128]{2,1,0:T(8,128)S(1)}, f32[3,288,128]{2,1,0:T(8,128)S(1)}, f32[3,288,128]{2,1,0:T(8,128)S(1)}...) custom-call(s32[256]{0:T(256)S(1)} %constant_dynamic-update-slice_fu, ...), custom_call_target="tpu_custom_call" | custom-call | flops 6000000000 | bytes 65536 | tf_op jit(solution)/shard_map/pallas_call | solution.py:360
  42.6 3.7 %shard_map.117 = (f32[3,288,128]{2,1,0:T(8,128)S(1)}, f32[3,288,128]{2,1,0:T(8,128)S(1)}, f32[3,288,128]{2,1,0:T(8,128)S(1)}, f32[3,288,128]{2,1,0:T(8,128)S(1)}...) custom-call(s32[256]{0:T(256)S(1)} %constant_dynamic-update-slice_fu, ...), custom_call_target="tpu_custom_call", output_to_operand_aliasing={{0}: (7, {}), {1}: (8, {}), {2}: (9, {}), {3}: (10, {}), {4... | custom-call | flops 4000000000 | bytes 65536 | tf_op jit(solution)/shard_map/pallas_call | solution.py:360
  46.2 0.2 collective-permute-done.6.refs_5_.refs_10_
  46.4 0.1 collective-permute-start.10
  46.5 0.0 collective-permute-done.9.refs_6_.refs_11_
  46.6 2.7 %collective-permute-start.11 = (bf16[1,6,144,128]{3,2,1,0:T(8,128)(2,1)S(1)}, bf16[1,6,144,128]{3,2,1,0:T(8,128)(2,1)S(1)}, u32[]{:S(2)}, u32[]{:S(2)}) collective-permute-start(bf16[1,6,144,128]{3,2,1,0:T(8,128)(2,1)S(1)} %slice.9), channel_id=1, source_target_pairs={{0,14},{2,0},{4,2},{6,4},{8,6},{10,8},{12,10},{14,12},{1,15},{3,1}... | collective-permute-start | bytes 663560 | tf_op jit(solution)/shard_map/ppermute | solution.py:318
  49.3 0.0 collective-permute-done.15.refs_12_
  49.3 2.2 %shard_map.119 = (bf16[912,128]{1,0:T(8,128)(2,1)S(1)}, bf16[912,128]{1,0:T(8,128)(2,1)S(1)}, bf16[912,128]{1,0:T(8,128)(2,1)S(1)}, bf16[912,128]{1,0:T(8,128)(2,1)S(1)}) custom-call(s32[256]{0:T(256)S(1)} %constant_dynamic-update-slice_fusion.refs_0_, bf16[3,288,128]{2,1,0:T(8,128)(2,1)S(1)} %get-tuple-element.49.refs_1_, ...), custom_call_target="tpu_custom_call" | custom-call | flops 4000000000 | bytes 65536 | tf_op jit(solution)/shard_map/pallas_call | solution.py:364
  51.5 2.5 %collective-permute-start.16 = (bf16[912,128]{1,0:T(8,128)(2,1)S(1)}, bf16[912,128]{1,0:T(8,128)(2,1)S(1)}, u32[]{:S(2)}, u32[]{:S(2)}) collective-permute-start(bf16[912,128]{1,0:T(8,128)(2,1)S(1)} %get-tuple-element.81), channel_id=1, source_target_pairs={{0,48},{16,0},{32,16},{48,32},{1,49},{17,1},{33,17},{49,33},{2,50}... | collective-permute-start | bytes 700424 | tf_op jit(solution)/shard_map/ppermute | solution.py:318
  54.0 1.0 %collective-permute-start.17 = (bf16[912,128]{1,0:T(8,128)(2,1)S(1)}, bf16[912,128]{1,0:T(8,128)(2,1)S(1)}, u32[]{:S(2)}, u32[]{:S(2)}) collective-permute-start(bf16[912,128]{1,0:T(8,128)(2,1)S(1)} %get-tuple-element.82), channel_id=1, source_target_pairs={{0,32},{16,48},{32,0},{48,16},{1,33},{17,49},{33,1},{49,17},{2,34}... | collective-permute-start | bytes 700424 | tf_op jit(solution)/shard_map/ppermute | solution.py:318
  55.0 0.0 collective-permute-start.18
  55.0 0.0 collective-permute-done.11.refs_8_
  55.0 0.0 slice-start
  55.1 0.0 slice-start.2
  55.1 0.0 slice-start.3
  55.1 5.6 %shard_map.118 = (bf16[912,128]{1,0:T(8,128)(2,1)S(1)}, bf16[912,128]{1,0:T(8,128)(2,1)S(1)}, bf16[912,128]{1,0:T(8,128)(2,1)S(1)}, bf16[912,128]{1,0:T(8,128)(2,1)S(1)}) custom-call(s32[256]{0:T(256)S(1)} %constant_dynamic-update-slice_fusion.refs_0_, bf16[3,288,128]{2,1,0:T(8,128)(2,1)S(1)} %get-tuple-element.49.refs_1_, ...), custom_call_target="tpu_custom_call" | custom-call | flops 6000000000 | bytes 65536 | tf_op jit(solution)/shard_map/pallas_call | solution.py:371
  60.7 2.7 %collective-permute-start.12 = (bf16[912,128]{1,0:T(8,128)(2,1)S(1)}, bf16[912,128]{1,0:T(8,128)(2,1)S(1)}, u32[]{:S(2)}, u32[]{:S(2)}) collective-permute-start(bf16[912,128]{1,0:T(8,128)(2,1)S(1)} %get-tuple-element.76), channel_id=1, source_target_pairs={{0,48},{16,0},{32,16},{48,32},{1,49},{17,1},{33,17},{49,33},{2,50}... | collective-permute-start | bytes 700424 | tf_op jit(solution)/shard_map/ppermute | solution.py:318
  63.4 0.7 collective-permute-start.13
  64.2 0.0 collective-permute-done.16.p1
  64.2 0.0 collective-permute-start.14
  64.2 0.0 collective-permute-done.17.p2
  64.2 0.7 shard_map.120.extra
  64.9 5.1 %collective-permute-done.12.p1 = bf16[912,128]{1,0:T(8,128)(2,1)S(1)} collective-permute-done((bf16[912,128]{1,0:T(8,128)(2,1)S(1)}, bf16[912,128]{1,0:T(8,128)(2,1)S(1)}, u32[]{:S(2)}, u32[]{:S(2)}) %collective-permute-start.12) | collective-permute-done | bytes 233504 | tf_op jit(solution)/shard_map/ppermute | solution.py:318
  70.0 1.2 %collective-permute-done.13.p2 = bf16[912,128]{1,0:T(8,128)(2,1)S(1)} collective-permute-done((bf16[912,128]{1,0:T(8,128)(2,1)S(1)}, bf16[912,128]{1,0:T(8,128)(2,1)S(1)}, u32[]{:S(2)}, u32[]{:S(2)}) %collective-permute-start.13) | collective-permute-done | bytes 233504 | tf_op jit(solution)/shard_map/ppermute | solution.py:318
  71.3 2.9 %collective-permute-done.14.p3 = bf16[912,128]{1,0:T(8,128)(2,1)S(1)} collective-permute-done((bf16[912,128]{1,0:T(8,128)(2,1)S(1)}, bf16[912,128]{1,0:T(8,128)(2,1)S(1)}, u32[]{:S(2)}, u32[]{:S(2)}) %collective-permute-start.14) | collective-permute-done | bytes 233504 | tf_op jit(solution)/shard_map/ppermute | solution.py:318
  74.2 0.7 shard_map.121
  74.9 5.3 %collective-permute-start.19 = (bf16[3,144,128]{2,1,0:T(8,128)(2,1)S(1)}, bf16[3,144,128]{2,1,0:T(8,128)(2,1)S(1)}, u32[]{:S(2)}, u32[]{:S(2)}) collective-permute-start(bf16[3,144,128]{2,1,0:T(8,128)(2,1)S(1)} %get-tuple-element.85), channel_id=1, source_target_pairs={{0,1},{1,0},{2,3},{3,2},{4,5},{5,4},{6,7},{7,6},{8,9},{9,8},{10,11... | collective-permute-start | bytes 331784 | tf_op jit(solution)/shard_map/ppermute | solution.py:318
  80.2 1.0 collective-permute-done.19.refs_1_
  81.2 0.5 shard_map.124
  81.7 2.8 %collective-permute-start.22 = (bf16[144,768]{1,0:T(8,128)(2,1)S(1)}, bf16[144,768]{1,0:T(8,128)(2,1)S(1)}, u32[]{:S(2)}, u32[]{:S(2)}) collective-permute-start(bf16[144,768]{1,0:T(8,128)(2,1)S(1)} %shard_map.124), channel_id=1, source_target_pairs={{0,192},{64,0},{128,64},{192,128},{1,193},{65,1},{129,65},{193,129... | collective-permute-start | bytes 663560 | tf_op jit(solution)/shard_map/ppermute | solution.py:318
  84.5 0.5 shard_map.123
  85.0 0.1 collective-permute-start.21
  85.1 0.5 shard_map.122
  85.6 1.7 %collective-permute-start.20 = (bf16[144,768]{1,0:T(8,128)(2,1)S(1)}, bf16[144,768]{1,0:T(8,128)(2,1)S(1)}, u32[]{:S(2)}, u32[]{:S(2)}) collective-permute-start(bf16[144,768]{1,0:T(8,128)(2,1)S(1)} %shard_map.122), channel_id=1, source_target_pairs={{0,128},{64,192},{128,0},{192,64},{1,129},{65,193},{129,1},{193,65... | collective-permute-start | bytes 663560 | tf_op jit(solution)/shard_map/ppermute | solution.py:318
  87.3 0.5 shard_map.125.p3
  87.8 1.1 %collective-permute-done.22.p2 = bf16[144,768]{1,0:T(8,128)(2,1)S(1)} collective-permute-done((bf16[144,768]{1,0:T(8,128)(2,1)S(1)}, bf16[144,768]{1,0:T(8,128)(2,1)S(1)}, u32[]{:S(2)}, u32[]{:S(2)}) %collective-permute-start.22) | collective-permute-done | bytes 221216 | tf_op jit(solution)/shard_map/ppermute | solution.py:318
  89.0 4.7 %collective-permute-done.21.p1 = bf16[144,768]{1,0:T(8,128)(2,1)S(1)} collective-permute-done((bf16[144,768]{1,0:T(8,128)(2,1)S(1)}, bf16[144,768]{1,0:T(8,128)(2,1)S(1)}, u32[]{:S(2)}, u32[]{:S(2)}) %collective-permute-start.21) | collective-permute-done | bytes 221216 | tf_op jit(solution)/shard_map/ppermute | solution.py:318
  93.6 2.8 %collective-permute-done.20.p0 = bf16[144,768]{1,0:T(8,128)(2,1)S(1)} collective-permute-done((bf16[144,768]{1,0:T(8,128)(2,1)S(1)}, bf16[144,768]{1,0:T(8,128)(2,1)S(1)}, u32[]{:S(2)}, u32[]{:S(2)}) %collective-permute-start.20) | collective-permute-done | bytes 221216 | tf_op jit(solution)/shard_map/ppermute | solution.py:318
  96.4 0.8 shard_map.126
  (21 shorter events, 0.1 us)
Async XLA Ops:
  0.6 23.7 %copy-start.1 = (s32[64,2]{0,1:T(2,128)S(1)}, s32[64,2]{0,1:T(2,128)}, u32[]{:S(2)}) copy-start(s32[64,2]{0,1:T(2,128)} %param.17) | copy-start | bytes 1540
  0.6 24.0 %copy-start.2 = (s32[64,2]{0,1:T(2,128)S(1)}, s32[64,2]{0,1:T(2,128)}, u32[]{:S(2)}) copy-start(s32[64,2]{0,1:T(2,128)} %param.16) | copy-start | bytes 1540
  2.8 4.8 %collective-permute-start = (bf16[9,144,128]{2,1,0:T(8,128)(2,1)}, bf16[9,144,128]{2,1,0:T(8,128)(2,1)S(1)}, u32[]{:S(2)}, u32[]{:S(2)}) collective-permute-start(bf16[9,144,128]{2,1,0:T(8,128)(2,1)} %get-tuple-element.44), channel_id=1, source_target_pairs={{0,1},{1,0},{2,3},{3,2},{4,5},{5,4},{6,7},{7,6},{8,9},{9,8},{10,11... | collective-permute-start | bytes 995336 | tf_op jit(solution)/shard_map/ppermute | solution.py:318
  6.1 1.0 %copy-start = (bf16[9,144,128]{2,1,0:T(8,128)(2,1)S(1)}, bf16[9,144,128]{2,1,0:T(8,128)(2,1)}, u32[]{:S(2)}) copy-start(bf16[9,144,128]{2,1,0:T(8,128)(2,1)} %get-tuple-element.45.src) | copy-start | bytes 995332
  7.6 14.1 %collective-permute-start.4 = (bf16[2,6,144,128]{3,2,1,0:T(8,128)(2,1)S(1)}, bf16[2,6,144,128]{3,2,1,0:T(8,128)(2,1)S(1)}, u32[]{:S(2)}, u32[]{:S(2)}) collective-permute-start(bf16[2,6,144,128]{3,2,1,0:T(8,128)(2,1)S(1)} %get-tuple-element.50.refs_5_), channel_id=1, source_target_pairs={{0,2},{2,4},{4,6},{6,8},{8,10},{10,12},{12,14},{14,0},{1,3},{3,5},... | collective-permute-start | bytes 1327112 | tf_op jit(solution)/shard_map/ppermute | solution.py:318
  7.7 14.0 %collective-permute-start.7 = (bf16[2,6,144,128]{3,2,1,0:T(8,128)(2,1)S(1)}, bf16[2,6,144,128]{3,2,1,0:T(8,128)(2,1)S(1)}, u32[]{:S(2)}, u32[]{:S(2)}) collective-permute-start(bf16[2,6,144,128]{3,2,1,0:T(8,128)(2,1)S(1)} %get-tuple-element.50.refs_5_), channel_id=1, source_target_pairs={{0,14},{2,0},{4,2},{6,4},{8,6},{10,8},{12,10},{14,12},{1,15},{3,1}... | collective-permute-start | bytes 1327112 | tf_op jit(solution)/shard_map/ppermute | solution.py:318
  21.7 13.4 %collective-permute-start.5 = (bf16[2,6,144,128]{3,2,1,0:T(8,128)(2,1)S(1)}, bf16[2,6,144,128]{3,2,1,0:T(8,128)(2,1)S(1)}, u32[]{:S(2)}, u32[]{:S(2)}) collective-permute-start(bf16[2,6,144,128]{3,2,1,0:T(8,128)(2,1)S(1)} %collective-permute-done.4.refs_6_), channel_id=1, source_target_pairs={{0,2},{2,4},{4,6},{6,8},{8,10},{10,12},{12,14},{14,0},{1,3},{3,5},... | collective-permute-start | bytes 1327112 | tf_op jit(solution)/shard_map/ppermute | solution.py:318
  21.7 13.4 %collective-permute-start.8 = (bf16[2,6,144,128]{3,2,1,0:T(8,128)(2,1)S(1)}, bf16[2,6,144,128]{3,2,1,0:T(8,128)(2,1)S(1)}, u32[]{:S(2)}, u32[]{:S(2)}) collective-permute-start(bf16[2,6,144,128]{3,2,1,0:T(8,128)(2,1)S(1)} %collective-permute-done.7.refs_7_), channel_id=1, source_target_pairs={{0,14},{2,0},{4,2},{6,4},{8,6},{10,8},{12,10},{14,12},{1,15},{3,1}... | collective-permute-start | bytes 1327112 | tf_op jit(solution)/shard_map/ppermute | solution.py:318
  24.9 6.8 %collective-permute-start.1 = (bf16[3,288,128]{2,1,0:T(8,128)(2,1)S(1)}, bf16[3,288,128]{2,1,0:T(8,128)(2,1)S(1)}, u32[]{:S(2)}, u32[]{:S(2)}) collective-permute-start(bf16[3,288,128]{2,1,0:T(8,128)(2,1)S(1)} %get-tuple-element.49.refs_1_), channel_id=1, source_target_pairs={{0,16},{16,32},{32,48},{48,0},{1,17},{17,33},{33,49},{49,1},{2,18}... | collective-permute-start | bytes 663560 | tf_op jit(solution)/shard_map/ppermute | solution.py:318
  26.1 11.6 %collective-permute-start.2 = (bf16[3,288,128]{2,1,0:T(8,128)(2,1)S(1)}, bf16[3,288,128]{2,1,0:T(8,128)(2,1)S(1)}, u32[]{:S(2)}, u32[]{:S(2)}) collective-permute-start(bf16[3,288,128]{2,1,0:T(8,128)(2,1)S(1)} %get-tuple-element.49.refs_1_), channel_id=1, source_target_pairs={{0,32},{16,48},{32,0},{48,16},{1,33},{17,49},{33,1},{49,17},{2,34}... | collective-permute-start | bytes 663560 | tf_op jit(solution)/shard_map/ppermute | solution.py:318
  28.6 9.2 %collective-permute-start.3 = (bf16[3,288,128]{2,1,0:T(8,128)(2,1)S(1)}, bf16[3,288,128]{2,1,0:T(8,128)(2,1)S(1)}, u32[]{:S(2)}, u32[]{:S(2)}) collective-permute-start(bf16[3,288,128]{2,1,0:T(8,128)(2,1)S(1)} %get-tuple-element.49.refs_1_), channel_id=1, source_target_pairs={{0,48},{16,0},{32,16},{48,32},{1,49},{17,1},{33,17},{49,33},{2,50}... | collective-permute-start | bytes 663560 | tf_op jit(solution)/shard_map/ppermute | solution.py:318
  31.6 17.7 %collective-permute-start.15 = (bf16[6,32,128]{2,1,0:T(8,128)(2,1)S(1)}, bf16[6,32,128]{2,1,0:T(8,128)(2,1)S(1)}, u32[]{:S(2)}, u32[]{:S(2)}) collective-permute-start(bf16[6,32,128]{2,1,0:T(8,128)(2,1)S(1)} %get-tuple-element.79), channel_id=1, source_target_pairs={{0,8},{2,10},{4,12},{6,14},{8,0},{10,2},{12,4},{14,6},{1,9},{3,11}... | collective-permute-start | bytes 147464 | tf_op jit(solution)/shard_map/ppermute | solution.py:318
  35.1 11.3 %collective-permute-start.6 = (bf16[2,6,144,128]{3,2,1,0:T(8,128)(2,1)S(1)}, bf16[2,6,144,128]{3,2,1,0:T(8,128)(2,1)S(1)}, u32[]{:S(2)}, u32[]{:S(2)}) collective-permute-start(bf16[2,6,144,128]{3,2,1,0:T(8,128)(2,1)S(1)} %collective-permute-done.5.refs_5_.refs_8_), channel_id=1, source_target_pairs={{0,2},{2,4},{4,6},{6,8},{8,10},{10,12},{12,14},{14,0},{1,3},{3,5},... | collective-permute-start | bytes 1327112 | tf_op jit(solution)/shard_map/ppermute | solution.py:318
  35.1 11.4 %collective-permute-start.9 = (bf16[2,6,144,128]{3,2,1,0:T(8,128)(2,1)S(1)}, bf16[2,6,144,128]{3,2,1,0:T(8,128)(2,1)S(1)}, u32[]{:S(2)}, u32[]{:S(2)}) collective-permute-start(bf16[2,6,144,128]{3,2,1,0:T(8,128)(2,1)S(1)} %collective-permute-done.8.refs_6_.refs_9_), channel_id=1, source_target_pairs={{0,14},{2,0},{4,2},{6,4},{8,6},{10,8},{12,10},{14,12},{1,15},{3,1}... | collective-permute-start | bytes 1327112 | tf_op jit(solution)/shard_map/ppermute | solution.py:318
  46.4 8.6 %collective-permute-start.10 = (bf16[1,6,144,128]{3,2,1,0:T(8,128)(2,1)S(1)}, bf16[1,6,144,128]{3,2,1,0:T(8,128)(2,1)S(1)}, u32[]{:S(2)}, u32[]{:S(2)}) collective-permute-start(bf16[1,6,144,128]{3,2,1,0:T(8,128)(2,1)S(1)} %slice.8), channel_id=1, source_target_pairs={{0,2},{2,4},{4,6},{6,8},{8,10},{10,12},{12,14},{14,0},{1,3},{3,5},... | collective-permute-start | bytes 663560 | tf_op jit(solution)/shard_map/ppermute | solution.py:318
  46.6 8.5 %collective-permute-start.11 = (bf16[1,6,144,128]{3,2,1,0:T(8,128)(2,1)S(1)}, bf16[1,6,144,128]{3,2,1,0:T(8,128)(2,1)S(1)}, u32[]{:S(2)}, u32[]{:S(2)}) collective-permute-start(bf16[1,6,144,128]{3,2,1,0:T(8,128)(2,1)S(1)} %slice.9), channel_id=1, source_target_pairs={{0,14},{2,0},{4,2},{6,4},{8,6},{10,8},{12,10},{14,12},{1,15},{3,1}... | collective-permute-start | bytes 663560 | tf_op jit(solution)/shard_map/ppermute | solution.py:318
  51.5 12.7 %collective-permute-start.16 = (bf16[912,128]{1,0:T(8,128)(2,1)S(1)}, bf16[912,128]{1,0:T(8,128)(2,1)S(1)}, u32[]{:S(2)}, u32[]{:S(2)}) collective-permute-start(bf16[912,128]{1,0:T(8,128)(2,1)S(1)} %get-tuple-element.81), channel_id=1, source_target_pairs={{0,48},{16,0},{32,16},{48,32},{1,49},{17,1},{33,17},{49,33},{2,50}... | collective-permute-start | bytes 700424 | tf_op jit(solution)/shard_map/ppermute | solution.py:318
  54.0 10.2 %collective-permute-start.17 = (bf16[912,128]{1,0:T(8,128)(2,1)S(1)}, bf16[912,128]{1,0:T(8,128)(2,1)S(1)}, u32[]{:S(2)}, u32[]{:S(2)}) collective-permute-start(bf16[912,128]{1,0:T(8,128)(2,1)S(1)} %get-tuple-element.82), channel_id=1, source_target_pairs={{0,32},{16,48},{32,0},{48,16},{1,33},{17,49},{33,1},{49,17},{2,34}... | collective-permute-start | bytes 700424 | tf_op jit(solution)/shard_map/ppermute | solution.py:318
  55.0 9.2 %collective-permute-start.18 = (bf16[912,128]{1,0:T(8,128)(2,1)S(1)}, bf16[912,128]{1,0:T(8,128)(2,1)S(1)}, u32[]{:S(2)}, u32[]{:S(2)}) collective-permute-start(bf16[912,128]{1,0:T(8,128)(2,1)S(1)} %get-tuple-element.83), channel_id=1, source_target_pairs={{0,16},{16,32},{32,48},{48,0},{1,17},{17,33},{33,49},{49,1},{2,18}... | collective-permute-start | bytes 700424 | tf_op jit(solution)/shard_map/ppermute | solution.py:318
  55.0 26.2 %slice-start = ((s8[4718592]{0:T(1024)(128)(4,1)}), s8[4194304]{0:T(1024)(128)(4,1)S(1)}, s32[]{:S(2)}) async-start(s8[4718592]{0:T(1024)(128)(4,1)} %bitcast), calls=%async_computation | async-start | bytes 8388608
  55.1 26.1 %slice-start.2 = ((s8[4718592]{0:T(1024)(128)(4,1)}), s8[4194304]{0:T(1024)(128)(4,1)S(1)}, s32[]{:S(2)}) async-start(s8[4718592]{0:T(1024)(128)(4,1)} %bitcast.2), calls=%async_computation.2 | async-start | bytes 8388608
  55.1 26.1 %slice-start.1 = ((s8[4718592]{0:T(1024)(128)(4,1)}), s8[524288]{0:T(1024)(128)(4,1)S(1)}, s32[]{:S(2)}) async-start(s8[4718592]{0:T(1024)(128)(4,1)} %bitcast), calls=%async_computation.1 | async-start | bytes 1048576
  55.1 26.1 %slice-start.3 = ((s8[4718592]{0:T(1024)(128)(4,1)}), s8[524288]{0:T(1024)(128)(4,1)S(1)}, s32[]{:S(2)}) async-start(s8[4718592]{0:T(1024)(128)(4,1)} %bitcast.2), calls=%async_computation.3 | async-start | bytes 1048576
  60.7 9.3 %collective-permute-start.12 = (bf16[912,128]{1,0:T(8,128)(2,1)S(1)}, bf16[912,128]{1,0:T(8,128)(2,1)S(1)}, u32[]{:S(2)}, u32[]{:S(2)}) collective-permute-start(bf16[912,128]{1,0:T(8,128)(2,1)S(1)} %get-tuple-element.76), channel_id=1, source_target_pairs={{0,48},{16,0},{32,16},{48,32},{1,49},{17,1},{33,17},{49,33},{2,50}... | collective-permute-start | bytes 700424 | tf_op jit(solution)/shard_map/ppermute | solution.py:318
  63.4 7.8 %collective-permute-start.13 = (bf16[912,128]{1,0:T(8,128)(2,1)S(1)}, bf16[912,128]{1,0:T(8,128)(2,1)S(1)}, u32[]{:S(2)}, u32[]{:S(2)}) collective-permute-start(bf16[912,128]{1,0:T(8,128)(2,1)S(1)} %get-tuple-element.77), channel_id=1, source_target_pairs={{0,32},{16,48},{32,0},{48,16},{1,33},{17,49},{33,1},{49,17},{2,34}... | collective-permute-start | bytes 700424 | tf_op jit(solution)/shard_map/ppermute | solution.py:318
  64.2 10.0 %collective-permute-start.14 = (bf16[912,128]{1,0:T(8,128)(2,1)S(1)}, bf16[912,128]{1,0:T(8,128)(2,1)S(1)}, u32[]{:S(2)}, u32[]{:S(2)}) collective-permute-start(bf16[912,128]{1,0:T(8,128)(2,1)S(1)} %get-tuple-element.78), channel_id=1, source_target_pairs={{0,16},{16,32},{32,48},{48,0},{1,17},{17,33},{33,49},{49,1},{2,18}... | collective-permute-start | bytes 700424 | tf_op jit(solution)/shard_map/ppermute | solution.py:318
  74.9 6.3 %collective-permute-start.19 = (bf16[3,144,128]{2,1,0:T(8,128)(2,1)S(1)}, bf16[3,144,128]{2,1,0:T(8,128)(2,1)S(1)}, u32[]{:S(2)}, u32[]{:S(2)}) collective-permute-start(bf16[3,144,128]{2,1,0:T(8,128)(2,1)S(1)} %get-tuple-element.85), channel_id=1, source_target_pairs={{0,1},{1,0},{2,3},{3,2},{4,5},{5,4},{6,7},{7,6},{8,9},{9,8},{10,11... | collective-permute-start | bytes 331784 | tf_op jit(solution)/shard_map/ppermute | solution.py:318
  81.7 7.2 %collective-permute-start.22 = (bf16[144,768]{1,0:T(8,128)(2,1)S(1)}, bf16[144,768]{1,0:T(8,128)(2,1)S(1)}, u32[]{:S(2)}, u32[]{:S(2)}) collective-permute-start(bf16[144,768]{1,0:T(8,128)(2,1)S(1)} %shard_map.124), channel_id=1, source_target_pairs={{0,192},{64,0},{128,64},{192,128},{1,193},{65,1},{129,65},{193,129... | collective-permute-start | bytes 663560 | tf_op jit(solution)/shard_map/ppermute | solution.py:318
  85.0 8.6 %collective-permute-start.21 = (bf16[144,768]{1,0:T(8,128)(2,1)S(1)}, bf16[144,768]{1,0:T(8,128)(2,1)S(1)}, u32[]{:S(2)}, u32[]{:S(2)}) collective-permute-start(bf16[144,768]{1,0:T(8,128)(2,1)S(1)} %shard_map.123), channel_id=1, source_target_pairs={{0,64},{64,128},{128,192},{192,0},{1,65},{65,129},{129,193},{193,1... | collective-permute-start | bytes 663560 | tf_op jit(solution)/shard_map/ppermute | solution.py:318
  85.6 10.8 %collective-permute-start.20 = (bf16[144,768]{1,0:T(8,128)(2,1)S(1)}, bf16[144,768]{1,0:T(8,128)(2,1)S(1)}, u32[]{:S(2)}, u32[]{:S(2)}) collective-permute-start(bf16[144,768]{1,0:T(8,128)(2,1)S(1)} %shard_map.122), channel_id=1, source_target_pairs={{0,128},{64,192},{128,0},{192,64},{1,129},{65,193},{129,1},{193,65... | collective-permute-start | bytes 663560 | tf_op jit(solution)/shard_map/ppermute | solution.py:318
